TPU v7x, 256 devices: a whole 4x4x8 slice. The times are simulated.
256 devices in a mesh: tile: 64 (over z, y_lo, x), mode: 4 (over y_hi, core).
Axes of the slice: x: 4, y: 4 (y_hi: 2, y_lo: 2; y = y_hi * 2 + y_lo), z: 8, core: 2. Of those that a mesh axis runs over, the one named last changes fastest.
Arguments:
- object_tiles: float32 [64, 2, 2, 256, 256], P('tile'), may hold values from -6 to 6
- object_previous: float32 [64, 2, 2, 256, 256], P('tile'), may hold values from -6 to 6
- probe: float32 [4, 8, 2, 256, 256], P(None, 'mode', None, 'tile'), may hold values from -2 to 2
- probe_previous: float32 [4, 8, 2, 256, 256], P(None, 'mode', None, 'tile'), may hold values from -6 to 6
- patterns: float32 [128, 256, 256], P('tile'), may hold values from 0 to 2
- offsets: int32 [2, 128], P(None, 'tile'), may hold values from 0 to 255
- scan_of_slot: int32 [128], P('tile'), may hold values from 0 to 3
- tile_load: int32 [64], P('tile'), may hold values from 1 to 2, as said below
- step_sizes: int32 [2], replicated, may hold values from 128 to 511
- object_norm_before: float32 [1], replicated, may hold values from 0.1 to 0.4
- probe_norm_before: float32 [1], replicated, may hold values from 12 to 64
Outputs:
- new_object: float32 [64, 2, 2, 256, 256], P('tile')
- object_direction: float32 [64, 2, 2, 256, 256], P('tile')
- new_probe: float32 [4, 8, 2, 256, 256], P(None, 'mode', None, 'tile')
- probe_direction: float32 [4, 8, 2, 256, 256], P(None, 'mode', None, 'tile')
Inputs may be any that keep to these rules, and one draw needn't show every extreme that they name: `tile_load`: every tile holds 1 to 2 used slots, and some tile holds exactly 2.
All inputs are finite; a program needn't handle non-finite values.
Results may differ from a plain program's by a relative error of at most 0.024.
Values may be sent and summed in bfloat16 or wider, within the bound.
No kernel may reach another device: no remote copies, remote signals or barrier semaphores. Data moves between devices by JAX's collectives and lax.ppermute only.
A program may use at most 64 MiB of HBM per device.

v0:
```python
import math

import jax
import jax.numpy as jnp
from jax import lax
from jax.sharding import PartitionSpec as P

TGX = 8
MODES = 8
SCAN_COUNT = 4


residual_weight = 2.0


def from_behind(block, axis, distance):
    devices = range(lax.axis_size(axis))
    route = [(i - distance, i) for i in devices if i - distance in devices]
    return lax.ppermute(block, axis, route)


def table_pair(width):
    index_row = jnp.arange(width, dtype=jnp.int32)
    product = index_row[:, None] * index_row[None, :] % width
    angle = product.astype(jnp.float32) * (2.0 * math.pi / width)
    factor = 1.0 / math.sqrt(width)
    cosine = (jnp.cos(angle) * factor).astype(jnp.bfloat16)
    sine = (-jnp.sin(angle) * factor).astype(jnp.bfloat16)
    index_free = jnp.where(index_row < width // 2, index_row, index_row - width).astype(jnp.float32)
    phase = (
        index_free[:, None] * index_free[:, None] + index_free[None, :] * index_free[None, :]
    ) * (math.pi / (4.0 * width))
    return (cosine, sine, jnp.cos(phase), jnp.sin(phase))


def right_product(left_data, table):
    return jnp.einsum("...jk,kl->...jl", left_data, table, preferred_element_type=jnp.float32)


def left_product(table, right_data):
    return jnp.einsum("ij,...jl->...il", table, right_data, preferred_element_type=jnp.float32)


def transform(wave_re, wave_im, tables, inverse):
    cosine = tables[0]
    sine = -tables[1] if inverse else tables[1]
    first_re = (right_product(wave_re, cosine) - right_product(wave_im, sine)).astype(jnp.bfloat16)
    first_im = (right_product(wave_re, sine) + right_product(wave_im, cosine)).astype(jnp.bfloat16)
    out_re = (left_product(cosine, first_re) - left_product(sine, first_im)).astype(jnp.bfloat16)
    out_im = (left_product(sine, first_re) + left_product(cosine, first_im)).astype(jnp.bfloat16)
    return (out_re, out_im)


def complex_times(first_re, first_im, second_re, second_im):
    first_portion = first_re.astype(jnp.float32)
    b_part = first_im.astype(jnp.float32)
    c_part = second_re.astype(jnp.float32)
    d_part = second_im.astype(jnp.float32)
    return (first_portion * c_part - b_part * d_part, first_portion * d_part + b_part * c_part)


def conj_times(first_re, first_im, second_re, second_im):
    first_portion = first_re.astype(jnp.float32)
    b_part = first_im.astype(jnp.float32)
    c_part = second_re.astype(jnp.float32)
    d_part = second_im.astype(jnp.float32)
    return (first_portion * c_part + b_part * d_part, first_portion * d_part - b_part * c_part)


def propagate(wave_re, wave_im, tables, adjoint):
    spec_re, spec_im = transform(wave_re, wave_im, tables, False)
    kernel_im = -tables[3] if adjoint else tables[3]
    moved_re, moved_im = complex_times(spec_re, spec_im, tables[2], kernel_im)
    return transform(moved_re.astype(jnp.bfloat16), moved_im.astype(jnp.bfloat16), tables, True)


def body(
    object_tiles,
    object_previous,
    probe,
    probe_previous,
    patterns,
    offsets,
    scan_of_slot,
    tile_load,
    step_sizes,
    object_norm_before,
    probe_norm_before,
):
    tile_count = lax.axis_size("tile")
    mode_count = lax.axis_size("mode")
    slots = patterns.shape[0]
    width = patterns.shape[1]
    layers = object_tiles.shape[1]
    tile_side = object_tiles.shape[3]
    scans = probe.shape[0]
    tables = table_pair(width)
    own_tile = object_tiles[0].astype(jnp.bfloat16)
    east_part = from_behind(own_tile, "tile", -1)
    upper = jnp.concatenate([own_tile, east_part], axis=3)
    lower = from_behind(upper, "tile", -TGX)
    region = jnp.concatenate([upper, lower], axis=2)
    gathered = lax.all_gather(probe.astype(jnp.bfloat16), "tile", axis=3, tiled=True)
    valid_mask = (jnp.arange(slots, dtype=jnp.int32) < tile_load[0]).astype(jnp.float32)

    def cut_patch(row_start, col_start):
        return lax.dynamic_slice(region, (0, 0, row_start, col_start), (layers, 2, width, width))

    patches = jax.vmap(cut_patch)(offsets[0], offsets[1])
    probe_pick = jnp.take(gathered, scan_of_slot, axis=0)
    wave_re = probe_pick[:, :, 0]
    wave_im = probe_pick[:, :, 1]
    incident = []
    for layer_index in range(layers):
        incident.append((wave_re, wave_im))
        next_re, next_im = complex_times(
            wave_re, wave_im, patches[:, None, layer_index, 0], patches[:, None, layer_index, 1]
        )
        wave_re = next_re.astype(jnp.bfloat16)
        wave_im = next_im.astype(jnp.bfloat16)
        if layer_index + 1 < layers:
            wave_re, wave_im = propagate(wave_re, wave_im, tables, False)
    far_re, far_im = transform(wave_re, wave_im, tables, False)
    far_re32 = far_re.astype(jnp.float32)
    far_im32 = far_im.astype(jnp.float32)
    partial_power = jnp.sum(far_re32 * far_re32 + far_im32 * far_im32, axis=1)
    power = lax.psum(partial_power, "mode")
    misfit = (power - patterns) * valid_mask[:, None, None]
    back_re = (residual_weight * misfit[:, None] * far_re32).astype(jnp.bfloat16)
    back_im = (residual_weight * misfit[:, None] * far_im32).astype(jnp.bfloat16)
    back_re, back_im = transform(back_re, back_im, tables, True)
    slice_terms = [None] * layers
    probe_terms = None
    for layer_index in reversed(range(layers)):
        inc_re, inc_im = incident[layer_index]
        grad_re, grad_im = conj_times(inc_re, inc_im, back_re, back_im)
        slice_terms[layer_index] = jnp.stack(
            [jnp.sum(grad_re, axis=1), jnp.sum(grad_im, axis=1)], axis=1
        )
        carry_re, carry_im = conj_times(
            patches[:, None, layer_index, 0], patches[:, None, layer_index, 1], back_re, back_im
        )
        if layer_index > 0:
            back_re, back_im = propagate(
                carry_re.astype(jnp.bfloat16), carry_im.astype(jnp.bfloat16), tables, True
            )
        else:
            probe_terms = jnp.stack([carry_re, carry_im], axis=2)
    slot_grads = jnp.stack(slice_terms, axis=1)
    region_grad = jnp.zeros((layers, 2, 2 * tile_side, 2 * tile_side), jnp.float32)
    for slot_index in range(slots):
        starts = (0, 0, offsets[0, slot_index], offsets[1, slot_index])
        current = lax.dynamic_slice(region_grad, starts, (layers, 2, width, width))
        region_grad = lax.dynamic_update_slice(
            region_grad, current + slot_grads[slot_index], starts
        )
    region_grad = lax.psum(region_grad.astype(jnp.bfloat16), "mode").astype(jnp.float32)
    from_above = from_behind(
        region_grad[:, :, tile_side:, :].astype(jnp.bfloat16), "tile", TGX
    ).astype(jnp.float32)
    upper_grad = region_grad[:, :, :tile_side, :] + from_above
    from_left = from_behind(upper_grad[:, :, :, tile_side:].astype(jnp.bfloat16), "tile", 1).astype(
        jnp.float32
    )
    tile_grad = upper_grad[:, :, :, :tile_side] + from_left
    scan_onehot = (scan_of_slot[:, None] == jnp.arange(scans, dtype=jnp.int32)[None, :]).astype(
        jnp.float32
    )
    probe_local = jnp.einsum(
        "cs,cmrij->smrij", scan_onehot, probe_terms, precision=lax.Precision.HIGHEST
    )
    probe_grad = lax.psum_scatter(probe_local, "tile", scatter_dimension=3, tiled=True)
    object_sum = jnp.sum(tile_grad * tile_grad) / float(mode_count)
    probe_sum = jnp.sum(probe_grad * probe_grad)
    object_total, probe_total = lax.psum((object_sum, probe_sum), ("tile", "mode"))
    object_square = object_total / float(tile_count * layers * 2 * tile_side * tile_side)
    probe_square = probe_total / float(SCAN_COUNT * MODES * 2 * width * width)
    object_direction = -tile_grad[None] + object_square / object_norm_before[0] * object_previous
    new_object = object_tiles + step_sizes[0].astype(jnp.float32) / 1024.0 * object_direction
    probe_direction = -probe_grad + probe_square / probe_norm_before[0] * probe_previous
    new_probe = probe + step_sizes[1].astype(jnp.float32) / 16384.0 * probe_direction
    return (new_object, object_direction, new_probe, probe_direction)


def solution(mesh):
    return jax.shard_map(
        body,
        mesh=mesh,
        in_specs=(
            P("tile", None, None, None, None),
            P("tile", None, None, None, None),
            P(None, "mode", None, "tile", None),
            P(None, "mode", None, "tile", None),
            P("tile", None, None),
            P(None, "tile"),
            P("tile"),
            P("tile"),
            P(),
            P(),
            P(),
        ),
        out_specs=(
            P("tile", None, None, None, None),
            P("tile", None, None, None, None),
            P(None, "mode", None, "tile", None),
            P(None, "mode", None, "tile", None),
        ),
        check_vma=False,
    )
```

profile of v0, /device:TPU:1, one launch (start us, length us, event | category | flops | bytes accessed | tf_op | source)
XLA Modules:
  0.0 1247.4 jit_solution(10554642321168706119)
XLA Ops:
  7.2 1.5 copy.264
  8.8 1.3 convert_bitcast_fusion
  10.1 1.3 collective-permute-start
  12.1 11.3 collective-permute-done
  23.5 1.3 collective-permute-start.1
  25.1 1.8 fusion.154
  26.9 28.3 %collective-permute-done.1 = bf16[2,2,256,512]{3,2,1,0:T(8,128)(2,1)} collective-permute-done((bf16[2,2,256,512]{3,2,1,0:T(8,128)(2,1)S(1)}, bf16[2,2,256,512]{3,2,1,0:T(8,128)(2,1)}, u32[]{:S(2)}, u32[]{:S(2)}) %collective-permute-start.1) | collective-permute-done | bytes 1048608 | tf_op jit(solution)/shard_map/ppermute | solution.py:19
  55.2 1.4 pad_maximum_fusion
  56.6 6.0 while.1
  57.2 2.4 bitcast_dynamic-update-slice_fusion.2
  60.2 2.4 bitcast_dynamic-update-slice_fusion.2
  62.6 1.4 bitcast_convert_fusion.3
  66.4 200.3 %all-gather.2.cloned.1.call-done = bf16[4,2,2,256,256]{4,0,2,1,3:T(4,128)(2,1)} async-done(((bf16[4,2,2,4,256]{4,0,2,1,3:T(4,128)(2,1)}), bf16[4,2,2,256,256]{4,0,2,1,3:T(4,128)(2,1)}) %all-gather.2.cloned.1.call-update) | async-done | bytes 2097168 | tf_op jit(solution)/shard_map/all_gather | solution.py:103
  266.7 2.3 copy.137
  269.0 1.6 gather_fusion
  270.6 1.7 copy.138
  272.8 1.3 fusion.102
  275.3 1.3 fusion
  279.1 1.3 fusion.1
  281.6 1.4 add_convert_fusion.3
  283.0 1.3 fusion.84
  284.3 1.7 fusion.133
  292.3 2.4 add_convert_fusion.2
  294.8 1.3 fusion.96
  297.3 1.3 fusion.16
  298.5 1.4 fusion.125
  303.8 2.1 add_reduce_fusion.1
  311.5 2.1 copy.169
  316.8 82.1 %all-reduce.6.cloned.1.call-done = f32[2,256,256]{1,2,0:T(8,128)} async-done(((f32[2,256,256]{1,2,0:T(8,128)}), f32[2,256,256]{1,2,0:T(8,128)}) %all-reduce.6.cloned.1.call-update) | async-done | bytes 524304 | tf_op jit(solution)/shard_map/psum | solution.py:127
  398.9 1.3 multiply_multiply_fusion
  400.2 1.3 fusion.78
  401.5 1.3 fusion.121
  402.8 1.3 fusion.24
  406.6 1.3 fusion.25
  409.5 2.7 add_reduce_fusion
  414.7 1.3 fusion.32
  421.1 1.4 add_convert_fusion
  422.5 1.3 fusion.72
  423.7 1.4 fusion.109
  425.2 1.3 fusion.40
  431.5 3.0 add_bitcast_fusion
  434.8 2.5 broadcast_in_dim.11
  437.3 11.8 dynamic_update_slice.6
  449.1 1.8 fusion.59
  450.9 11.1 dynamic_update_slice.7
  462.0 3.9 convert_element_type.598
  467.4 1.6 pad_maximum_fusion.1
  469.0 3.1 copy.197
  472.1 6.6 fusion.156
  478.7 51.3 %all-reduce.8.cloned.1.call-done = bf16[2,2,512,512]{2,3,1,0:T(8,128)(2,1)} async-done(((bf16[2,2,512,512]{2,3,1,0:T(8,128)(2,1)}), bf16[2,2,512,512]{2,3,1,0:T(8,128)(2,1)}) %all-reduce.8.cloned.1.call-update) | async-done | bytes 2097168 | tf_op jit(solution)/shard_map/psum | solution.py:157
  530.0 1.4 slice.116
  531.5 3.4 collective-permute-start.2
  534.8 22.3 %collective-permute-done.2 = bf16[2,2,256,512]{2,3,1,0:T(8,128)(2,1)S(1)} collective-permute-done((bf16[2,2,256,512]{2,3,1,0:T(8,128)(2,1)S(1)}, bf16[2,2,256,512]{2,3,1,0:T(8,128)(2,1)S(1)}, u32[]{:S(2)}, u32[]{:S(2)}) %collective-permute-start.2) | collective-permute-done | bytes 1048608 | tf_op jit(solution)/shard_map/ppermute | solution.py:19
  558.2 3.9 collective-permute-start.3
  562.1 1.3 copy.196
  566.7 2.6 copy.195
  570.6 2.8 collective-permute-done.3
  573.4 1.9 multiply_reduce_fusion
  576.0 531.9 %all-reduce.10.cloned.1.call-done = f32[4,2,2,256,256]{4,0,3,2,1:T(4,128)} async-done(((f32[4,2,2,256,256]{4,0,3,2,1:T(4,128)}), f32[4,2,2,256,256]{4,0,3,2,1:T(4,128)}) %all-reduce.10.cloned.1.call-update) | async-done | bytes 4194320
  1107.8 1.5 multiply_reduce_fusion.1
  1109.3 120.8 %all-reduce.1 = (f32[]{:T(128)}, f32[]{:T(128)}) all-reduce(f32[]{:T(128)S(6)} %div.27, f32[]{:T(128)} %multiply_reduce_fusion.1), channel_id=1, replica_groups=mesh['tile'=64,'mode'=4] {'tile','mode'}, use_global_device_ids=true, to_apply=%region_8.9 | all-reduce | flops 2 | bytes 16 | tf_op jit(solution)/shard_map/psum | solution.py:175
  1233.8 2.9 multiply_add_fusion
  1236.7 2.6 copy.200
  1239.3 1.3 copy.201
  (117 shorter events, 45.2 us)
Async XLA Ops:
  7.2 17.8 %copy-start.23 = (s32[2]{0:T(128)S(1)}, s32[2]{0:T(128)}, u32[]{:S(2)}) copy-start(s32[2]{0:T(128)} %param.17) | copy-start | bytes 28
  7.2 259.5 %all-gather.2.cloned.1.call-start = ((), (), s32[]{:S(2)}) async-start(), calls=%async_computation | async-start | bytes 2129920 | tf_op jit(solution)/shard_map/all_gather | solution.py:103
  8.7 390.2 %all-reduce.6.cloned.1.call-start = ((), (), s32[]{:S(2)}) async-start(), calls=%async_computation.1 | async-start | bytes 1048576 | tf_op jit(solution)/shard_map/psum | solution.py:127
  10.1 13.3 %collective-permute-start = (bf16[2,2,256,256]{3,2,1,0:T(8,128)(2,1)S(1)}, bf16[2,2,256,256]{3,2,1,0:T(8,128)(2,1)S(1)}, u32[]{:S(2)}, u32[]{:S(2)}) collective-permute-start(bf16[2,2,256,256]{3,2,1,0:T(8,128)(2,1)S(1)} %convert_bitcast_fusion), channel_id=1, source_target_pairs={{4,0},{8,4},{12,8},{16,12},{20,16},{24,20},{28,24},{32,28},{36,32}... | collective-permute-start | bytes 1572872 | tf_op jit(solution)/shard_map/ppermute | solution.py:19
  23.5 31.7 %collective-permute-start.1 = (bf16[2,2,256,512]{3,2,1,0:T(8,128)(2,1)S(1)}, bf16[2,2,256,512]{3,2,1,0:T(8,128)(2,1)}, u32[]{:S(2)}, u32[]{:S(2)}) collective-permute-start(bf16[2,2,256,512]{3,2,1,0:T(8,128)(2,1)S(1)} %pad_maximum_fusion.3), channel_id=1, source_target_pairs={{32,0},{36,4},{40,8},{44,12},{48,16},{52,20},{56,24},{60,28},{64,3... | collective-permute-start | bytes 3145736 | tf_op jit(solution)/shard_map/ppermute | solution.py:19
  64.2 208.2 %copy-start.2 = (f32[2,256,256]{1,2,0:T(8,128)}, f32[2,256,256]{1,2,0:T(8,128)S(1)}, u32[]{:S(2)}) copy-start(f32[2,256,256]{1,2,0:T(8,128)S(1)} %copy.142) | copy-start | bytes 1572868
  64.4 208.0 %copy-start.4 = (f32[2,256,256]{1,2,0:T(8,128)}, f32[2,256,256]{1,2,0:T(8,128)S(1)}, u32[]{:S(2)}) copy-start(f32[2,256,256]{1,2,0:T(8,128)S(1)} %copy.143) | copy-start | bytes 1572868
  272.4 1.6 copy-start
  279.1 2.5 copy-start.18
  289.7 2.5 copy-start.6
  289.8 2.5 copy-start.8
  303.7 2.2 copy-start.21
  305.9 224.1 %all-reduce.8.cloned.1.call-start = ((), (), s32[]{:S(2)}) async-start(), calls=%async_computation.2 | async-start | bytes 4194304 | tf_op jit(solution)/shard_map/psum | solution.py:157
  407.9 1.3 copy-start.7
  407.9 1.3 copy-start.9
  407.9 1.5 copy-start.11
  418.5 2.5 copy-start.17
  428.9 2.6 copy-start.1
  429.0 2.6 copy-start.3
  429.0 2.6 copy-start.5
  465.9 1.2 copy-start.12
  465.9 1.5 copy-start.13
  465.9 641.9 %all-reduce.10.cloned.1.call-start = ((), (), s32[]{:S(2)}) async-start(), calls=%async_computation.3 | async-start | bytes 8388608
  530.0 27.1 %copy-start.16 = (bf16[2,2,512,512]{2,3,1,0:T(8,128)(2,1)S(1)}, bf16[2,2,512,512]{2,3,1,0:T(8,128)(2,1)}, u32[]{:S(2)}) copy-start(bf16[2,2,512,512]{2,3,1,0:T(8,128)(2,1)} %all-reduce.8.cloned.1.call-done) | copy-start | bytes 6291460
  531.5 30.7 %copy-start.10 = (f32[1,2,2,256,256]{4,3,2,1,0:T(8,128)S(1)}, f32[1,2,2,256,256]{4,3,2,1,0:T(8,128)}, u32[]{:S(2)}) copy-start(f32[1,2,2,256,256]{4,3,2,1,0:T(8,128)} %param.11) | copy-start | bytes 3145732
  531.5 25.6 %collective-permute-start.2 = (bf16[2,2,256,512]{2,3,1,0:T(8,128)(2,1)S(1)}, bf16[2,2,256,512]{2,3,1,0:T(8,128)(2,1)S(1)}, u32[]{:S(2)}, u32[]{:S(2)}) collective-permute-start(bf16[2,2,256,512]{2,3,1,0:T(8,128)(2,1)S(1)} %slice.116), channel_id=1, source_target_pairs={{0,32},{4,36},{8,40},{12,44},{16,48},{20,52},{24,56},{28,60},{32,6... | collective-permute-start | bytes 3145736 | tf_op jit(solution)/shard_map/ppermute | solution.py:19
  557.3 6.8 copy-start.22
  558.2 15.2 %collective-permute-start.3 = (bf16[2,2,256,256]{2,3,1,0:T(8,128)(2,1)}, bf16[2,2,256,256]{2,3,1,0:T(8,128)(2,1)}, u32[]{:S(2)}, u32[]{:S(2)}) collective-permute-start(bf16[2,2,256,256]{2,3,1,0:T(8,128)(2,1)} %slice.159), channel_id=1, source_target_pairs={{0,4},{4,8},{8,12},{12,16},{16,20},{20,24},{24,28},{28,32},{32,36}... | collective-permute-start | bytes 1572872 | tf_op jit(solution)/shard_map/ppermute | solution.py:19
  562.1 7.2 copy-start.24
  563.4 667.3 %copy-start.19 = (f32[4,2,2,4,256]{4,3,2,1,0:T(4,128)S(1)}, f32[4,2,2,4,256]{4,3,2,1,0:T(4,128)}, u32[]{:S(2)}) copy-start(f32[4,2,2,4,256]{4,3,2,1,0:T(4,128)} %param.13) | copy-start | bytes 196612
  563.4 667.3 %copy-start.20 = (f32[4,2,2,4,256]{4,3,2,1,0:T(4,128)S(1)}, f32[4,2,2,4,256]{4,3,2,1,0:T(4,128)}, u32[]{:S(2)}) copy-start(f32[4,2,2,4,256]{4,3,2,1,0:T(4,128)} %param.14) | copy-start | bytes 196612
  566.7 667.1 %copy-start.14 = (f32[1,2,2,256,256]{3,4,2,1,0:T(8,128)S(1)}, f32[1,2,2,256,256]{3,4,2,1,0:T(8,128)}, u32[]{:S(2)}) copy-start(f32[1,2,2,256,256]{3,4,2,1,0:T(8,128)} %copy.196) | copy-start | bytes 3145732
  1236.7 2.6 copy-start.15
Sparse Core Ops, SparseCore 0:
  10.3 256.2 all-gather.1
  306.0 92.8 all-reduce.5
  466.0 63.9 all-reduce.7
  532.5 575.3 all-reduce.9
where the time goes:
time: 1250 us
  waiting for transfers between devices  930 us (74%)
  blocking collectives  121 us (10%)
  matrix products  73.4 us (6%)
  local copies, waits for them, and re-layouts  61.2 us (5%)
  between operations  28.2 us (2%)
  other arithmetic  23.5 us (2%)
    unnamed x5, waiting for transfers between devices  532 us
    all_gather x1, waiting for transfers between devices, body(): lax.all_gather(probe.astype(jnp.bfloat16), 'tile', axis=3, tiled=True)  200 us
    psum x1, blocking collectives, body(): lax.psum((object_sum, probe_sum), ('tile', 'mode'))  121 us
    psum x1, waiting for transfers between devices, body(): power = lax.psum(partial_power, 'mode')  82.1 us
    ppermute x4, waiting for transfers between devices, from_behind(): return lax.ppermute(block, axis, route)  64.6 us
    psum x1, waiting for transfers between devices, body(): lax.psum(region_grad.astype(jnp.bfloat16), 'mode').astype(jnp.float32)  51.3 us
    dot_general x24, matrix products, left_product(): jnp.einsum('ij,...jl->...il', table, right_data, preferred_element_type=j...  35.8 us
    dot_general x24, matrix products, right_product(): jnp.einsum('...jk,kl->...jl', left_data, table, preferred_element_type=jn...  30.9 us
  transfers between devices with their start and end apart: 8, of which 8 were waited for; matrix products, arithmetic and copies ran while one was open for 3% of the time, Pallas kernels for 0%

commit v1 on v0

v1 whole, which is shorter than its diff:
```python
import functools
import math

import jax
import jax.numpy as jnp
import numpy as np
from jax import lax
from jax.experimental import pallas as pl
from jax.experimental.pallas import tpu as pltpu
from jax.sharding import Mesh, PartitionSpec as P

TGX = 8
LAYERS = 2
MODES = 8
SCANS = 4
W = 256
NZ, NYL, NX, NYH, NC = 8, 2, 4, 2, 2
NYLX = NYL * NX
TILES = NZ * NYLX
ROWS = W // TILES
BAND = NYLX * ROWS
TILE_AXES = ("z", "yl", "x")
PLANE = ("yl", "x", "yh")
VMEM = pltpu.VMEM
F32 = jnp.float32
BF16 = jnp.bfloat16


def tables():
    index = np.arange(W, dtype=np.int64)
    angle = ((index[:, None] * index[None, :]) % W).astype(np.float32) * np.float32(2.0 * math.pi / W)
    factor = np.float32(1.0 / math.sqrt(W))
    cosine = np.cos(angle, dtype=np.float32) * factor
    sine = -np.sin(angle, dtype=np.float32) * factor
    plus = np.block([[cosine, sine], [-sine, cosine]])
    minus = np.block([[cosine, -sine], [sine, cosine]])
    free = np.where(index < W // 2, index, index - W).astype(np.float32)
    phase = (free[:, None] * free[:, None] + free[None, :] * free[None, :]) * np.float32(math.pi / (4.0 * W))
    kernel = np.stack([np.cos(phase, dtype=np.float32), np.sin(phase, dtype=np.float32)])
    rows = np.arange(128)
    band, i, ri, r = rows // 16, rows // 8 % 2, rows // 4 % 2, rows % 4
    natural = i * 64 + ri * 32 + band * 4 + r
    order = np.zeros((128, 128), np.float32)
    order[natural, rows] = 1.0
    return plus, minus, kernel, order


def mm(a, b):
    return jnp.dot(a, b, preferred_element_type=F32)


def transform(wave_re, wave_im, right, left):
    across = jnp.concatenate([wave_re, wave_im], axis=1)
    first = mm(across, right).astype(BF16)
    down = jnp.concatenate([first[:, :W], first[:, W:]], axis=0)
    out = mm(left, down).astype(BF16)
    return out[:W], out[W:]


def times(a_re, a_im, b_re, b_im):
    a_re, a_im, b_re, b_im = (v.astype(F32) for v in (a_re, a_im, b_re, b_im))
    return a_re * b_re - a_im * b_im, a_re * b_im + a_im * b_re


def conj_times(a_re, a_im, b_re, b_im):
    a_re, a_im, b_re, b_im = (v.astype(F32) for v in (a_re, a_im, b_re, b_im))
    return a_re * b_re + a_im * b_im, a_re * b_im - a_im * b_re


def window_masks(row, col):
    rows = lax.broadcasted_iota(jnp.int32, (W, W), 0)
    cols = lax.broadcasted_iota(jnp.int32, (W, W), 1)
    return rows >= row, cols >= col


def patch_kernel(info, own, east, south, corner, out):
    row, col = info[0], info[1]
    upper, left = window_masks(row, col)
    for ri in range(2):
        top = jnp.where(left, own[ri].astype(F32), east[ri].astype(F32))
        low = jnp.where(left, south[ri].astype(F32), corner[ri].astype(F32))
        value = jnp.where(upper, top, low)
        value = pltpu.roll(value, (W - row) % W, 0)
        value = pltpu.roll(value, (W - col) % W, 1)
        out[ri] = value.astype(BF16)


def pick_kernel(ids, src, out):
    for d in range(NYLX * NYH):
        out[d] = src[:, ids[d]]


def forward_kernel(info, blocks, mine, other, plus, minus, kern, order, psi, inc, far, power):
    step = pl.program_id(0)
    first = info[2] == 0
    for z in range(NZ):
        piece = blocks[:, 0, z].reshape(128, W)
        placed = mm(order[...], piece).astype(BF16)
        for i in range(2):
            for ri in range(2):
                at = i * 64 + ri * 32
                psi[i, ri, z * BAND : (z + 1) * BAND] = placed[at : at + BAND]
    fwd, inv = plus[...], minus[...]
    p0 = [jnp.where(first, mine[ri], other[ri]) for ri in range(2)]
    p1 = [jnp.where(first, other[ri], mine[ri]) for ri in range(2)]
    total = None
    for i in range(2):
        e_re, e_im = times(psi[i, 0], psi[i, 1], p0[0], p0[1])
        s_re, s_im = transform(e_re.astype(BF16), e_im.astype(BF16), fwd, inv)
        m_re, m_im = times(s_re, s_im, kern[0], kern[1])
        w_re, w_im = transform(m_re.astype(BF16), m_im.astype(BF16), inv, fwd)
        inc[i, 0] = w_re
        inc[i, 1] = w_im
        e_re, e_im = times(w_re, w_im, p1[0], p1[1])
        f_re, f_im = transform(e_re.astype(BF16), e_im.astype(BF16), fwd, inv)
        far[i, 0] = f_re
        far[i, 1] = f_im
        f_re, f_im = f_re.astype(F32), f_im.astype(F32)
        part = f_re * f_re + f_im * f_im
        total = part if total is None else total + part

    @pl.when(step == 0)
    def _():
        power[...] = total

    @pl.when(step != 0)
    def _():
        power[...] += total


def backward_kernel(
    info, psi, inc, far, power_a, power_b, pattern, mine, other, plus, minus, kern, order, terms, out, scratch
):
    step = pl.program_id(0)
    core = info[2]
    first = core == 0
    used = info[4].astype(F32)
    fwd, inv = plus[...], minus[...]
    p0 = [jnp.where(first, mine[ri], other[ri]) for ri in range(2)]
    p1 = [jnp.where(first, other[ri], mine[ri]) for ri in range(2)]
    double = 2.0 * ((power_a[...] + power_b[...] - pattern[0]) * used)
    sums = [None] * 4
    for i in range(2):
        b_re = (double * far[i, 0].astype(F32)).astype(BF16)
        b_im = (double * far[i, 1].astype(F32)).astype(BF16)
        b_re, b_im = transform(b_re, b_im, inv, fwd)
        t1 = conj_times(inc[i, 0], inc[i, 1], b_re, b_im)
        c_re, c_im = conj_times(p1[0], p1[1], b_re, b_im)
        s_re, s_im = transform(c_re.astype(BF16), c_im.astype(BF16), fwd, inv)
        m_re, m_im = times(s_re, s_im, kern[0], -kern[1])
        b_re, b_im = transform(m_re.astype(BF16), m_im.astype(BF16), inv, fwd)
        t0 = conj_times(psi[i, 0], psi[i, 1], b_re, b_im)
        c_re, c_im = conj_times(p0[0], p0[1], b_re, b_im)
        scratch[i, 0] = c_re.astype(BF16)
        scratch[i, 1] = c_im.astype(BF16)
        new = [t0[0], t0[1], t1[0], t1[1]]
        sums = [n if s is None else s + n for s, n in zip(sums, new)]
    back = order[...].T
    for z in range(NZ):
        pieces = [
            scratch[i, ri, z * BAND : (z + 1) * BAND] for i in range(2) for ri in range(2)
        ]
        piece = mm(back, jnp.concatenate(pieces, axis=0)).astype(BF16)
        out[:, 0, z] = piece.reshape(NYLX, 16, W)
    for layer in range(LAYERS):
        slot = core if layer == 0 else 1 - core

        @pl.when(step == 0)
        def _():
            terms[slot, 0] = sums[2 * layer]
            terms[slot, 1] = sums[2 * layer + 1]

        @pl.when(step != 0)
        def _():
            terms[slot, 0] += sums[2 * layer]
            terms[slot, 1] += sums[2 * layer + 1]


def place_kernel(info, mine, theirs, own, right, below, corner):
    row, col = info[0], info[1]
    upper, left = window_masks(row, col)
    zero = jnp.zeros((W, W), F32)
    for ri in range(2):
        value = mine[ri] + theirs[ri].astype(F32)
        value = pltpu.roll(value, row, 0)
        value = pltpu.roll(value, col, 1)
        top = jnp.where(upper, value, zero)
        low = jnp.where(upper, zero, value)
        own[ri] = jnp.where(left, top, zero)
        right[ri] = jnp.where(left, zero, top).astype(BF16)
        below[ri] = jnp.where(left, low, zero).astype(BF16)
        corner[ri] = jnp.where(left, zero, low).astype(BF16)


def scan_sum_kernel(ids, src, out, total):
    total[...] = jnp.zeros_like(total)
    for d in range(NYLX * NYH):
        s = ids[d]
        total[s] += src[d].astype(F32)
    for s in range(SCANS):
        out[:, s] = total[s].astype(BF16)


def shape(dims, dtype):
    return jax.ShapeDtypeStruct(dims, dtype)


def whole(kernel, out_shape, scalars, arrays, scratch=()):
    spec = pl.BlockSpec(memory_space=VMEM)
    single = not isinstance(out_shape, (list, tuple))
    return pl.pallas_call(
        kernel,
        grid_spec=pltpu.PrefetchScalarGridSpec(
            num_scalar_prefetch=1,
            grid=(),
            in_specs=[spec] * len(arrays),
            out_specs=spec if single else [spec] * len(out_shape),
            scratch_shapes=list(scratch),
        ),
        out_shape=out_shape,
    )(scalars, *arrays)


def fixed(dims):
    return pl.BlockSpec(dims, lambda g, info: (0,) * len(dims))


def stepped(dims, axis):
    return pl.BlockSpec(dims, lambda g, info: tuple(g if a == axis else 0 for a in range(len(dims))))


PAIR = (2, 2, W, W)
BLOCKS = (NYLX, 1, NZ, 16, W)
ALL_BLOCKS = (NYLX, NYH, NZ, 16, W)


def forward(info, blocks, mine, other, consts):
    plus, minus, kern, order = consts
    half = (2, W, W)
    return pl.pallas_call(
        forward_kernel,
        grid_spec=pltpu.PrefetchScalarGridSpec(
            num_scalar_prefetch=1,
            grid=(2,),
            in_specs=[
                stepped(BLOCKS, 1),
                fixed(half),
                fixed(half),
                fixed((2 * W, 2 * W)),
                fixed((2 * W, 2 * W)),
                fixed(half),
                fixed((128, 128)),
            ],
            out_specs=[stepped(PAIR, 0), stepped(PAIR, 0), stepped(PAIR, 0), fixed((W, W))],
        ),
        out_shape=[shape((4, 2, W, W), BF16)] * 3 + [shape((W, W), F32)],
        compiler_params=pltpu.CompilerParams(dimension_semantics=("arbitrary",)),
    )(info, blocks, mine, other, plus, minus, kern, order)


def backward(info, psi, inc, far, power_a, power_b, patterns, mine, other, consts):
    plus, minus, kern, order = consts
    half = (2, W, W)
    return pl.pallas_call(
        backward_kernel,
        grid_spec=pltpu.PrefetchScalarGridSpec(
            num_scalar_prefetch=1,
            grid=(2,),
            in_specs=[
                stepped(PAIR, 0),
                stepped(PAIR, 0),
                stepped(PAIR, 0),
                fixed((W, W)),
                fixed((W, W)),
                pl.BlockSpec((1, W, W), lambda g, info: (info[3], 0, 0)),
                fixed(half),
                fixed(half),
                fixed((2 * W, 2 * W)),
                fixed((2 * W, 2 * W)),
                fixed(half),
                fixed((128, 128)),
            ],
            out_specs=[fixed(PAIR), stepped(BLOCKS, 1)],
            scratch_shapes=[VMEM(PAIR, BF16)],
        ),
        out_shape=[shape(PAIR, F32), shape(ALL_BLOCKS, BF16)],
        compiler_params=pltpu.CompilerParams(dimension_semantics=("arbitrary",)),
    )(info, psi, inc, far, power_a, power_b, patterns, mine, other, plus, minus, kern, order)


def swap(value, axis):
    return lax.ppermute(value, axis, [(0, 1), (1, 0)])


def from_tile(value, distance):
    route = [(t + distance, t) for t in range(TILES) if 0 <= t + distance < TILES]
    return lax.ppermute(value, TILE_AXES, route)


def exchange(value, axes):
    return lax.all_to_all(value, axes, 0, 0, tiled=True)


def spread(value, axes, count):
    return exchange(jnp.broadcast_to(value[None], (count,) + value.shape), axes)


def body(
    object_tiles,
    object_previous,
    probe,
    probe_previous,
    patterns,
    offsets,
    scan_of_slot,
    tile_load,
    step_sizes,
    object_norm_before,
    probe_norm_before,
):
    core = lax.axis_index("c")
    slot = lax.axis_index("yh")
    plus, minus, kern, order = tables()
    consts = (
        jnp.asarray(plus, BF16),
        jnp.asarray(minus, BF16),
        jnp.asarray(kern, F32),
        jnp.asarray(order, BF16),
    )
    my_offset = lax.dynamic_index_in_dim(offsets, slot, 1, keepdims=False)
    used = (slot < tile_load[0]).astype(jnp.int32)
    info = jnp.stack([my_offset[0], my_offset[1], core.astype(jnp.int32), slot.astype(jnp.int32), used])

    with jax.named_scope("ids"):
        id_row = jnp.broadcast_to(jnp.pad(scan_of_slot, (0, 126))[None, :], (8, 128))
        ids = spread(id_row, ("yl", "x"), NYLX)[:, 0, :2].reshape(NYLX * NYH)

    with jax.named_scope("object_in"):
        own = lax.dynamic_index_in_dim(object_tiles[0], core, 0, keepdims=False).astype(BF16)
        east, south, corner = (from_tile(own, d) for d in (1, TGX, TGX + 1))

    with jax.named_scope("probe_z"):
        rows = probe.astype(BF16).reshape(SCANS * 16, W)
        banded = spread(rows, "z", NZ).reshape(NZ, SCANS, 16, W)
    with jax.named_scope("probe_plane"):
        picked = whole(pick_kernel, shape((NYLX * NYH, NZ, 16, W), BF16), ids, [banded])
        blocks = exchange(picked, PLANE).reshape(ALL_BLOCKS)

    with jax.named_scope("patch"):
        mine = whole(patch_kernel, shape((2, W, W), BF16), info, [own, east, south, corner])
        other = swap(mine, "c")

    psi, inc, far, power = forward(info, blocks, mine, other, consts)
    with jax.named_scope("power"):
        power_other = swap(power, "c")
    terms, probe_terms = backward(info, psi, inc, far, power, power_other, patterns, mine, other, consts)

    with jax.named_scope("object_core"):
        theirs = swap(terms[1].astype(BF16), "c")
    with jax.named_scope("place"):
        half = (2, W, W)
        kept, right, below, diagonal = whole(
            place_kernel, [shape(half, F32)] + [shape(half, BF16)] * 3, info, [terms[0], theirs]
        )
    with jax.named_scope("object_out"):
        from_left, from_above, from_corner = (
            from_tile(v, -d) for v, d in ((right, 1), (below, TGX), (diagonal, TGX + 1))
        )
    with jax.named_scope("grad_plane"):
        received = exchange(probe_terms.reshape(NYLX * NYH, NZ, 16, W), PLANE)
        by_scan = whole(
            scan_sum_kernel,
            shape((NZ, SCANS, 16, W), BF16),
            ids,
            [received],
            [VMEM((SCANS, NZ, 16, W), F32)],
        )
    with jax.named_scope("object_slots"):
        layer_part = (
            kept + from_left.astype(F32) + from_above.astype(F32) + from_corner.astype(F32)
        ).astype(BF16)
        layer_grad = layer_part.astype(F32) + swap(layer_part, "yh").astype(F32)
    with jax.named_scope("object_layers"):
        other_grad = swap(layer_grad, "c")
        first = core == 0
        tile_grad = jnp.stack(
            [jnp.where(first, layer_grad, other_grad), jnp.where(first, other_grad, layer_grad)]
        )
    with jax.named_scope("grad_z"):
        summed = exchange(by_scan.reshape(NZ, SCANS * 16, W), "z")
        probe_grad = jnp.sum(summed.astype(F32), axis=0).reshape(SCANS, 2, 2, ROWS, W)

    with jax.named_scope("norms"):
        object_part = jnp.sum(tile_grad * tile_grad)
        probe_part = jnp.sum(probe_grad * probe_grad)
        probe_part = probe_part + swap(probe_part.reshape(1), "c")[0]
        lane = lax.broadcasted_iota(jnp.int32, (8, 128), 1)
        packed = jnp.where(lane == 0, object_part, probe_part)
        packed = jnp.sum(spread(packed, PLANE, NYLX * NYH), axis=0)
        packed = jnp.sum(spread(packed, "z", NZ), axis=0)
        object_square = packed[0, 0] / float(NYH * TILES * LAYERS * 2 * W * W)
        probe_square = packed[0, 1] / float(SCANS * MODES * 2 * W * W)

    object_direction = -tile_grad[None] + object_square / object_norm_before[0] * object_previous
    new_object = object_tiles + step_sizes[0].astype(F32) / 1024.0 * object_direction
    probe_direction = -probe_grad + probe_square / probe_norm_before[0] * probe_previous
    new_probe = probe + step_sizes[1].astype(F32) / 16384.0 * probe_direction
    return (new_object, object_direction, new_probe, probe_direction)


def solution(mesh):
    fine = Mesh(mesh.devices.reshape(NZ, NYL, NX, NYH, NC), ("z", "yl", "x", "yh", "c"))
    tile, mode = TILE_AXES, ("yh", "c")
    objects = P(tile, None, None, None, None)
    probes = P(None, mode, None, tile, None)
    return jax.shard_map(
        body,
        mesh=fine,
        in_specs=(
            objects,
            objects,
            probes,
            probes,
            P(tile, None, None),
            P(None, tile),
            P(tile),
            P(tile),
            P(),
            P(),
            P(),
        ),
        out_specs=(objects, objects, probes, probes),
        check_vma=False,
    )
```

time: 1250 us -> 206 us (0.16)
  waiting for transfers between devices: 930 us -> 71.2 us
  blocking collectives: 121 us -> 0 us
  matrix products: 73.4 us -> 0 us
  starting transfers between devices: 10.1 us -> 66.2 us
  local copies, waits for them, and re-layouts: 61.2 us -> 16.9 us
  Pallas kernels: 0 us -> 34.7 us
  between operations: 28.2 us -> 6.77 us
  other arithmetic: 23.5 us -> 8.08 us
    unnamed x5 -> x0, waiting for transfers between devices: 532 us -> none
    all_gather x1 -> x0, waiting for transfers between devices: 200 us -> none  [body(): lax.all_gather(probe.astype(jnp.bfloat16), 'tile', axis=3, tiled=True)]
    psum x2 -> x0, waiting for transfers between devices: 133 us -> none  [the longest x1 82.1 us: body(): power = lax.psum(partial_power, 'mode')]
    psum x1 -> x0, blocking collectives: 121 us -> none  [body(): lax.psum((object_sum, probe_sum), ('tile', 'mode'))]
    dot_general x49 -> x0, matrix products: 73.4 us -> none  [the longest x24 35.8 us: left_product(): jnp.einsum('ij,...jl->...il', table, right_data, preferred_element_type=j...]
    all_to_all x0 -> x7, starting transfers between devices: none -> 44.3 us  [exchange(): return lax.all_to_all(value, axes, 0, 0, tiled=True)]
    pallas_call x0 -> x6, Pallas kernels: none -> 34.7 us  [the longest x1 12.4 us: backward(): pl.pallas_call(backward_kernel, grid_spec=pltpu.PrefetchScalarGridSpec(nu...]
    all_to_all x0 -> x7, waiting for transfers between devices: none -> 34.4 us  [exchange(): return lax.all_to_all(value, axes, 0, 0, tiled=True)]
  transfers between devices with their start and end apart: 8 -> 19, of which waited for: 8 -> 10; matrix products, arithmetic and copies ran while one was open for 3% -> 4% of each run, Pallas kernels for 0% -> 3%
where the time goes in v1:
time: 206 us; the launch traced here: 204 us
  waiting for transfers between devices  71.2 us (35%)
  starting transfers between devices  66.2 us (32%)
  Pallas kernels  34.7 us (17%)
  local copies, waits for them, and re-layouts  16.9 us (8%)
  other arithmetic  8.08 us (4%)
  between operations  6.77 us (3%)
    all_to_all x7, starting transfers between devices, exchange(): return lax.all_to_all(value, axes, 0, 0, tiled=True)  44.3 us
    all_to_all x7, waiting for transfers between devices, exchange(): return lax.all_to_all(value, axes, 0, 0, tiled=True)  34.4 us
    ppermute x6, waiting for transfers between devices, swap(): return lax.ppermute(value, axis, [(0, 1), (1, 0)])  22.5 us
    ppermute x6, waiting for transfers between devices, from_tile(): return lax.ppermute(value, TILE_AXES, route)  14.3 us
    pallas_call x1, Pallas kernels, backward(): pl.pallas_call(backward_kernel, grid_spec=pltpu.PrefetchScalarGridSpec(nu...  12.4 us
    pallas_call x4, Pallas kernels, whole(): pl.pallas_call(kernel, grid_spec=pltpu.PrefetchScalarGridSpec(num_scalar_...  11.8 us
    ppermute x6, starting transfers between devices, from_tile(): return lax.ppermute(value, TILE_AXES, route)  11.4 us
    pallas_call x1, Pallas kernels, forward(): pl.pallas_call(forward_kernel, grid_spec=pltpu.PrefetchScalarGridSpec(num...  10.5 us
  transfers between devices with their start and end apart: 19, of which 10 were waited for; matrix products, arithmetic and copies ran while one was open for 4% of the time, Pallas kernels for 3%

profile of v1, /device:TPU:1, one launch (start us, length us, event | category | flops | bytes accessed | tf_op | source)
XLA Modules:
  0.0 203.8 jit_solution(2186877285129626420)
XLA Ops:
  0.7 0.7 pad.4
  1.3 0.6 broadcast_in_dim.18
  2.0 5.9 %all-to-all-start = ((s32[8,8,128]{2,1,0:T(8,128)}), s32[8,8,128]{2,1,0:T(8,128)S(1)}, u32[]{:S(2)}, u32[]{:S(2)}) async-start(s32[8,8,128]{2,1,0:T(8,128)} %broadcast_in_dim.18), calls=%async_computation | async-start | bytes 65536 | tf_op jit(solution)/shard_map/ids/all_to_all | solution.py:301
  7.9 5.1 %all-to-all-done = s32[8,8,128]{2,1,0:T(8,128)S(1)} async-done(((s32[8,8,128]{2,1,0:T(8,128)}), s32[8,8,128]{2,1,0:T(8,128)S(1)}, u32[]{:S(2)}, u32[]{:S(2)}) %all-to-all-start) | async-done | bytes 32800 | tf_op jit(solution)/shard_map/ids/all_to_all | solution.py:301
  12.9 0.7 broadcast_in_dim.36
  13.7 8.2 %all-to-all-start.1 = ((bf16[8,64,256]{2,1,0:T(8,128)(2,1)}), bf16[8,64,256]{2,1,0:T(8,128)(2,1)S(1)}, u32[]{:S(2)}, u32[]{:S(2)}) async-start(bf16[8,64,256]{2,1,0:T(8,128)(2,1)} %broadcast_in_dim.36), calls=%async_computation.1 | async-start | bytes 524288 | tf_op jit(solution)/shard_map/probe_z/all_to_all | solution.py:301
  21.9 0.6 squeeze.29.ids
  22.4 8.8 %all-to-all-done.1 = bf16[8,64,256]{2,1,0:T(8,128)(2,1)S(1)} async-done(((bf16[8,64,256]{2,1,0:T(8,128)(2,1)}), bf16[8,64,256]{2,1,0:T(8,128)(2,1)S(1)}, u32[]{:S(2)}, u32[]{:S(2)}) %all-to-all-start.1) | async-done | bytes 262176 | tf_op jit(solution)/shard_map/probe_z/all_to_all | solution.py:301
  31.3 0.7 copy-done.5
  32.0 2.6 %probe_plane.1 = bf16[16,8,16,256]{3,2,1,0:T(8,128)(2,1)} custom-call(s32[16]{0:T(128)} %squeeze.29.ids, bf16[8,4,16,256]{3,2,1,0:T(8,128)(2,1)} %bitcast.42), custom_call_target="tpu_custom_call" | custom-call | tf_op jit(solution)/shard_map/probe_plane/pallas_call | solution.py:211
  34.6 4.8 %all-to-all-start.2 = ((bf16[16,8,16,256]{3,2,1,0:T(8,128)(2,1)}), bf16[16,8,16,256]{3,2,1,0:T(8,128)(2,1)S(1)}, u32[]{:S(2)}, u32[]{:S(2)}) async-start(bf16[16,8,16,256]{3,2,1,0:T(8,128)(2,1)} %probe_plane.1), calls=%async_computation.2 | async-start | bytes 2097152 | tf_op jit(solution)/shard_map/probe_plane/all_to_all | solution.py:301
  39.5 1.3 collective-permute-start
  40.8 1.3 collective-permute-start.1
  42.1 1.3 collective-permute-start.2
  44.1 0.6 fusion.11
  44.7 1.8 stack.34.info
  46.5 14.3 %collective-permute-done.east = bf16[2,256,256]{2,1,0:T(8,128)(2,1)S(1)} collective-permute-done((bf16[2,256,256]{2,1,0:T(8,128)(2,1)S(1)}, bf16[2,256,256]{2,1,0:T(8,128)(2,1)S(1)}, u32[]{:S(2)}, u32[]{:S(2)}) %collective-permute-start) | collective-permute-done | bytes 262176 | tf_op jit(solution)/shard_map/object_in/ppermute | solution.py:297
  60.8 0.7 copy-done.8
  61.5 0.1 copy-done.9
  61.6 0.7 copy-done.10
  62.3 3.1 %patch.1.mine = bf16[2,256,256]{2,1,0:T(8,128)(2,1)} custom-call(s32[5]{0:T(128)} %stack.34.info, bf16[2,256,256]{2,1,0:T(8,128)(2,1)} %copy-done.4, bf16[2,256,256]{2,1,0:T(8,128)(2,1)} %copy-done.8, bf16[2,256,256]{2,1,0:T(8,128)(2,1)} %copy-done.9, bf16[2,256,256]{2,1,0:T(8,128)(2,1)} %copy-done.10), custom_call_target="tpu_custom_call" | custom-call | tf_op jit(solution)/shard_map/patch/pallas_call | solution.py:211
  65.4 4.6 %collective-permute-start.3 = (bf16[2,256,256]{2,1,0:T(8,128)(2,1)}, bf16[2,256,256]{2,1,0:T(8,128)(2,1)S(1)}, u32[]{:S(2)}, u32[]{:S(2)}) collective-permute-start(bf16[2,256,256]{2,1,0:T(8,128)(2,1)} %patch.1.mine), channel_id=1, source_target_pairs={{0,1},{1,0},{2,3},{3,2},{4,5},{5,4},{6,7},{7,6},{8,9},{9,8},{10,11... | collective-permute-start | bytes 786440 | tf_op jit(solution)/shard_map/patch/ppermute | solution.py:292
  70.0 1.4 collective-permute-done.3.other
  71.4 0.7 copy-done.6
  72.1 0.3 copy-done.1
  72.4 10.5 %shard_map.174 = (bf16[4,2,256,256]{3,2,1,0:T(8,128)(2,1)}, bf16[4,2,256,256]{3,2,1,0:T(8,128)(2,1)}, bf16[4,2,256,256]{3,2,1,0:T(8,128)(2,1)}, f32[256,256]{1,0:T(8,128)}) custom-call(s32[5]{0:T(128)} %stack.34.info, bf16[8,2,8,16,256]{4,3,2,1,0:T(8,128)(2,1)} %bitcast.40, bf16[2,256,256]{2,1,0:T(8,128)(2,1)} %patch.1.mine, bf16[2,256,256]{2,1,0:T(8,128)(2,1)} %copy-done.6, ...), custom_call_target="tpu_custom_call" | custom-call | tf_op jit(solution)/shard_map/pallas_call | solution.py:240
  83.0 0.5 collective-permute-start.4
  83.4 1.4 collective-permute-done.4.power_b
  84.8 0.7 copy-done.11
  85.5 12.4 %shard_map.175 = (f32[2,2,256,256]{3,2,1,0:T(8,128)}, bf16[8,2,8,16,256]{4,3,2,1,0:T(8,128)(2,1)}) custom-call(s32[5]{0:T(128)} %stack.34.info, bf16[4,2,256,256]{3,2,1,0:T(8,128)(2,1)} %get-tuple-element.14.psi, bf16[4,2,256,256]{3,2,1,0:T(8,128)(2,1)} %get-tuple-element.15.inc, bf16[4,2,256,256]{3,2,1,0:T(8,128)(2,1)} %get-tuple-element.16.far, ...), custom_call_target="tpu_custom_call" | custom-call | tf_op jit(solution)/shard_map/pallas_call | solution.py:264
  97.9 1.1 fusion.3
  98.9 0.4 collective-permute-start.5
  99.4 1.9 slice_bitcast_fusion.mine
  101.2 0.7 copy-done.14
  102.0 3.2 %place.1 = (f32[2,256,256]{2,1,0:T(8,128)}, bf16[2,256,256]{2,1,0:T(8,128)(2,1)}, bf16[2,256,256]{2,1,0:T(8,128)(2,1)}, bf16[2,256,256]{2,1,0:T(8,128)(2,1)}) custom-call(s32[5]{0:T(128)} %stack.34.info, f32[2,256,256]{2,1,0:T(8,128)} %slice_bitcast_fusion.mine, bf16[2,256,256]{2,1,0:T(8,128)(2,1)} %copy-done.14), custom_call_target="tpu_custom_call" | custom-call | tf_op jit(solution)/shard_map/place/pallas_call | solution.py:211
  105.1 2.8 %collective-permute-start.6 = (bf16[2,256,256]{2,1,0:T(8,128)(2,1)}, bf16[2,256,256]{2,1,0:T(8,128)(2,1)S(1)}, u32[]{:S(2)}, u32[]{:S(2)}) collective-permute-start(bf16[2,256,256]{2,1,0:T(8,128)(2,1)} %get-tuple-element.20), channel_id=1, source_target_pairs={{0,4},{4,8},{8,12},{12,16},{16,20},{20,24},{24,28},{28,32},{32,36}... | collective-permute-start | bytes 786440 | tf_op jit(solution)/shard_map/object_out/ppermute | solution.py:297
  107.9 2.0 collective-permute-start.7
  109.9 2.7 %collective-permute-start.8 = (bf16[2,256,256]{2,1,0:T(8,128)(2,1)}, bf16[2,256,256]{2,1,0:T(8,128)(2,1)S(1)}, u32[]{:S(2)}, u32[]{:S(2)}) collective-permute-start(bf16[2,256,256]{2,1,0:T(8,128)(2,1)} %get-tuple-element.22), channel_id=1, source_target_pairs={{0,36},{4,40},{8,44},{12,48},{16,52},{20,56},{24,60},{28,64},{32,6... | collective-permute-start | bytes 786440 | tf_op jit(solution)/shard_map/object_out/ppermute | solution.py:297
  112.6 10.5 %all-to-all-start.3 = ((bf16[16,8,16,256]{3,2,1,0:T(8,128)(2,1)}), bf16[16,8,16,256]{3,2,1,0:T(8,128)(2,1)S(1)}, u32[]{:S(2)}, u32[]{:S(2)}) async-start(bf16[16,8,16,256]{3,2,1,0:T(8,128)(2,1)} %bitcast.16), calls=%async_computation.3 | async-start | bytes 2097152 | tf_op jit(solution)/shard_map/grad_plane/all_to_all | solution.py:301
  123.2 0.7 copy-done.13
  123.9 1.1 add_convert_fusion
  125.0 3.0 %collective-permute-start.9 = (bf16[2,256,256]{2,1,0:T(8,128)(2,1)S(1)}, bf16[2,256,256]{2,1,0:T(8,128)(2,1)S(1)}, u32[]{:S(2)}, u32[]{:S(2)}) collective-permute-start(bf16[2,256,256]{2,1,0:T(8,128)(2,1)S(1)} %add_convert_fusion), channel_id=1, source_target_pairs={{0,2},{2,0},{1,3},{3,1},{4,6},{6,4},{5,7},{7,5},{8,10},{10,8},{9,1... | collective-permute-start | bytes 786440 | tf_op jit(solution)/shard_map/object_slots/ppermute | solution.py:292
  128.0 18.6 %collective-permute-done.9 = bf16[2,256,256]{2,1,0:T(8,128)(2,1)S(1)} collective-permute-done((bf16[2,256,256]{2,1,0:T(8,128)(2,1)S(1)}, bf16[2,256,256]{2,1,0:T(8,128)(2,1)S(1)}, u32[]{:S(2)}, u32[]{:S(2)}) %collective-permute-start.9) | collective-permute-done | bytes 262176 | tf_op jit(solution)/shard_map/object_slots/ppermute | solution.py:292
  146.6 1.6 collective-permute-start.10
  148.3 1.0 copy-done.2
  149.2 2.8 %grad_plane.1 = bf16[8,4,16,256]{3,2,1,0:T(8,128)(2,1)} custom-call(s32[16]{0:T(128)} %squeeze.29.ids, bf16[16,8,16,256]{3,2,1,0:T(8,128)(2,1)} %copy-done.2), custom_call_target="tpu_custom_call" | custom-call | tf_op jit(solution)/shard_map/grad_plane/pallas_call | solution.py:211
  152.1 7.9 %all-to-all-start.4 = ((bf16[8,64,256]{2,1,0:T(8,128)(2,1)}), bf16[8,64,256]{2,1,0:T(8,128)(2,1)S(1)}, u32[]{:S(2)}, u32[]{:S(2)}) async-start(bf16[8,64,256]{2,1,0:T(8,128)(2,1)} %bitcast.41), calls=%async_computation.4 | async-start | bytes 524288 | tf_op jit(solution)/shard_map/grad_z/all_to_all | solution.py:301
  160.0 1.2 fusion.5
  161.2 0.9 fusion.1
  162.1 10.2 %all-to-all-done.4 = bf16[8,64,256]{2,1,0:T(8,128)(2,1)S(1)} async-done(((bf16[8,64,256]{2,1,0:T(8,128)(2,1)}), bf16[8,64,256]{2,1,0:T(8,128)(2,1)S(1)}, u32[]{:S(2)}, u32[]{:S(2)}) %all-to-all-start.4) | async-done | bytes 262176 | tf_op jit(solution)/shard_map/grad_z/all_to_all | solution.py:301
  172.4 0.6 fusion.9
  173.0 0.5 collective-permute-start.11
  173.5 1.1 collective-permute-done.11
  175.8 0.7 compare_select_fusion
  176.4 0.6 broadcast_in_dim.39
  177.1 3.5 %all-to-all-start.5 = ((f32[16,8,128]{2,1,0:T(8,128)}), f32[16,8,128]{2,1,0:T(8,128)S(1)}, u32[]{:S(2)}, u32[]{:S(2)}) async-start(f32[16,8,128]{2,1,0:T(8,128)} %broadcast_in_dim.39), calls=%async_computation.5 | async-start | bytes 131072 | tf_op jit(solution)/shard_map/norms/all_to_all | solution.py:301
  181.3 6.1 %all-to-all-done.5 = f32[16,8,128]{2,1,0:T(8,128)S(1)} async-done(((f32[16,8,128]{2,1,0:T(8,128)}), f32[16,8,128]{2,1,0:T(8,128)S(1)}, u32[]{:S(2)}, u32[]{:S(2)}) %all-to-all-start.5) | async-done | bytes 65568 | tf_op jit(solution)/shard_map/norms/all_to_all | solution.py:301
  187.4 0.6 broadcast_in_dim.40
  188.0 3.5 %all-to-all-start.6 = ((f32[8,8,128]{2,1,0:T(8,128)}), f32[8,8,128]{2,1,0:T(8,128)S(1)}, u32[]{:S(2)}, u32[]{:S(2)}) async-start(f32[8,8,128]{2,1,0:T(8,128)} %broadcast_in_dim.40), calls=%async_computation.6 | async-start | bytes 65536 | tf_op jit(solution)/shard_map/norms/all_to_all | solution.py:301
  191.5 0.6 fusion.12
  194.1 4.2 %all-to-all-done.6 = f32[8,8,128]{2,1,0:T(8,128)S(1)} async-done(((f32[8,8,128]{2,1,0:T(8,128)}), f32[8,8,128]{2,1,0:T(8,128)S(1)}, u32[]{:S(2)}, u32[]{:S(2)}) %all-to-all-start.6) | async-done | bytes 32800 | tf_op jit(solution)/shard_map/norms/all_to_all | solution.py:301
  198.3 0.6 fusion.10
  200.3 0.7 multiply_add_fusion.1
  200.9 2.8 %multiply_add_fusion = (f32[1,2,2,256,256]{4,3,2,1,0:T(8,128)}, f32[1,2,2,256,256]{4,3,2,1,0:T(8,128)}) fusion(f32[1,2,2,256,256]{4,3,2,1,0:T(8,128)S(1)} %copy-done.3, f32[]{:T(128)} %bitcast, f32[1,2,2,256,256]{4,3,2,1,0:T(8,128)} %param.16, f32[]{:T(128)S(6)} %div.30, f32[1,1,2,256,256]{4,3,2,1,0:T(8,128)S(1)} %get-tuple-element.31, ...), kind=kLoop, calls=%fused_computation.4 | loop fusion | flops 1572864 | bytes 5242888 | tf_op jit(solution)/shard_map/add | solution.py:405
  (43 shorter events, 0.4 us)
Async XLA Ops:
  0.6 43.4 %copy-start = (s32[2,2]{1,0:T(2,128)S(1)}, s32[2,2]{1,0:T(2,128)}, u32[]{:S(2)}) copy-start(s32[2,2]{1,0:T(2,128)} %param.20) | copy-start | bytes 52
  0.6 7.2 %copy-start.12 = (f32[4,2,2,4,256]{4,3,2,1,0:T(4,128)S(1)}, f32[4,2,2,4,256]{4,3,2,1,0:T(4,128)}, u32[]{:S(2)}) copy-start(f32[4,2,2,4,256]{4,3,2,1,0:T(4,128)} %param.17) | copy-start | bytes 196612
  2.0 11.0 %all-to-all-start = ((s32[8,8,128]{2,1,0:T(8,128)}), s32[8,8,128]{2,1,0:T(8,128)S(1)}, u32[]{:S(2)}, u32[]{:S(2)}) async-start(s32[8,8,128]{2,1,0:T(8,128)} %broadcast_in_dim.18), calls=%async_computation | async-start | bytes 65536 | tf_op jit(solution)/shard_map/ids/all_to_all | solution.py:301
  13.7 17.6 %all-to-all-start.1 = ((bf16[8,64,256]{2,1,0:T(8,128)(2,1)}), bf16[8,64,256]{2,1,0:T(8,128)(2,1)S(1)}, u32[]{:S(2)}, u32[]{:S(2)}) async-start(bf16[8,64,256]{2,1,0:T(8,128)(2,1)} %broadcast_in_dim.36), calls=%async_computation.1 | async-start | bytes 524288 | tf_op jit(solution)/shard_map/probe_z/all_to_all | solution.py:301
  31.3 0.7 copy-start.5
  34.6 4.8 %copy-start.3 = (f32[1,2,2,256,256]{4,3,2,1,0:T(8,128)S(1)}, f32[1,2,2,256,256]{4,3,2,1,0:T(8,128)}, u32[]{:S(2)}) copy-start(f32[1,2,2,256,256]{4,3,2,1,0:T(8,128)} %param.15) | copy-start | bytes 3145732
  34.6 36.7 %all-to-all-start.2 = ((bf16[16,8,16,256]{3,2,1,0:T(8,128)(2,1)}), bf16[16,8,16,256]{3,2,1,0:T(8,128)(2,1)S(1)}, u32[]{:S(2)}, u32[]{:S(2)}) async-start(bf16[16,8,16,256]{3,2,1,0:T(8,128)(2,1)} %probe_plane.1), calls=%async_computation.2 | async-start | bytes 2097152 | tf_op jit(solution)/shard_map/probe_plane/all_to_all | solution.py:301
  39.5 21.4 %copy-start.4 = (bf16[2,256,256]{2,1,0:T(8,128)(2,1)}, bf16[2,256,256]{2,1,0:T(8,128)(2,1)S(1)}, u32[]{:S(2)}) copy-start(bf16[2,256,256]{2,1,0:T(8,128)(2,1)S(1)} %fusion.2.own) | copy-start | bytes 786436
  39.5 21.3 %collective-permute-start = (bf16[2,256,256]{2,1,0:T(8,128)(2,1)S(1)}, bf16[2,256,256]{2,1,0:T(8,128)(2,1)S(1)}, u32[]{:S(2)}, u32[]{:S(2)}) collective-permute-start(bf16[2,256,256]{2,1,0:T(8,128)(2,1)S(1)} %fusion.2.own), channel_id=1, source_target_pairs={{4,0},{8,4},{12,8},{16,12},{20,16},{24,20},{28,24},{32,28},{36,32}... | collective-permute-start | bytes 786440 | tf_op jit(solution)/shard_map/object_in/ppermute | solution.py:297
  40.8 20.0 %collective-permute-start.1 = (bf16[2,256,256]{2,1,0:T(8,128)(2,1)S(1)}, bf16[2,256,256]{2,1,0:T(8,128)(2,1)S(1)}, u32[]{:S(2)}, u32[]{:S(2)}) collective-permute-start(bf16[2,256,256]{2,1,0:T(8,128)(2,1)S(1)} %fusion.2.own), channel_id=1, source_target_pairs={{32,0},{36,4},{40,8},{44,12},{48,16},{52,20},{56,24},{60,28},{64,3... | collective-permute-start | bytes 786440 | tf_op jit(solution)/shard_map/object_in/ppermute | solution.py:297
  42.1 18.7 %collective-permute-start.2 = (bf16[2,256,256]{2,1,0:T(8,128)(2,1)S(1)}, bf16[2,256,256]{2,1,0:T(8,128)(2,1)S(1)}, u32[]{:S(2)}, u32[]{:S(2)}) collective-permute-start(bf16[2,256,256]{2,1,0:T(8,128)(2,1)S(1)} %fusion.2.own), channel_id=1, source_target_pairs={{36,0},{40,4},{44,8},{48,12},{52,16},{56,20},{60,24},{64,28},{68,3... | collective-permute-start | bytes 786440 | tf_op jit(solution)/shard_map/object_in/ppermute | solution.py:297
  60.8 0.7 copy-start.8
  60.8 0.8 copy-start.9
  61.6 0.7 copy-start.10
  65.4 5.9 %collective-permute-start.3 = (bf16[2,256,256]{2,1,0:T(8,128)(2,1)}, bf16[2,256,256]{2,1,0:T(8,128)(2,1)S(1)}, u32[]{:S(2)}, u32[]{:S(2)}) collective-permute-start(bf16[2,256,256]{2,1,0:T(8,128)(2,1)} %patch.1.mine), channel_id=1, source_target_pairs={{0,1},{1,0},{2,3},{3,2},{4,5},{5,4},{6,7},{7,6},{8,9},{9,8},{10,11... | collective-permute-start | bytes 786440 | tf_op jit(solution)/shard_map/patch/ppermute | solution.py:292
  71.4 0.7 copy-start.6
  71.4 1.1 copy-start.1
  83.0 1.8 collective-permute-start.4
  84.8 0.7 copy-start.11
  98.9 2.3 %collective-permute-start.5 = (bf16[2,256,256]{2,1,0:T(8,128)(2,1)S(1)}, bf16[2,256,256]{2,1,0:T(8,128)(2,1)S(1)}, u32[]{:S(2)}, u32[]{:S(2)}) collective-permute-start(bf16[2,256,256]{2,1,0:T(8,128)(2,1)S(1)} %fusion.3), channel_id=1, source_target_pairs={{0,1},{1,0},{2,3},{3,2},{4,5},{5,4},{6,7},{7,6},{8,9},{9,8},{10,11... | collective-permute-start | bytes 786440 | tf_op jit(solution)/shard_map/object_core/ppermute | solution.py:292
  101.2 0.7 copy-start.14
  105.1 18.1 %collective-permute-start.6 = (bf16[2,256,256]{2,1,0:T(8,128)(2,1)}, bf16[2,256,256]{2,1,0:T(8,128)(2,1)S(1)}, u32[]{:S(2)}, u32[]{:S(2)}) collective-permute-start(bf16[2,256,256]{2,1,0:T(8,128)(2,1)} %get-tuple-element.20), channel_id=1, source_target_pairs={{0,4},{4,8},{8,12},{12,16},{16,20},{20,24},{24,28},{28,32},{32,36}... | collective-permute-start | bytes 786440 | tf_op jit(solution)/shard_map/object_out/ppermute | solution.py:297
  107.9 15.3 %collective-permute-start.7 = (bf16[2,256,256]{2,1,0:T(8,128)(2,1)}, bf16[2,256,256]{2,1,0:T(8,128)(2,1)S(1)}, u32[]{:S(2)}, u32[]{:S(2)}) collective-permute-start(bf16[2,256,256]{2,1,0:T(8,128)(2,1)} %get-tuple-element.21), channel_id=1, source_target_pairs={{0,32},{4,36},{8,40},{12,44},{16,48},{20,52},{24,56},{28,60},{32,6... | collective-permute-start | bytes 786440 | tf_op jit(solution)/shard_map/object_out/ppermute | solution.py:297
  109.9 13.3 %collective-permute-start.8 = (bf16[2,256,256]{2,1,0:T(8,128)(2,1)}, bf16[2,256,256]{2,1,0:T(8,128)(2,1)S(1)}, u32[]{:S(2)}, u32[]{:S(2)}) collective-permute-start(bf16[2,256,256]{2,1,0:T(8,128)(2,1)} %get-tuple-element.22), channel_id=1, source_target_pairs={{0,36},{4,40},{8,44},{12,48},{16,52},{20,56},{24,60},{28,64},{32,6... | collective-permute-start | bytes 786440 | tf_op jit(solution)/shard_map/object_out/ppermute | solution.py:297
  112.6 11.3 %copy-start.7 = (f32[2,256,256]{2,1,0:T(8,128)S(1)}, f32[2,256,256]{2,1,0:T(8,128)}, u32[]{:S(2)}) copy-start(f32[2,256,256]{2,1,0:T(8,128)} %get-tuple-element.19) | copy-start | bytes 1572868
  112.6 35.6 %all-to-all-start.3 = ((bf16[16,8,16,256]{3,2,1,0:T(8,128)(2,1)}), bf16[16,8,16,256]{3,2,1,0:T(8,128)(2,1)S(1)}, u32[]{:S(2)}, u32[]{:S(2)}) async-start(bf16[16,8,16,256]{3,2,1,0:T(8,128)(2,1)} %bitcast.16), calls=%async_computation.3 | async-start | bytes 2097152 | tf_op jit(solution)/shard_map/grad_plane/all_to_all | solution.py:301
  123.2 0.7 copy-start.13
  125.0 21.6 %collective-permute-start.9 = (bf16[2,256,256]{2,1,0:T(8,128)(2,1)S(1)}, bf16[2,256,256]{2,1,0:T(8,128)(2,1)S(1)}, u32[]{:S(2)}, u32[]{:S(2)}) collective-permute-start(bf16[2,256,256]{2,1,0:T(8,128)(2,1)S(1)} %add_convert_fusion), channel_id=1, source_target_pairs={{0,2},{2,0},{1,3},{3,1},{4,6},{6,4},{5,7},{7,5},{8,10},{10,8},{9,1... | collective-permute-start | bytes 786440 | tf_op jit(solution)/shard_map/object_slots/ppermute | solution.py:292
  146.6 13.4 %collective-permute-start.10 = (f32[2,256,256]{2,1,0:T(8,128)S(1)}, f32[2,256,256]{2,1,0:T(8,128)}, u32[]{:S(2)}, u32[]{:S(2)}) collective-permute-start(f32[2,256,256]{2,1,0:T(8,128)S(1)} %convert_add_fusion), channel_id=1, source_target_pairs={{0,1},{1,0},{2,3},{3,2},{4,5},{5,4},{6,7},{7,6},{8,9},{9,8},{10,11... | collective-permute-start | bytes 1572872 | tf_op jit(solution)/shard_map/object_layers/ppermute | solution.py:292
  148.2 1.0 copy-start.2
  152.1 20.3 %all-to-all-start.4 = ((bf16[8,64,256]{2,1,0:T(8,128)(2,1)}), bf16[8,64,256]{2,1,0:T(8,128)(2,1)S(1)}, u32[]{:S(2)}, u32[]{:S(2)}) async-start(bf16[8,64,256]{2,1,0:T(8,128)(2,1)} %bitcast.41), calls=%async_computation.4 | async-start | bytes 524288 | tf_op jit(solution)/shard_map/grad_z/all_to_all | solution.py:301
  173.0 1.6 collective-permute-start.11
  177.1 10.3 %all-to-all-start.5 = ((f32[16,8,128]{2,1,0:T(8,128)}), f32[16,8,128]{2,1,0:T(8,128)S(1)}, u32[]{:S(2)}, u32[]{:S(2)}) async-start(f32[16,8,128]{2,1,0:T(8,128)} %broadcast_in_dim.39), calls=%async_computation.5 | async-start | bytes 131072 | tf_op jit(solution)/shard_map/norms/all_to_all | solution.py:301
  188.0 3.5 %copy-start.16 = (s32[2]{0:T(128)S(1)}, s32[2]{0:T(128)}, u32[]{:S(2)}) copy-start(s32[2]{0:T(128)} %param.23) | copy-start | bytes 28
  188.0 10.3 %all-to-all-start.6 = ((f32[8,8,128]{2,1,0:T(8,128)}), f32[8,8,128]{2,1,0:T(8,128)S(1)}, u32[]{:S(2)}, u32[]{:S(2)}) async-start(f32[8,8,128]{2,1,0:T(8,128)} %broadcast_in_dim.40), calls=%async_computation.6 | async-start | bytes 65536 | tf_op jit(solution)/shard_map/norms/all_to_all | solution.py:301
  194.1 6.2 %copy-start.15 = (f32[4,2,2,4,256]{4,3,2,1,0:T(4,128)S(1)}, f32[4,2,2,4,256]{4,3,2,1,0:T(4,128)}, u32[]{:S(2)}) copy-start(f32[4,2,2,4,256]{4,3,2,1,0:T(4,128)} %param.18) | copy-start | bytes 196612

commit v2 on v1

--- a/solution.py
+++ b/solution.py
@@ -1,4 +1,3 @@
-import functools
 import math
 
 import jax
@@ -73,13 +72,12 @@
     return rows >= row, cols >= col
 
 
-def patch_kernel(info, own, east, south, corner, out):
+def patch_kernel(info, own, east, low, out):
     row, col = info[0], info[1]
     upper, left = window_masks(row, col)
     for ri in range(2):
         top = jnp.where(left, own[ri].astype(F32), east[ri].astype(F32))
-        low = jnp.where(left, south[ri].astype(F32), corner[ri].astype(F32))
-        value = jnp.where(upper, top, low)
+        value = jnp.where(upper, top, low[ri].astype(F32))
         value = pltpu.roll(value, (W - row) % W, 0)
         value = pltpu.roll(value, (W - col) % W, 1)
         out[ri] = value.astype(BF16)
@@ -176,20 +174,16 @@
             terms[slot, 1] += sums[2 * layer + 1]
 
 
-def place_kernel(info, mine, theirs, own, right, below, corner):
+def place_kernel(info, mine, theirs, up, low):
     row, col = info[0], info[1]
-    upper, left = window_masks(row, col)
+    upper, _ = window_masks(row, col)
     zero = jnp.zeros((W, W), F32)
     for ri in range(2):
         value = mine[ri] + theirs[ri].astype(F32)
         value = pltpu.roll(value, row, 0)
         value = pltpu.roll(value, col, 1)
-        top = jnp.where(upper, value, zero)
-        low = jnp.where(upper, zero, value)
-        own[ri] = jnp.where(left, top, zero)
-        right[ri] = jnp.where(left, zero, top).astype(BF16)
-        below[ri] = jnp.where(left, low, zero).astype(BF16)
-        corner[ri] = jnp.where(left, zero, low).astype(BF16)
+        up[ri] = jnp.where(upper, value, zero)
+        low[ri] = jnp.where(upper, zero, value).astype(BF16)
 
 
 def scan_sum_kernel(ids, src, out, total):
@@ -218,6 +212,7 @@
             scratch_shapes=list(scratch),
         ),
         out_shape=out_shape,
+        compiler_params=pltpu.CompilerParams(vmem_limit_bytes=8 << 20),
     )(scalars, *arrays)
 
 
@@ -254,7 +249,7 @@
             out_specs=[stepped(PAIR, 0), stepped(PAIR, 0), stepped(PAIR, 0), fixed((W, W))],
         ),
         out_shape=[shape((4, 2, W, W), BF16)] * 3 + [shape((W, W), F32)],
-        compiler_params=pltpu.CompilerParams(dimension_semantics=("arbitrary",)),
+        compiler_params=pltpu.CompilerParams(dimension_semantics=("arbitrary",), vmem_limit_bytes=28 << 20),
     )(info, blocks, mine, other, plus, minus, kern, order)
 
 
@@ -284,7 +279,7 @@
             scratch_shapes=[VMEM(PAIR, BF16)],
         ),
         out_shape=[shape(PAIR, F32), shape(ALL_BLOCKS, BF16)],
-        compiler_params=pltpu.CompilerParams(dimension_semantics=("arbitrary",)),
+        compiler_params=pltpu.CompilerParams(dimension_semantics=("arbitrary",), vmem_limit_bytes=28 << 20),
     )(info, psi, inc, far, power_a, power_b, patterns, mine, other, plus, minus, kern, order)
 
 
@@ -305,7 +300,7 @@
     return exchange(jnp.broadcast_to(value[None], (count,) + value.shape), axes)
 
 
-def body(
+def update(
     object_tiles,
     object_previous,
     probe,
@@ -330,76 +325,65 @@
     my_offset = lax.dynamic_index_in_dim(offsets, slot, 1, keepdims=False)
     used = (slot < tile_load[0]).astype(jnp.int32)
     info = jnp.stack([my_offset[0], my_offset[1], core.astype(jnp.int32), slot.astype(jnp.int32), used])
-
-    with jax.named_scope("ids"):
-        id_row = jnp.broadcast_to(jnp.pad(scan_of_slot, (0, 126))[None, :], (8, 128))
-        ids = spread(id_row, ("yl", "x"), NYLX)[:, 0, :2].reshape(NYLX * NYH)
-
-    with jax.named_scope("object_in"):
-        own = lax.dynamic_index_in_dim(object_tiles[0], core, 0, keepdims=False).astype(BF16)
-        east, south, corner = (from_tile(own, d) for d in (1, TGX, TGX + 1))
-
-    with jax.named_scope("probe_z"):
-        rows = probe.astype(BF16).reshape(SCANS * 16, W)
-        banded = spread(rows, "z", NZ).reshape(NZ, SCANS, 16, W)
-    with jax.named_scope("probe_plane"):
-        picked = whole(pick_kernel, shape((NYLX * NYH, NZ, 16, W), BF16), ids, [banded])
-        blocks = exchange(picked, PLANE).reshape(ALL_BLOCKS)
-
-    with jax.named_scope("patch"):
-        mine = whole(patch_kernel, shape((2, W, W), BF16), info, [own, east, south, corner])
-        other = swap(mine, "c")
+    columns = lax.broadcasted_iota(jnp.int32, (1, 1, W), 2)
+    my_left = columns >= my_offset[1]
+
+    at = lax.broadcasted_iota(jnp.int32, (1, 128), 1)
+    here = 2 * (NX * lax.axis_index("yl") + lax.axis_index("x"))
+    row = jnp.where(at == here, scan_of_slot[0], 0) + jnp.where(at == here + 1, scan_of_slot[1], 0)
+    rows = [row]
+    for d in range(1, NX):
+        rows.append(lax.ppermute(row, "x", [((x + d) % NX, x) for x in range(NX)]))
+    row = sum(rows[1:], rows[0])
+    row = row + swap(row, "yl")
+    ids = row[0, : NYLX * NYH]
+
+    own = lax.dynamic_index_in_dim(object_tiles[0], core, 0, keepdims=False).astype(BF16)
+    col_row = jnp.broadcast_to(my_offset[1].reshape(1, 1), (1, 128))
+    above_col = from_tile(col_row, -TGX)[:1, :1].reshape(1, 1, 1)
+    above_left = columns >= above_col
+    east = from_tile(own, 1)
+    south = from_tile(jnp.where(above_left, own, east), TGX)
+
+    rows = probe.astype(BF16).reshape(SCANS * 16, W)
+    banded = spread(rows, "z", NZ).reshape(NZ, SCANS, 16, W)
+    picked = whole(pick_kernel, shape((NYLX * NYH, NZ, 16, W), BF16), ids, [banded])
+    blocks = exchange(picked, PLANE).reshape(ALL_BLOCKS)
+
+    mine = whole(patch_kernel, shape((2, W, W), BF16), info, [own, east, south])
+    other = swap(mine, "c")
 
     psi, inc, far, power = forward(info, blocks, mine, other, consts)
-    with jax.named_scope("power"):
-        power_other = swap(power, "c")
+    power_other = swap(power, "c")
     terms, probe_terms = backward(info, psi, inc, far, power, power_other, patterns, mine, other, consts)
 
-    with jax.named_scope("object_core"):
-        theirs = swap(terms[1].astype(BF16), "c")
-    with jax.named_scope("place"):
-        half = (2, W, W)
-        kept, right, below, diagonal = whole(
-            place_kernel, [shape(half, F32)] + [shape(half, BF16)] * 3, info, [terms[0], theirs]
-        )
-    with jax.named_scope("object_out"):
-        from_left, from_above, from_corner = (
-            from_tile(v, -d) for v, d in ((right, 1), (below, TGX), (diagonal, TGX + 1))
-        )
-    with jax.named_scope("grad_plane"):
-        received = exchange(probe_terms.reshape(NYLX * NYH, NZ, 16, W), PLANE)
-        by_scan = whole(
-            scan_sum_kernel,
-            shape((NZ, SCANS, 16, W), BF16),
-            ids,
-            [received],
-            [VMEM((SCANS, NZ, 16, W), F32)],
-        )
-    with jax.named_scope("object_slots"):
-        layer_part = (
-            kept + from_left.astype(F32) + from_above.astype(F32) + from_corner.astype(F32)
-        ).astype(BF16)
-        layer_grad = layer_part.astype(F32) + swap(layer_part, "yh").astype(F32)
-    with jax.named_scope("object_layers"):
-        other_grad = swap(layer_grad, "c")
-        first = core == 0
-        tile_grad = jnp.stack(
-            [jnp.where(first, layer_grad, other_grad), jnp.where(first, other_grad, layer_grad)]
-        )
-    with jax.named_scope("grad_z"):
-        summed = exchange(by_scan.reshape(NZ, SCANS * 16, W), "z")
-        probe_grad = jnp.sum(summed.astype(F32), axis=0).reshape(SCANS, 2, 2, ROWS, W)
-
-    with jax.named_scope("norms"):
-        object_part = jnp.sum(tile_grad * tile_grad)
-        probe_part = jnp.sum(probe_grad * probe_grad)
-        probe_part = probe_part + swap(probe_part.reshape(1), "c")[0]
-        lane = lax.broadcasted_iota(jnp.int32, (8, 128), 1)
-        packed = jnp.where(lane == 0, object_part, probe_part)
-        packed = jnp.sum(spread(packed, PLANE, NYLX * NYH), axis=0)
-        packed = jnp.sum(spread(packed, "z", NZ), axis=0)
-        object_square = packed[0, 0] / float(NYH * TILES * LAYERS * 2 * W * W)
-        probe_square = packed[0, 1] / float(SCANS * MODES * 2 * W * W)
+    theirs = swap(terms[1].astype(BF16), "c")
+    half = (2, W, W)
+    up, low = whole(place_kernel, [shape(half, F32), shape(half, BF16)], info, [terms[0], theirs])
+    from_above = from_tile(low, -TGX).astype(F32)
+    kept = jnp.where(my_left, up, 0.0) + jnp.where(above_left, from_above, 0.0)
+    right = jnp.where(my_left, 0.0, up) + jnp.where(above_left, 0.0, from_above)
+    from_left = from_tile(right.astype(BF16), -1)
+    received = exchange(probe_terms.reshape(NYLX * NYH, NZ, 16, W), PLANE)
+    by_scan = whole(scan_sum_kernel, shape((NZ, SCANS, 16, W), BF16), ids, [received], [VMEM((SCANS, NZ, 16, W), F32)])
+    layer_part = (kept + from_left.astype(F32)).astype(BF16)
+    layer_grad = layer_part.astype(F32) + swap(layer_part, "yh").astype(F32)
+    other_grad = swap(layer_grad, "c")
+    first = core == 0
+    tile_grad = jnp.stack(
+        [jnp.where(first, layer_grad, other_grad), jnp.where(first, other_grad, layer_grad)]
+    )
+    summed = exchange(by_scan.reshape(NZ, SCANS * 16, W), "z")
+    probe_grad = jnp.sum(summed.astype(F32), axis=0).reshape(SCANS, 2, 2, ROWS, W)
+
+    lane = lax.broadcasted_iota(jnp.int32, (1, 128), 1)
+    object_part = jnp.sum(layer_grad * layer_grad)
+    probe_part = jnp.sum(probe_grad * probe_grad)
+    packed = jnp.where(lane == 0, object_part, probe_part)
+    packed = packed + swap(packed, "c")
+    packed = jnp.sum(spread(packed, ("z",) + PLANE, TILES * NYH), axis=0)
+    object_square = packed[0, 0] / float(NYH * TILES * LAYERS * 2 * W * W)
+    probe_square = packed[0, 1] / float(SCANS * MODES * 2 * W * W)
 
     object_direction = -tile_grad[None] + object_square / object_norm_before[0] * object_previous
     new_object = object_tiles + step_sizes[0].astype(F32) / 1024.0 * object_direction
@@ -414,7 +398,7 @@
     objects = P(tile, None, None, None, None)
     probes = P(None, mode, None, tile, None)
     return jax.shard_map(
-        body,
+        update,
         mesh=fine,
         in_specs=(
             objects,

time: 206 us -> 163 us (0.79)
  waiting for transfers between devices: 71.2 us -> 46.3 us
  Pallas kernels: 34.7 us -> 21.8 us
  local copies, waits for them, and re-layouts: 16.9 us -> 9.97 us
  other arithmetic: 8.08 us -> 13.5 us
    all_to_all x7 -> x5, waiting for transfers between devices: 34.4 us -> 17.2 us  [exchange(): return lax.all_to_all(value, axes, 0, 0, tiled=True)]
    ppermute x6 -> x7, waiting for transfers between devices: 22.5 us -> 10.7 us  [swap(): return lax.ppermute(value, axis, [(0, 1), (1, 0)])]
    all_to_all x7 -> x5, starting transfers between devices: 44.3 us -> 35.5 us  [exchange(): return lax.all_to_all(value, axes, 0, 0, tiled=True)]
    pallas_call x4, Pallas kernels: 11.8 us -> 4.97 us  [whole(): pl.pallas_call(kernel, grid_spec=pltpu.PrefetchScalarGridSpec(num_scalar_...]
    ppermute x0 -> x3, starting transfers between devices: none -> 4.5 us  [update(): rows.append(lax.ppermute(row, 'x', [((x + d) % NX, x) for x in range(NX)]))]
    ppermute x6 -> x5, waiting for transfers between devices: 14.3 us -> 18.4 us  [from_tile(): return lax.ppermute(value, TILE_AXES, route)]
    pallas_call x1, Pallas kernels: 12.4 us -> 8.94 us  [backward(): pl.pallas_call(backward_kernel, grid_spec=pltpu.PrefetchScalarGridSpec(nu...]
    unnamed x34 -> x36, local copies, waits for them, and re-layouts: 6.34 us -> 3.02 us
  transfers between devices with their start and end apart: 19 -> 20, of which waited for: 10 -> 12; matrix products, arithmetic and copies ran while one was open for 4% -> 6% of each run, Pallas kernels for 3% -> 3%
where the time goes in v2:
time: 163 us; the launch traced here: 162 us
  starting transfers between devices  65.1 us (40%)
  waiting for transfers between devices  46.3 us (28%)
  Pallas kernels  21.8 us (13%)
  other arithmetic  13.5 us (8%)
  local copies, waits for them, and re-layouts  9.97 us (6%)
  between operations  5.65 us (3%)
    all_to_all x5, starting transfers between devices, exchange(): return lax.all_to_all(value, axes, 0, 0, tiled=True)  35.5 us
    ppermute x5, waiting for transfers between devices, from_tile(): return lax.ppermute(value, TILE_AXES, route)  18.4 us
    all_to_all x5, waiting for transfers between devices, exchange(): return lax.all_to_all(value, axes, 0, 0, tiled=True)  17.2 us
    ppermute x7, starting transfers between devices, swap(): return lax.ppermute(value, axis, [(0, 1), (1, 0)])  13.3 us
    ppermute x5, starting transfers between devices, from_tile(): return lax.ppermute(value, TILE_AXES, route)  11.8 us
    ppermute x7, waiting for transfers between devices, swap(): return lax.ppermute(value, axis, [(0, 1), (1, 0)])  10.7 us
    pallas_call x1, Pallas kernels, backward(): pl.pallas_call(backward_kernel, grid_spec=pltpu.PrefetchScalarGridSpec(nu...  8.94 us
    pallas_call x1, Pallas kernels, forward(): pl.pallas_call(forward_kernel, grid_spec=pltpu.PrefetchScalarGridSpec(num...  7.87 us
  transfers between devices with their start and end apart: 20, of which 12 were waited for; matrix products, arithmetic and copies ran while one was open for 6% of the time, Pallas kernels for 3%

profile of v2, /device:TPU:1, one launch (start us, length us, event | category | flops | bytes accessed | tf_op | source)
XLA Modules:
  0.0 162.3 jit_solution(12112930105793356061)
XLA Ops:
  0.7 0.6 copy-done.16
  1.3 0.6 fusion.14
  1.9 1.3 fusion.8
  3.2 3.4 %collective-permute-start = (s32[1,128]{1,0:T(1,128)S(1)}, s32[1,128]{1,0:T(1,128)S(1)}, u32[]{:S(2)}, u32[]{:S(2)}) collective-permute-start(s32[1,128]{1,0:T(1,128)S(1)} %fusion.8), channel_id=1, source_target_pairs={{4,0},{8,4},{12,8},{0,12},{5,1},{9,5},{13,9},{1,13},{6,2},{10,6},{... | collective-permute-start | bytes 1544 | tf_op jit(solution)/shard_map/ppermute | solution.py:336
  6.6 0.5 collective-permute-start.1
  7.1 0.6 collective-permute-start.2
  7.7 1.1 fusion.6.own
  8.8 1.3 collective-permute-start.4
  10.2 0.7 broadcast_in_dim.82
  10.9 11.9 %all-to-all-start = ((bf16[8,64,256]{2,1,0:T(8,128)(2,1)}), bf16[8,64,256]{2,1,0:T(8,128)(2,1)S(1)}, u32[]{:S(2)}, u32[]{:S(2)}) async-start(bf16[8,64,256]{2,1,0:T(8,128)(2,1)} %broadcast_in_dim.82), calls=%async_computation | async-start | bytes 524288 | tf_op jit(solution)/shard_map/all_to_all | solution.py:296
  22.8 1.3 add_add_fusion
  24.1 0.3 collective-permute-start.3
  24.4 0.1 constant_dynamic-slice_fusion
  24.4 2.2 %collective-permute-done.3 = s32[1,128]{1,0:T(1,128)S(1)} collective-permute-done((s32[1,128]{1,0:T(1,128)S(1)}, s32[1,128]{1,0:T(1,128)S(1)}, u32[]{:S(2)}, u32[]{:S(2)}) %collective-permute-start.3) | collective-permute-done | bytes 544 | tf_op jit(solution)/shard_map/ppermute | solution.py:287
  26.6 5.4 %all-to-all-done = bf16[8,64,256]{2,1,0:T(8,128)(2,1)S(1)} async-done(((bf16[8,64,256]{2,1,0:T(8,128)(2,1)}), bf16[8,64,256]{2,1,0:T(8,128)(2,1)S(1)}, u32[]{:S(2)}, u32[]{:S(2)}) %all-to-all-start) | async-done | bytes 262176 | tf_op jit(solution)/shard_map/all_to_all | solution.py:296
  32.0 1.6 shard_map.174
  33.5 4.2 %all-to-all-start.1 = ((bf16[16,8,16,256]{3,2,1,0:T(8,128)(2,1)}), bf16[16,8,16,256]{3,2,1,0:T(8,128)(2,1)S(1)}, u32[]{:S(2)}, u32[]{:S(2)}) async-start(bf16[16,8,16,256]{3,2,1,0:T(8,128)(2,1)} %shard_map.174), calls=%async_computation.1 | async-start | bytes 2097152 | tf_op jit(solution)/shard_map/all_to_all | solution.py:296
  37.8 0.5 fusion.11
  38.3 0.6 broadcast_in_dim.83
  39.0 2.3 %collective-permute-start.5 = (s32[1,128]{1,0:T(1,128)S(1)}, s32[1,128]{1,0:T(1,128)S(1)}, u32[]{:S(2)}, u32[]{:S(2)}) collective-permute-start(s32[1,128]{1,0:T(1,128)S(1)} %broadcast_in_dim.83), channel_id=1, source_target_pairs={{0,32},{4,36},{8,40},{12,44},{16,48},{20,52},{24,56},{28,60},{32,6... | collective-permute-start | bytes 1544 | tf_op jit(solution)/shard_map/ppermute | solution.py:292
  41.2 0.7 collective-permute-done.5
  42.0 1.9 %broadcast_select_fusion = bf16[2,256,256]{2,1,0:T(8,128)(2,1)} fusion(bf16[2,256,256]{2,1,0:T(8,128)(2,1)S(1)} %collective-permute-done.4.east, pred[256]{0:T(512)(128)(4,1)S(1)} %iota_compare_fusion, f32[1,2,2,256,256]{4,3,2,1,0:T(8,128)} %param.15, s32[]{:T(128)S(6)} %select_n.77), kind=kLoop, calls=%fused_computation.20 | loop fusion | flops 131072 | bytes 786692 | tf_op jit(solution)/shard_map/jit(_where)/select_n | solution.py:346
  43.9 1.3 collective-permute-start.6
  45.8 1.4 stack.28.info
  47.2 4.5 %collective-permute-done.6.low = bf16[2,256,256]{2,1,0:T(8,128)(2,1)S(1)} collective-permute-done((bf16[2,256,256]{2,1,0:T(8,128)(2,1)}, bf16[2,256,256]{2,1,0:T(8,128)(2,1)S(1)}, u32[]{:S(2)}, u32[]{:S(2)}) %collective-permute-start.6) | collective-permute-done | bytes 262176 | tf_op jit(solution)/shard_map/ppermute | solution.py:292
  51.7 0.7 copy-done.6
  52.4 0.9 copy-done.7
  53.4 1.1 shard_map.175.mine
  54.4 5.7 %collective-permute-start.7 = (bf16[2,256,256]{2,1,0:T(8,128)(2,1)S(1)}, bf16[2,256,256]{2,1,0:T(8,128)(2,1)S(1)}, u32[]{:S(2)}, u32[]{:S(2)}) collective-permute-start(bf16[2,256,256]{2,1,0:T(8,128)(2,1)S(1)} %shard_map.175.mine), channel_id=1, source_target_pairs={{0,1},{1,0},{2,3},{3,2},{4,5},{5,4},{6,7},{7,6},{8,9},{9,8},{10,11... | collective-permute-start | bytes 786440 | tf_op jit(solution)/shard_map/ppermute | solution.py:287
  60.1 1.2 collective-permute-done.7.other
  61.3 7.9 %shard_map.176 = (bf16[4,2,256,256]{3,2,1,0:T(8,128)(2,1)S(1)}, bf16[4,2,256,256]{3,2,1,0:T(8,128)(2,1)S(1)}, bf16[4,2,256,256]{3,2,1,0:T(8,128)(2,1)S(1)}, f32[256,256]{1,0:T(8,128)S(1)}) custom-call(s32[5]{0:T(128)S(1)} %stack.28.info, bf16[8,2,8,16,256]{4,3,2,1,0:T(8,128)(2,1)S(1)} %bitcast.47, bf16[2,256,256]{2,1,0:T(8,128)(2,1)S(1)} %shard_map.175.mine, ...), custom_call_target="tpu_custom_call" | custom-call | tf_op jit(solution)/shard_map/pallas_call | solution.py:235
  69.2 0.5 collective-permute-start.8
  69.6 1.2 collective-permute-done.8.power_b
  70.8 8.9 %shard_map.177 = (f32[2,2,256,256]{3,2,1,0:T(8,128)S(1)}, bf16[8,2,8,16,256]{4,3,2,1,0:T(8,128)(2,1)S(1)}) custom-call(s32[5]{0:T(128)S(1)} %stack.28.info, bf16[4,2,256,256]{3,2,1,0:T(8,128)(2,1)S(1)} %get-tuple-element.12.psi, bf16[4,2,256,256]{3,2,1,0:T(8,128)(2,1)S(1)} %get-tuple-element.13.inc, bf16[4,2,256,256]{3,2,1,0:T(8,128)(2,1)S(1)} %get-tuple-element.14.far, ...), custom_call_target="tpu_custom_call" | custom-call | tf_op jit(solution)/shard_map/pallas_call | solution.py:259
  79.8 0.6 collective-permute-start.9
  80.5 1.1 collective-permute-done.9.theirs
  81.6 0.8 shard_map.178
  82.5 3.7 %collective-permute-start.10 = (bf16[2,256,256]{2,1,0:T(8,128)(2,1)S(1)}, bf16[2,256,256]{2,1,0:T(8,128)(2,1)S(1)}, u32[]{:S(2)}, u32[]{:S(2)}) collective-permute-start(bf16[2,256,256]{2,1,0:T(8,128)(2,1)S(1)} %get-tuple-element.18), channel_id=1, source_target_pairs={{0,32},{4,36},{8,40},{12,44},{16,48},{20,52},{24,56},{28,60},{32,6... | collective-permute-start | bytes 786440 | tf_op jit(solution)/shard_map/ppermute | solution.py:292
  86.1 0.7 iota_compare_fusion.1
  86.8 6.9 %all-to-all-start.2 = ((bf16[16,8,16,256]{3,2,1,0:T(8,128)(2,1)}), bf16[16,8,16,256]{3,2,1,0:T(8,128)(2,1)S(1)}, u32[]{:S(2)}, u32[]{:S(2)}) async-start(bf16[16,8,16,256]{3,2,1,0:T(8,128)(2,1)} %bitcast.49), calls=%async_computation.2 | async-start | bytes 2097152 | tf_op jit(solution)/shard_map/all_to_all | solution.py:296
  93.8 0.1 fusion.5
  93.9 3.3 %collective-permute-start.11 = (bf16[2,256,256]{2,1,0:T(8,128)(2,1)S(1)}, bf16[2,256,256]{2,1,0:T(8,128)(2,1)S(1)}, u32[]{:S(2)}, u32[]{:S(2)}) collective-permute-start(bf16[2,256,256]{2,1,0:T(8,128)(2,1)S(1)} %fusion.5), channel_id=1, source_target_pairs={{0,4},{4,8},{8,12},{12,16},{16,20},{20,24},{24,28},{28,32},{32,36}... | collective-permute-start | bytes 786440 | tf_op jit(solution)/shard_map/ppermute | solution.py:292
  97.1 13.1 %collective-permute-done.11 = bf16[2,256,256]{2,1,0:T(8,128)(2,1)S(1)} collective-permute-done((bf16[2,256,256]{2,1,0:T(8,128)(2,1)S(1)}, bf16[2,256,256]{2,1,0:T(8,128)(2,1)S(1)}, u32[]{:S(2)}, u32[]{:S(2)}) %collective-permute-start.11) | collective-permute-done | bytes 262176 | tf_op jit(solution)/shard_map/ppermute | solution.py:292
  110.3 0.1 fusion.3
  110.4 3.2 %collective-permute-start.12 = (bf16[2,256,256]{2,1,0:T(8,128)(2,1)S(1)}, bf16[2,256,256]{2,1,0:T(8,128)(2,1)S(1)}, u32[]{:S(2)}, u32[]{:S(2)}) collective-permute-start(bf16[2,256,256]{2,1,0:T(8,128)(2,1)S(1)} %fusion.3), channel_id=1, source_target_pairs={{0,2},{2,0},{1,3},{3,1},{4,6},{6,4},{5,7},{7,5},{8,10},{10,8},{9,1... | collective-permute-start | bytes 786440 | tf_op jit(solution)/shard_map/ppermute | solution.py:287
  113.7 1.5 shard_map.179
  115.1 4.6 %all-to-all-start.3 = ((bf16[8,64,256]{2,1,0:T(8,128)(2,1)}), bf16[8,64,256]{2,1,0:T(8,128)(2,1)S(1)}, u32[]{:S(2)}, u32[]{:S(2)}) async-start(bf16[8,64,256]{2,1,0:T(8,128)(2,1)} %bitcast.20), calls=%async_computation.3 | async-start | bytes 524288 | tf_op jit(solution)/shard_map/all_to_all | solution.py:296
  119.7 4.2 %collective-permute-done.12 = bf16[2,256,256]{2,1,0:T(8,128)(2,1)S(1)} collective-permute-done((bf16[2,256,256]{2,1,0:T(8,128)(2,1)S(1)}, bf16[2,256,256]{2,1,0:T(8,128)(2,1)S(1)}, u32[]{:S(2)}, u32[]{:S(2)}) %collective-permute-start.12) | collective-permute-done | bytes 262176 | tf_op jit(solution)/shard_map/ppermute | solution.py:287
  124.0 0.6 copy-done.11
  124.7 0.5 collective-permute-start.13
  125.1 4.9 %all-to-all-done.3 = bf16[8,64,256]{2,1,0:T(8,128)(2,1)S(1)} async-done(((bf16[8,64,256]{2,1,0:T(8,128)(2,1)}), bf16[8,64,256]{2,1,0:T(8,128)(2,1)S(1)}, u32[]{:S(2)}, u32[]{:S(2)}) %all-to-all-start.3) | async-done | bytes 262176 | tf_op jit(solution)/shard_map/all_to_all | solution.py:296
  130.1 1.2 fusion.10
  131.4 1.9 %select_bitcast_fusion.1 = (f32[1,1,2,256,256]{4,3,2,1,0:T(8,128)S(1)}, f32[1,1,2,256,256]{4,3,2,1,0:T(8,128)S(1)}, f32[]{:T(128)}) fusion(f32[2,256,256]{2,1,0:T(8,128)} %collective-permute-done.13, pred[]{:T(512)S(6)} %eq.43, bf16[2,256,256]{2,1,0:T(8,128)(2,1)S(1)} %copy-done.12, bf16[2,256,256]{2,1,0:T(8,128)(2,1)S(1)} %fusion.3), kind=kLoop, calls=%fused_computation.14 | loop fusion | flops 917503 | bytes 2097157 | tf_op jit(solution)/shard_map/stack | solution.py:373
  133.3 1.3 compare_select_fusion
  134.6 2.6 %collective-permute-start.14 = (f32[1,128]{1,0:T(1,128)S(1)}, f32[1,128]{1,0:T(1,128)S(1)}, u32[]{:S(2)}, u32[]{:S(2)}) collective-permute-start(f32[1,128]{1,0:T(1,128)S(1)} %compare_select_fusion), channel_id=1, source_target_pairs={{0,1},{1,0},{2,3},{3,2},{4,5},{5,4},{6,7},{7,6},{8,9},{9,8},{10,11... | collective-permute-start | bytes 1544 | tf_op jit(solution)/shard_map/ppermute | solution.py:287
  137.2 0.8 collective-permute-done.14
  138.0 1.3 add_bitcast_fusion
  139.3 0.7 broadcast_in_dim.89
  140.0 7.9 %all-to-all-start.4 = ((f32[128,1,128]{2,1,0:T(1,128)}), f32[128,1,128]{2,1,0:T(1,128)S(1)}, u32[]{:S(2)}, u32[]{:S(2)}) async-start(f32[128,1,128]{2,1,0:T(1,128)} %broadcast_in_dim.89), calls=%async_computation.4 | async-start | bytes 131072 | tf_op jit(solution)/shard_map/all_to_all | solution.py:296
  148.5 0.6 fusion.13
  151.1 6.9 %all-to-all-done.4 = f32[128,1,128]{2,1,0:T(1,128)S(1)} async-done(((f32[128,1,128]{2,1,0:T(1,128)}), f32[128,1,128]{2,1,0:T(1,128)S(1)}, u32[]{:S(2)}, u32[]{:S(2)}) %all-to-all-start.4) | async-done | bytes 65568 | tf_op jit(solution)/shard_map/all_to_all | solution.py:296
  158.1 0.6 fusion.12
  160.0 0.7 multiply_add_fusion.1
  160.7 1.6 multiply_add_fusion
  (51 shorter events, 0.4 us)
Async XLA Ops:
  0.6 23.7 %copy-start = (s32[2,2]{1,0:T(2,128)S(1)}, s32[2,2]{1,0:T(2,128)}, u32[]{:S(2)}) copy-start(s32[2,2]{1,0:T(2,128)} %param.20) | copy-start | bytes 52
  0.7 0.7 copy-start.16
  3.2 19.6 %collective-permute-start = (s32[1,128]{1,0:T(1,128)S(1)}, s32[1,128]{1,0:T(1,128)S(1)}, u32[]{:S(2)}, u32[]{:S(2)}) collective-permute-start(s32[1,128]{1,0:T(1,128)S(1)} %fusion.8), channel_id=1, source_target_pairs={{4,0},{8,4},{12,8},{0,12},{5,1},{9,5},{13,9},{1,13},{6,2},{10,6},{... | collective-permute-start | bytes 1544 | tf_op jit(solution)/shard_map/ppermute | solution.py:336
  6.6 16.2 %collective-permute-start.1 = (s32[1,128]{1,0:T(1,128)S(1)}, s32[1,128]{1,0:T(1,128)S(1)}, u32[]{:S(2)}, u32[]{:S(2)}) collective-permute-start(s32[1,128]{1,0:T(1,128)S(1)} %fusion.8), channel_id=1, source_target_pairs={{8,0},{12,4},{0,8},{4,12},{9,1},{13,5},{1,9},{5,13},{10,2},{14,6},... | collective-permute-start | bytes 1544 | tf_op jit(solution)/shard_map/ppermute | solution.py:336
  7.1 15.7 %collective-permute-start.2 = (s32[1,128]{1,0:T(1,128)S(1)}, s32[1,128]{1,0:T(1,128)S(1)}, u32[]{:S(2)}, u32[]{:S(2)}) collective-permute-start(s32[1,128]{1,0:T(1,128)S(1)} %fusion.8), channel_id=1, source_target_pairs={{12,0},{0,4},{4,8},{8,12},{13,1},{1,5},{5,9},{9,13},{14,2},{2,6},{... | collective-permute-start | bytes 1544 | tf_op jit(solution)/shard_map/ppermute | solution.py:336
  7.7 2.4 %copy-start.13 = (f32[4,2,2,4,256]{4,3,2,1,0:T(4,128)S(1)}, f32[4,2,2,4,256]{4,3,2,1,0:T(4,128)}, u32[]{:S(2)}) copy-start(f32[4,2,2,4,256]{4,3,2,1,0:T(4,128)} %param.17) | copy-start | bytes 196612
  8.8 33.2 %collective-permute-start.4 = (bf16[2,256,256]{2,1,0:T(8,128)(2,1)S(1)}, bf16[2,256,256]{2,1,0:T(8,128)(2,1)S(1)}, u32[]{:S(2)}, u32[]{:S(2)}) collective-permute-start(bf16[2,256,256]{2,1,0:T(8,128)(2,1)S(1)} %fusion.6.own), channel_id=1, source_target_pairs={{4,0},{8,4},{12,8},{16,12},{20,16},{24,20},{28,24},{32,28},{36,32}... | collective-permute-start | bytes 786440 | tf_op jit(solution)/shard_map/ppermute | solution.py:292
  10.9 21.1 %all-to-all-start = ((bf16[8,64,256]{2,1,0:T(8,128)(2,1)}), bf16[8,64,256]{2,1,0:T(8,128)(2,1)S(1)}, u32[]{:S(2)}, u32[]{:S(2)}) async-start(bf16[8,64,256]{2,1,0:T(8,128)(2,1)} %broadcast_in_dim.82), calls=%async_computation | async-start | bytes 524288 | tf_op jit(solution)/shard_map/all_to_all | solution.py:296
  24.1 2.5 %collective-permute-start.3 = (s32[1,128]{1,0:T(1,128)S(1)}, s32[1,128]{1,0:T(1,128)S(1)}, u32[]{:S(2)}, u32[]{:S(2)}) collective-permute-start(s32[1,128]{1,0:T(1,128)S(1)} %add_add_fusion), channel_id=1, source_target_pairs={{0,16},{16,0},{1,17},{17,1},{2,18},{18,2},{3,19},{19,3},{4,20},{20... | collective-permute-start | bytes 1544 | tf_op jit(solution)/shard_map/ppermute | solution.py:287
  33.5 27.7 %all-to-all-start.1 = ((bf16[16,8,16,256]{3,2,1,0:T(8,128)(2,1)}), bf16[16,8,16,256]{3,2,1,0:T(8,128)(2,1)S(1)}, u32[]{:S(2)}, u32[]{:S(2)}) async-start(bf16[16,8,16,256]{3,2,1,0:T(8,128)(2,1)} %shard_map.174), calls=%async_computation.1 | async-start | bytes 2097152 | tf_op jit(solution)/shard_map/all_to_all | solution.py:296
  39.0 3.0 %collective-permute-start.5 = (s32[1,128]{1,0:T(1,128)S(1)}, s32[1,128]{1,0:T(1,128)S(1)}, u32[]{:S(2)}, u32[]{:S(2)}) collective-permute-start(s32[1,128]{1,0:T(1,128)S(1)} %broadcast_in_dim.83), channel_id=1, source_target_pairs={{0,32},{4,36},{8,40},{12,44},{16,48},{20,52},{24,56},{28,60},{32,6... | collective-permute-start | bytes 1544 | tf_op jit(solution)/shard_map/ppermute | solution.py:292
  42.0 19.3 %copy-start.3 = (f32[2,256,256]{2,1,0:T(8,128)S(1)}, f32[2,256,256]{2,1,0:T(8,128)}, u32[]{:S(2)}) copy-start(f32[2,256,256]{2,1,0:T(8,128)} %constant.61.clone.kern) | copy-start | bytes 1572868
  42.0 19.3 %copy-start.8 = (bf16[128,128]{1,0:T(8,128)(2,1)S(1)}, bf16[128,128]{1,0:T(8,128)(2,1)}, u32[]{:S(2)}) copy-start(bf16[128,128]{1,0:T(8,128)(2,1)} %constant.62.clone.order) | copy-start | bytes 98308
  43.9 7.9 %collective-permute-start.6 = (bf16[2,256,256]{2,1,0:T(8,128)(2,1)}, bf16[2,256,256]{2,1,0:T(8,128)(2,1)S(1)}, u32[]{:S(2)}, u32[]{:S(2)}) collective-permute-start(bf16[2,256,256]{2,1,0:T(8,128)(2,1)} %broadcast_select_fusion), channel_id=1, source_target_pairs={{32,0},{36,4},{40,8},{44,12},{48,16},{52,20},{56,24},{60,28},{64,3... | collective-permute-start | bytes 786440 | tf_op jit(solution)/shard_map/ppermute | solution.py:292
  47.2 14.1 %copy-start.1 = (bf16[512,512]{1,0:T(8,128)(2,1)S(1)}, bf16[512,512]{1,0:T(8,128)(2,1)}, u32[]{:S(2)}) copy-start(bf16[512,512]{1,0:T(8,128)(2,1)} %constant.59.clone.plus) | copy-start | bytes 1572868
  47.2 14.1 %copy-start.2 = (bf16[512,512]{1,0:T(8,128)(2,1)S(1)}, bf16[512,512]{1,0:T(8,128)(2,1)}, u32[]{:S(2)}) copy-start(bf16[512,512]{1,0:T(8,128)(2,1)} %constant.60.clone.minus) | copy-start | bytes 1572868
  51.7 0.7 copy-start.6
  52.4 0.9 copy-start.7
  54.4 6.8 %collective-permute-start.7 = (bf16[2,256,256]{2,1,0:T(8,128)(2,1)S(1)}, bf16[2,256,256]{2,1,0:T(8,128)(2,1)S(1)}, u32[]{:S(2)}, u32[]{:S(2)}) collective-permute-start(bf16[2,256,256]{2,1,0:T(8,128)(2,1)S(1)} %shard_map.175.mine), channel_id=1, source_target_pairs={{0,1},{1,0},{2,3},{3,2},{4,5},{5,4},{6,7},{7,6},{8,9},{9,8},{10,11... | collective-permute-start | bytes 786440 | tf_op jit(solution)/shard_map/ppermute | solution.py:287
  61.3 9.5 %copy-start.5 = (f32[2,256,256]{2,1,0:T(8,128)S(1)}, f32[2,256,256]{2,1,0:T(8,128)}, u32[]{:S(2)}) copy-start(f32[2,256,256]{2,1,0:T(8,128)} %pattern.1) | copy-start | bytes 1572868
  69.2 1.6 %collective-permute-start.8 = (f32[256,256]{1,0:T(8,128)S(1)}, f32[256,256]{1,0:T(8,128)S(1)}, u32[]{:S(2)}, u32[]{:S(2)}) collective-permute-start(f32[256,256]{1,0:T(8,128)S(1)} %get-tuple-element.15.power_a), channel_id=1, source_target_pairs={{0,1},{1,0},{2,3},{3,2},{4,5},{5,4},{6,7},{7,6},{8,9},{9,8},{10,11... | collective-permute-start | bytes 786440 | tf_op jit(solution)/shard_map/ppermute | solution.py:287
  79.8 2.7 %copy-start.4 = (bf16[8,2,8,16,256]{4,3,2,1,0:T(8,128)(2,1)}, bf16[8,2,8,16,256]{4,3,2,1,0:T(8,128)(2,1)S(1)}, u32[]{:S(2)}) copy-start(bf16[8,2,8,16,256]{4,3,2,1,0:T(8,128)(2,1)S(1)} %get-tuple-element.19) | copy-start | bytes 3145732
  79.8 1.8 %collective-permute-start.9 = (bf16[2,256,256]{2,1,0:T(8,128)(2,1)S(1)}, bf16[2,256,256]{2,1,0:T(8,128)(2,1)S(1)}, u32[]{:S(2)}, u32[]{:S(2)}) collective-permute-start(bf16[2,256,256]{2,1,0:T(8,128)(2,1)S(1)} %fusion.7), channel_id=1, source_target_pairs={{0,1},{1,0},{2,3},{3,2},{4,5},{5,4},{6,7},{7,6},{8,9},{9,8},{10,11... | collective-permute-start | bytes 786440 | tf_op jit(solution)/shard_map/ppermute | solution.py:287
  82.5 11.3 %collective-permute-start.10 = (bf16[2,256,256]{2,1,0:T(8,128)(2,1)S(1)}, bf16[2,256,256]{2,1,0:T(8,128)(2,1)S(1)}, u32[]{:S(2)}, u32[]{:S(2)}) collective-permute-start(bf16[2,256,256]{2,1,0:T(8,128)(2,1)S(1)} %get-tuple-element.18), channel_id=1, source_target_pairs={{0,32},{4,36},{8,40},{12,44},{16,48},{20,52},{24,56},{28,60},{32,6... | collective-permute-start | bytes 786440 | tf_op jit(solution)/shard_map/ppermute | solution.py:292
  86.8 26.9 %all-to-all-start.2 = ((bf16[16,8,16,256]{3,2,1,0:T(8,128)(2,1)}), bf16[16,8,16,256]{3,2,1,0:T(8,128)(2,1)S(1)}, u32[]{:S(2)}, u32[]{:S(2)}) async-start(bf16[16,8,16,256]{3,2,1,0:T(8,128)(2,1)} %bitcast.49), calls=%async_computation.2 | async-start | bytes 2097152 | tf_op jit(solution)/shard_map/all_to_all | solution.py:296
  93.9 16.4 %collective-permute-start.11 = (bf16[2,256,256]{2,1,0:T(8,128)(2,1)S(1)}, bf16[2,256,256]{2,1,0:T(8,128)(2,1)S(1)}, u32[]{:S(2)}, u32[]{:S(2)}) collective-permute-start(bf16[2,256,256]{2,1,0:T(8,128)(2,1)S(1)} %fusion.5), channel_id=1, source_target_pairs={{0,4},{4,8},{8,12},{12,16},{16,20},{20,24},{24,28},{28,32},{32,36}... | collective-permute-start | bytes 786440 | tf_op jit(solution)/shard_map/ppermute | solution.py:292
  110.4 13.5 %collective-permute-start.12 = (bf16[2,256,256]{2,1,0:T(8,128)(2,1)S(1)}, bf16[2,256,256]{2,1,0:T(8,128)(2,1)S(1)}, u32[]{:S(2)}, u32[]{:S(2)}) collective-permute-start(bf16[2,256,256]{2,1,0:T(8,128)(2,1)S(1)} %fusion.3), channel_id=1, source_target_pairs={{0,2},{2,0},{1,3},{3,1},{4,6},{6,4},{5,7},{7,5},{8,10},{10,8},{9,1... | collective-permute-start | bytes 786440 | tf_op jit(solution)/shard_map/ppermute | solution.py:287
  115.1 14.9 %all-to-all-start.3 = ((bf16[8,64,256]{2,1,0:T(8,128)(2,1)}), bf16[8,64,256]{2,1,0:T(8,128)(2,1)S(1)}, u32[]{:S(2)}, u32[]{:S(2)}) async-start(bf16[8,64,256]{2,1,0:T(8,128)(2,1)} %bitcast.20), calls=%async_computation.3 | async-start | bytes 524288 | tf_op jit(solution)/shard_map/all_to_all | solution.py:296
  124.0 0.7 copy-start.11
  124.7 6.7 %collective-permute-start.13 = (f32[2,256,256]{2,1,0:T(8,128)S(1)}, f32[2,256,256]{2,1,0:T(8,128)}, u32[]{:S(2)}, u32[]{:S(2)}) collective-permute-start(f32[2,256,256]{2,1,0:T(8,128)S(1)} %convert_add_fusion), channel_id=1, source_target_pairs={{0,1},{1,0},{2,3},{3,2},{4,5},{5,4},{6,7},{7,6},{8,9},{9,8},{10,11... | collective-permute-start | bytes 1572872 | tf_op jit(solution)/shard_map/ppermute | solution.py:287
  130.1 1.3 copy-start.12
  131.4 29.3 %copy-start.9 = (f32[1,2,2,256,256]{4,3,2,1,0:T(8,128)S(1)}, f32[1,2,2,256,256]{4,3,2,1,0:T(8,128)}, u32[]{:S(2)}) copy-start(f32[1,2,2,256,256]{4,3,2,1,0:T(8,128)} %param.15) | copy-start | bytes 3145732
  131.4 29.3 %copy-start.10 = (f32[1,2,2,256,256]{4,3,2,1,0:T(8,128)S(1)}, f32[1,2,2,256,256]{4,3,2,1,0:T(8,128)}, u32[]{:S(2)}) copy-start(f32[1,2,2,256,256]{4,3,2,1,0:T(8,128)} %param.16) | copy-start | bytes 3145732
  134.6 3.4 %collective-permute-start.14 = (f32[1,128]{1,0:T(1,128)S(1)}, f32[1,128]{1,0:T(1,128)S(1)}, u32[]{:S(2)}, u32[]{:S(2)}) collective-permute-start(f32[1,128]{1,0:T(1,128)S(1)} %compare_select_fusion), channel_id=1, source_target_pairs={{0,1},{1,0},{2,3},{3,2},{4,5},{5,4},{6,7},{7,6},{8,9},{9,8},{10,11... | collective-permute-start | bytes 1544 | tf_op jit(solution)/shard_map/ppermute | solution.py:287
  140.0 11.1 %copy-start.14 = (f32[64,256]{1,0:T(8,128)S(1)}, f32[64,256]{1,0:T(8,128)}, u32[]{:S(2)}) copy-start(f32[64,256]{1,0:T(8,128)} %get-tuple-element.27) | copy-start | bytes 196612
  140.0 18.0 %all-to-all-start.4 = ((f32[128,1,128]{2,1,0:T(1,128)}), f32[128,1,128]{2,1,0:T(1,128)S(1)}, u32[]{:S(2)}, u32[]{:S(2)}) async-start(f32[128,1,128]{2,1,0:T(1,128)} %broadcast_in_dim.89), calls=%async_computation.4 | async-start | bytes 131072 | tf_op jit(solution)/shard_map/all_to_all | solution.py:296
  147.8 0.7 copy-start.17
  151.1 8.9 %copy-start.15 = (f32[4,2,2,4,256]{4,3,2,1,0:T(4,128)S(1)}, f32[4,2,2,4,256]{4,3,2,1,0:T(4,128)}, u32[]{:S(2)}) copy-start(f32[4,2,2,4,256]{4,3,2,1,0:T(4,128)} %param.18) | copy-start | bytes 196612

commit v3 on v2

--- a/solution.py
+++ b/solution.py
@@ -31,8 +31,7 @@
     factor = np.float32(1.0 / math.sqrt(W))
     cosine = np.cos(angle, dtype=np.float32) * factor
     sine = -np.sin(angle, dtype=np.float32) * factor
-    plus = np.block([[cosine, sine], [-sine, cosine]])
-    minus = np.block([[cosine, -sine], [sine, cosine]])
+    dft = np.stack([cosine, sine])
     free = np.where(index < W // 2, index, index - W).astype(np.float32)
     phase = (free[:, None] * free[:, None] + free[None, :] * free[None, :]) * np.float32(math.pi / (4.0 * W))
     kernel = np.stack([np.cos(phase, dtype=np.float32), np.sin(phase, dtype=np.float32)])
@@ -41,19 +40,26 @@
     natural = i * 64 + ri * 32 + band * 4 + r
     order = np.zeros((128, 128), np.float32)
     order[natural, rows] = 1.0
-    return plus, minus, kernel, order
+    return dft, kernel, order
 
 
 def mm(a, b):
     return jnp.dot(a, b, preferred_element_type=F32)
 
 
-def transform(wave_re, wave_im, right, left):
-    across = jnp.concatenate([wave_re, wave_im], axis=1)
-    first = mm(across, right).astype(BF16)
-    down = jnp.concatenate([first[:, :W], first[:, W:]], axis=0)
+def transform(pairs, right, left):
+    across = jnp.concatenate([jnp.concatenate(p, axis=1) for p in pairs], axis=0)
+    first = mm(across.astype(BF16), right).astype(BF16)
+    spans = [slice(i * W, (i + 1) * W) for i in range(len(pairs))]
+    down = jnp.concatenate(
+        [
+            jnp.concatenate([first[at, :W] for at in spans], axis=1),
+            jnp.concatenate([first[at, W:] for at in spans], axis=1),
+        ],
+        axis=0,
+    )
     out = mm(left, down).astype(BF16)
-    return out[:W], out[W:]
+    return [(out[:W, at], out[W:, at]) for at in spans]
 
 
 def times(a_re, a_im, b_re, b_im):
@@ -64,6 +70,18 @@
 def conj_times(a_re, a_im, b_re, b_im):
     a_re, a_im, b_re, b_im = (v.astype(F32) for v in (a_re, a_im, b_re, b_im))
     return a_re * b_re + a_im * b_im, a_re * b_im - a_im * b_re
+
+
+def fill(step, dft, plus, minus):
+    @pl.when(step == 0)
+    def _():
+        for i in range(2):
+            at = slice(i * W, (i + 1) * W)
+            plus[at, at] = dft[0]
+            minus[at, at] = dft[0]
+        for ref, a, b in ((plus, dft[1], -dft[1]), (minus, -dft[1], dft[1])):
+            ref[:W, W:] = a
+            ref[W:, :W] = b
 
 
 def window_masks(row, col):
@@ -88,9 +106,10 @@
         out[d] = src[:, ids[d]]
 
 
-def forward_kernel(info, blocks, mine, other, plus, minus, kern, order, psi, inc, far, power):
+def forward_kernel(info, blocks, mine, other, dft, kern, order, psi, inc, far, power, plus, minus):
     step = pl.program_id(0)
     first = info[2] == 0
+    fill(step, dft, plus, minus)
     for z in range(NZ):
         piece = blocks[:, 0, z].reshape(128, W)
         placed = mm(order[...], piece).astype(BF16)
@@ -101,19 +120,16 @@
     fwd, inv = plus[...], minus[...]
     p0 = [jnp.where(first, mine[ri], other[ri]) for ri in range(2)]
     p1 = [jnp.where(first, other[ri], mine[ri]) for ri in range(2)]
+    pairs = range(2)
+    spec = transform([times(psi[i, 0], psi[i, 1], *p0) for i in pairs], fwd, inv)
+    moved = transform([times(*spec[i], kern[0], kern[1]) for i in pairs], inv, fwd)
+    for i in pairs:
+        inc[i, 0], inc[i, 1] = moved[i]
+    waves = transform([times(*moved[i], *p1) for i in pairs], fwd, inv)
     total = None
-    for i in range(2):
-        e_re, e_im = times(psi[i, 0], psi[i, 1], p0[0], p0[1])
-        s_re, s_im = transform(e_re.astype(BF16), e_im.astype(BF16), fwd, inv)
-        m_re, m_im = times(s_re, s_im, kern[0], kern[1])
-        w_re, w_im = transform(m_re.astype(BF16), m_im.astype(BF16), inv, fwd)
-        inc[i, 0] = w_re
-        inc[i, 1] = w_im
-        e_re, e_im = times(w_re, w_im, p1[0], p1[1])
-        f_re, f_im = transform(e_re.astype(BF16), e_im.astype(BF16), fwd, inv)
-        far[i, 0] = f_re
-        far[i, 1] = f_im
-        f_re, f_im = f_re.astype(F32), f_im.astype(F32)
+    for i in pairs:
+        far[i, 0], far[i, 1] = waves[i]
+        f_re, f_im = waves[i][0].astype(F32), waves[i][1].astype(F32)
         part = f_re * f_re + f_im * f_im
         total = part if total is None else total + part
 
@@ -127,32 +143,27 @@
 
 
 def backward_kernel(
-    info, psi, inc, far, power_a, power_b, pattern, mine, other, plus, minus, kern, order, terms, out, scratch
+    info, psi, inc, far, power_a, power_b, pattern, mine, other, dft, kern, order, terms, out, scratch, plus, minus
 ):
     step = pl.program_id(0)
     core = info[2]
     first = core == 0
+    fill(step, dft, plus, minus)
     used = info[4].astype(F32)
     fwd, inv = plus[...], minus[...]
     p0 = [jnp.where(first, mine[ri], other[ri]) for ri in range(2)]
     p1 = [jnp.where(first, other[ri], mine[ri]) for ri in range(2)]
     double = 2.0 * ((power_a[...] + power_b[...] - pattern[0]) * used)
-    sums = [None] * 4
-    for i in range(2):
-        b_re = (double * far[i, 0].astype(F32)).astype(BF16)
-        b_im = (double * far[i, 1].astype(F32)).astype(BF16)
-        b_re, b_im = transform(b_re, b_im, inv, fwd)
-        t1 = conj_times(inc[i, 0], inc[i, 1], b_re, b_im)
-        c_re, c_im = conj_times(p1[0], p1[1], b_re, b_im)
-        s_re, s_im = transform(c_re.astype(BF16), c_im.astype(BF16), fwd, inv)
-        m_re, m_im = times(s_re, s_im, kern[0], -kern[1])
-        b_re, b_im = transform(m_re.astype(BF16), m_im.astype(BF16), inv, fwd)
-        t0 = conj_times(psi[i, 0], psi[i, 1], b_re, b_im)
-        c_re, c_im = conj_times(p0[0], p0[1], b_re, b_im)
-        scratch[i, 0] = c_re.astype(BF16)
-        scratch[i, 1] = c_im.astype(BF16)
-        new = [t0[0], t0[1], t1[0], t1[1]]
-        sums = [n if s is None else s + n for s, n in zip(sums, new)]
+    pairs = range(2)
+    back = transform([[double * far[i, ri].astype(F32) for ri in range(2)] for i in pairs], inv, fwd)
+    term1 = [conj_times(inc[i, 0], inc[i, 1], *back[i]) for i in pairs]
+    spec = transform([conj_times(*p1, *back[i]) for i in pairs], fwd, inv)
+    back = transform([times(*spec[i], kern[0], -kern[1]) for i in pairs], inv, fwd)
+    term0 = [conj_times(psi[i, 0], psi[i, 1], *back[i]) for i in pairs]
+    for i in pairs:
+        for ri, value in enumerate(conj_times(*p0, *back[i])):
+            scratch[i, ri] = value.astype(BF16)
+    sums = [t[0][ri] + t[1][ri] for t in (term0, term1) for ri in range(2)]
     back = order[...].T
     for z in range(NZ):
         pieces = [
@@ -186,13 +197,41 @@
         low[ri] = jnp.where(upper, zero, value).astype(BF16)
 
 
-def scan_sum_kernel(ids, src, out, total):
-    total[...] = jnp.zeros_like(total)
-    for d in range(NYLX * NYH):
-        s = ids[d]
-        total[s] += src[d].astype(F32)
-    for s in range(SCANS):
-        out[:, s] = total[s].astype(BF16)
+def scan_sum_kernel(src, ids, out):
+    wide = NYLX * NYH * 16
+    spread_of = lax.broadcasted_iota(jnp.int32, (128, wide), 1) // 16
+    expand = (spread_of == lax.broadcasted_iota(jnp.int32, (128, wide), 0)).astype(BF16)
+    idrow = jnp.broadcast_to(ids[...], (8, 128)).astype(F32).astype(BF16)
+    scan = mm(idrow, expand)[:1]
+    target = lax.broadcasted_iota(jnp.int32, (SCANS * 16, wide), 0)
+    column = lax.broadcasted_iota(jnp.int32, (SCANS * 16, wide), 1)
+    take = (scan == (target // 16).astype(F32)) & (target % 16 == column % 16)
+    take = take.astype(BF16)
+    for z in range(NZ):
+        out[z] = mm(take, src[:, z].reshape(wide, W)).astype(BF16)
+
+
+def grad_sum_kernel(src, layer, out, packed):
+    total = src[0].astype(F32)
+    for z in range(1, NZ):
+        total += src[z].astype(F32)
+    out[...] = total
+    object_part = jnp.sum(layer[...] * layer[...])
+    probe_part = jnp.sum(total * total)
+    lane = lax.broadcasted_iota(jnp.int32, (1, 128), 1)
+    packed[...] = jnp.where(lane == 0, object_part, probe_part)
+
+
+def plain(kernel, out_shape, *arrays):
+    spec = pl.BlockSpec(memory_space=VMEM)
+    single = not isinstance(out_shape, (list, tuple))
+    return pl.pallas_call(
+        kernel,
+        in_specs=[spec] * len(arrays),
+        out_specs=spec if single else [spec] * len(out_shape),
+        out_shape=out_shape,
+        compiler_params=pltpu.CompilerParams(vmem_limit_bytes=8 << 20),
+    )(*arrays)
 
 
 def shape(dims, dtype):
@@ -230,7 +269,7 @@
 
 
 def forward(info, blocks, mine, other, consts):
-    plus, minus, kern, order = consts
+    dft, kern, order = consts
     half = (2, W, W)
     return pl.pallas_call(
         forward_kernel,
@@ -241,20 +280,20 @@
                 stepped(BLOCKS, 1),
                 fixed(half),
                 fixed(half),
-                fixed((2 * W, 2 * W)),
-                fixed((2 * W, 2 * W)),
+                fixed(half),
                 fixed(half),
                 fixed((128, 128)),
             ],
             out_specs=[stepped(PAIR, 0), stepped(PAIR, 0), stepped(PAIR, 0), fixed((W, W))],
+            scratch_shapes=[VMEM((2 * W, 2 * W), BF16), VMEM((2 * W, 2 * W), BF16)],
         ),
         out_shape=[shape((4, 2, W, W), BF16)] * 3 + [shape((W, W), F32)],
         compiler_params=pltpu.CompilerParams(dimension_semantics=("arbitrary",), vmem_limit_bytes=28 << 20),
-    )(info, blocks, mine, other, plus, minus, kern, order)
+    )(info, blocks, mine, other, dft, kern, order)
 
 
 def backward(info, psi, inc, far, power_a, power_b, patterns, mine, other, consts):
-    plus, minus, kern, order = consts
+    dft, kern, order = consts
     half = (2, W, W)
     return pl.pallas_call(
         backward_kernel,
@@ -270,17 +309,16 @@
                 pl.BlockSpec((1, W, W), lambda g, info: (info[3], 0, 0)),
                 fixed(half),
                 fixed(half),
-                fixed((2 * W, 2 * W)),
-                fixed((2 * W, 2 * W)),
+                fixed(half),
                 fixed(half),
                 fixed((128, 128)),
             ],
             out_specs=[fixed(PAIR), stepped(BLOCKS, 1)],
-            scratch_shapes=[VMEM(PAIR, BF16)],
+            scratch_shapes=[VMEM(PAIR, BF16), VMEM((2 * W, 2 * W), BF16), VMEM((2 * W, 2 * W), BF16)],
         ),
         out_shape=[shape(PAIR, F32), shape(ALL_BLOCKS, BF16)],
         compiler_params=pltpu.CompilerParams(dimension_semantics=("arbitrary",), vmem_limit_bytes=28 << 20),
-    )(info, psi, inc, far, power_a, power_b, patterns, mine, other, plus, minus, kern, order)
+    )(info, psi, inc, far, power_a, power_b, patterns, mine, other, dft, kern, order)
 
 
 def swap(value, axis):
@@ -315,10 +353,9 @@
 ):
     core = lax.axis_index("c")
     slot = lax.axis_index("yh")
-    plus, minus, kern, order = tables()
+    dft, kern, order = tables()
     consts = (
-        jnp.asarray(plus, BF16),
-        jnp.asarray(minus, BF16),
+        jnp.asarray(dft, BF16),
         jnp.asarray(kern, F32),
         jnp.asarray(order, BF16),
     )
@@ -328,9 +365,11 @@
     columns = lax.broadcasted_iota(jnp.int32, (1, 1, W), 2)
     my_left = columns >= my_offset[1]
 
-    at = lax.broadcasted_iota(jnp.int32, (1, 128), 1)
+    zeros = jnp.zeros((1, 128), jnp.int32)
     here = 2 * (NX * lax.axis_index("yl") + lax.axis_index("x"))
-    row = jnp.where(at == here, scan_of_slot[0], 0) + jnp.where(at == here + 1, scan_of_slot[1], 0)
+    row = lax.dynamic_update_slice(zeros, offsets.reshape(1, 4), (0, 64))
+    row = lax.dynamic_update_slice(row, scan_of_slot[None], (0, here))
+    base_row = row
     rows = [row]
     for d in range(1, NX):
         rows.append(lax.ppermute(row, "x", [((x + d) % NX, x) for x in range(NX)]))
@@ -339,8 +378,8 @@
     ids = row[0, : NYLX * NYH]
 
     own = lax.dynamic_index_in_dim(object_tiles[0], core, 0, keepdims=False).astype(BF16)
-    col_row = jnp.broadcast_to(my_offset[1].reshape(1, 1), (1, 128))
-    above_col = from_tile(col_row, -TGX)[:1, :1].reshape(1, 1, 1)
+    above_row = from_tile(base_row, -TGX)
+    above_col = lax.dynamic_slice(above_row, (0, 66 + slot), (1, 1)).reshape(1, 1, 1)
     above_left = columns >= above_col
     east = from_tile(own, 1)
     south = from_tile(jnp.where(above_left, own, east), TGX)
@@ -365,25 +404,20 @@
     right = jnp.where(my_left, 0.0, up) + jnp.where(above_left, 0.0, from_above)
     from_left = from_tile(right.astype(BF16), -1)
     received = exchange(probe_terms.reshape(NYLX * NYH, NZ, 16, W), PLANE)
-    by_scan = whole(scan_sum_kernel, shape((NZ, SCANS, 16, W), BF16), ids, [received], [VMEM((SCANS, NZ, 16, W), F32)])
+    by_scan = plain(scan_sum_kernel, shape((NZ, SCANS * 16, W), BF16), received, row)
     layer_part = (kept + from_left.astype(F32)).astype(BF16)
     layer_grad = layer_part.astype(F32) + swap(layer_part, "yh").astype(F32)
+    summed = exchange(by_scan, "z")
+    probe_grad, packed = plain(grad_sum_kernel, [shape((SCANS * 16, W), F32), shape((1, 128), F32)], summed, layer_grad)
+    probe_grad = probe_grad.reshape(SCANS, 2, 2, ROWS, W)
+    packed = jnp.sum(spread(packed, ("z",) + PLANE + ("c",), 4 * TILES), axis=0)
+    object_square = packed[0, 0] / float(NYH * TILES * LAYERS * 2 * W * W)
+    probe_square = packed[0, 1] / float(SCANS * MODES * 2 * W * W)
     other_grad = swap(layer_grad, "c")
     first = core == 0
     tile_grad = jnp.stack(
         [jnp.where(first, layer_grad, other_grad), jnp.where(first, other_grad, layer_grad)]
     )
-    summed = exchange(by_scan.reshape(NZ, SCANS * 16, W), "z")
-    probe_grad = jnp.sum(summed.astype(F32), axis=0).reshape(SCANS, 2, 2, ROWS, W)
-
-    lane = lax.broadcasted_iota(jnp.int32, (1, 128), 1)
-    object_part = jnp.sum(layer_grad * layer_grad)
-    probe_part = jnp.sum(probe_grad * probe_grad)
-    packed = jnp.where(lane == 0, object_part, probe_part)
-    packed = packed + swap(packed, "c")
-    packed = jnp.sum(spread(packed, ("z",) + PLANE, TILES * NYH), axis=0)
-    object_square = packed[0, 0] / float(NYH * TILES * LAYERS * 2 * W * W)
-    probe_square = packed[0, 1] / float(SCANS * MODES * 2 * W * W)
 
     object_direction = -tile_grad[None] + object_square / object_norm_before[0] * object_previous
     new_object = object_tiles + step_sizes[0].astype(F32) / 1024.0 * object_direction

time: 163 us -> 161 us (0.988)
  waiting for transfers between devices: 46.3 us -> 58.7 us
  other arithmetic: 13.5 us -> 7.1 us
  Pallas kernels: 21.8 us -> 17.7 us
  starting transfers between devices: 65.1 us -> 63 us
  local copies, waits for them, and re-layouts: 9.97 us -> 7.92 us
    ppermute x7 -> x6, waiting for transfers between devices: 10.7 us -> 22 us  [swap(): return lax.ppermute(value, axis, [(0, 1), (1, 0)])]
    all_to_all x5, waiting for transfers between devices: 17.2 us -> 28 us  [exchange(): return lax.all_to_all(value, axes, 0, 0, tiled=True)]
    ppermute x5, waiting for transfers between devices: 18.4 us -> 8.73 us  [from_tile(): return lax.ppermute(value, TILE_AXES, route)]
    pallas_call x1, Pallas kernels: 7.87 us -> 5.67 us  [forward(): pl.pallas_call(forward_kernel, grid_spec=pltpu.PrefetchScalarGridSpec(num...]
    another operation x1, other arithmetic: 1.94 us -> 0.1 us  [update(): jnp.stack([jnp.where(first, layer_grad, other_grad), jnp.where(first, oth...]
    all_to_all x5, starting transfers between devices: 35.5 us -> 33.8 us  [exchange(): return lax.all_to_all(value, axes, 0, 0, tiled=True)]
    pallas_call x1, Pallas kernels: 8.94 us -> 7.23 us  [backward(): pl.pallas_call(backward_kernel, grid_spec=pltpu.PrefetchScalarGridSpec(nu...]
    unnamed x36 -> x20, local copies, waits for them, and re-layouts: 3.02 us -> 1.36 us
  transfers between devices with their start and end apart: 20 -> 19, of which waited for: 12 -> 10; matrix products, arithmetic and copies ran while one was open for 6% -> 6% of each run, Pallas kernels for 3% -> 2%
where the time goes in v3:
time: 161 us; the launch traced here: 160 us
  starting transfers between devices  63 us (39%)
  waiting for transfers between devices  58.7 us (36%)
  Pallas kernels  17.7 us (11%)
  local copies, waits for them, and re-layouts  7.92 us (5%)
  other arithmetic  7.1 us (4%)
  between operations  5.61 us (3%)
    all_to_all x5, starting transfers between devices, exchange(): return lax.all_to_all(value, axes, 0, 0, tiled=True)  33.8 us
    all_to_all x5, waiting for transfers between devices, exchange(): return lax.all_to_all(value, axes, 0, 0, tiled=True)  28 us
    ppermute x6, waiting for transfers between devices, swap(): return lax.ppermute(value, axis, [(0, 1), (1, 0)])  22 us
    ppermute x6, starting transfers between devices, swap(): return lax.ppermute(value, axis, [(0, 1), (1, 0)])  13.2 us
    ppermute x5, starting transfers between devices, from_tile(): return lax.ppermute(value, TILE_AXES, route)  11.5 us
    ppermute x5, waiting for transfers between devices, from_tile(): return lax.ppermute(value, TILE_AXES, route)  8.73 us
    pallas_call x1, Pallas kernels, backward(): pl.pallas_call(backward_kernel, grid_spec=pltpu.PrefetchScalarGridSpec(nu...  7.23 us
    pallas_call x1, Pallas kernels, forward(): pl.pallas_call(forward_kernel, grid_spec=pltpu.PrefetchScalarGridSpec(num...  5.67 us
  transfers between devices with their start and end apart: 19, of which 10 were waited for; matrix products, arithmetic and copies ran while one was open for 6% of the time, Pallas kernels for 2%

profile of v3, /device:TPU:1, one launch (start us, length us, event | category | flops | bytes accessed | tf_op | source)
XLA Modules:
  0.0 160.1 jit_solution(5168783530087371131)
XLA Ops:
  0.6 0.7 copy-done.8
  1.3 0.1 reshape.90
  1.4 0.1 dynamic_update_slice.6
  1.5 0.7 copy-done.9
  2.1 0.1 dynamic_update_slice.7
  2.2 3.5 %collective-permute-start = (s32[1,128]{1,0:T(1,128)S(1)}, s32[1,128]{1,0:T(1,128)S(1)}, u32[]{:S(2)}, u32[]{:S(2)}) collective-permute-start(s32[1,128]{1,0:T(1,128)S(1)} %dynamic_update_slice.7), channel_id=1, source_target_pairs={{4,0},{8,4},{12,8},{0,12},{5,1},{9,5},{13,9},{1,13},{6,2},{10,6},{... | collective-permute-start | bytes 1544 | tf_op jit(solution)/shard_map/ppermute | solution.py:375
  5.7 0.5 collective-permute-start.1
  6.2 0.6 collective-permute-start.2
  6.8 0.9 convert_element_type.40
  7.7 0.7 broadcast_in_dim.59
  8.4 8.2 %all-to-all-start = ((bf16[8,64,256]{2,1,0:T(8,128)(2,1)}), bf16[8,64,256]{2,1,0:T(8,128)(2,1)S(1)}, u32[]{:S(2)}, u32[]{:S(2)}) async-start(bf16[8,64,256]{2,1,0:T(8,128)(2,1)} %broadcast_in_dim.59), calls=%async_computation | async-start | bytes 524288 | tf_op jit(solution)/shard_map/all_to_all | solution.py:334
  16.6 0.0 collective-permute-done.1
  16.6 0.0 collective-permute-done.2
  16.6 1.4 collective-permute-start.3
  18.0 1.1 fusion.6.own
  19.1 1.3 collective-permute-start.4
  20.4 5.8 %all-to-all-done = bf16[8,64,256]{2,1,0:T(8,128)(2,1)S(1)} async-done(((bf16[8,64,256]{2,1,0:T(8,128)(2,1)}), bf16[8,64,256]{2,1,0:T(8,128)(2,1)S(1)}, u32[]{:S(2)}, u32[]{:S(2)}) %all-to-all-start) | async-done | bytes 262176 | tf_op jit(solution)/shard_map/all_to_all | solution.py:334
  26.2 1.6 shard_map.165
  27.8 6.4 %all-to-all-start.1 = ((bf16[16,8,16,256]{3,2,1,0:T(8,128)(2,1)}), bf16[16,8,16,256]{3,2,1,0:T(8,128)(2,1)S(1)}, u32[]{:S(2)}, u32[]{:S(2)}) async-start(bf16[16,8,16,256]{3,2,1,0:T(8,128)(2,1)} %shard_map.165), calls=%async_computation.1 | async-start | bytes 2097152 | tf_op jit(solution)/shard_map/all_to_all | solution.py:334
  34.2 1.7 %collective-permute-start.5 = (s32[1,128]{1,0:T(1,128)S(1)}, s32[1,128]{1,0:T(1,128)S(1)}, u32[]{:S(2)}, u32[]{:S(2)}) collective-permute-start(s32[1,128]{1,0:T(1,128)S(1)} %dynamic_update_slice.7), channel_id=1, source_target_pairs={{0,32},{4,36},{8,40},{12,44},{16,48},{20,52},{24,56},{28,60},{32,6... | collective-permute-start | bytes 1544 | tf_op jit(solution)/shard_map/ppermute | solution.py:330
  35.9 0.7 collective-permute-done.5
  36.6 0.6 constant_dynamic-slice_fusion
  37.2 0.6 iota_compare_fusion
  37.8 1.1 broadcast_select_fusion
  39.0 1.3 collective-permute-start.6
  40.9 0.1 constant_dynamic-slice_fusion.1
  41.0 0.5 fusion.9
  41.5 1.4 stack.28.info
  42.9 3.4 %collective-permute-done.6.low = bf16[2,256,256]{2,1,0:T(8,128)(2,1)S(1)} collective-permute-done((bf16[2,256,256]{2,1,0:T(8,128)(2,1)S(1)}, bf16[2,256,256]{2,1,0:T(8,128)(2,1)S(1)}, u32[]{:S(2)}, u32[]{:S(2)}) %collective-permute-start.6) | collective-permute-done | bytes 262176 | tf_op jit(solution)/shard_map/ppermute | solution.py:330
  46.3 1.1 shard_map.166.mine
  47.4 5.8 %collective-permute-start.7 = (bf16[2,256,256]{2,1,0:T(8,128)(2,1)S(1)}, bf16[2,256,256]{2,1,0:T(8,128)(2,1)S(1)}, u32[]{:S(2)}, u32[]{:S(2)}) collective-permute-start(bf16[2,256,256]{2,1,0:T(8,128)(2,1)S(1)} %shard_map.166.mine), channel_id=1, source_target_pairs={{0,1},{1,0},{2,3},{3,2},{4,5},{5,4},{6,7},{7,6},{8,9},{9,8},{10,11... | collective-permute-start | bytes 786440 | tf_op jit(solution)/shard_map/ppermute | solution.py:325
  53.1 1.2 collective-permute-done.7.other
  54.3 0.0 copy-start.2
  54.3 5.7 %shard_map.167 = (bf16[4,2,256,256]{3,2,1,0:T(8,128)(2,1)S(1)}, bf16[4,2,256,256]{3,2,1,0:T(8,128)(2,1)S(1)}, bf16[4,2,256,256]{3,2,1,0:T(8,128)(2,1)S(1)}, f32[256,256]{1,0:T(8,128)S(1)}) custom-call(s32[5]{0:T(128)S(1)} %stack.28.info, bf16[8,2,8,16,256]{4,3,2,1,0:T(8,128)(2,1)S(1)} %bitcast.43, bf16[2,256,256]{2,1,0:T(8,128)(2,1)S(1)} %shard_map.166.mine, ...), custom_call_target="tpu_custom_call" | custom-call | tf_op jit(solution)/shard_map/pallas_call | solution.py:274
  60.0 0.5 collective-permute-start.8
  60.5 1.2 collective-permute-done.8.power_b
  61.6 7.2 %shard_map.168 = (f32[2,2,256,256]{3,2,1,0:T(8,128)S(1)}, bf16[8,2,8,16,256]{4,3,2,1,0:T(8,128)(2,1)}) custom-call(s32[5]{0:T(128)S(1)} %stack.28.info, bf16[4,2,256,256]{3,2,1,0:T(8,128)(2,1)S(1)} %get-tuple-element.14.psi, bf16[4,2,256,256]{3,2,1,0:T(8,128)(2,1)S(1)} %get-tuple-element.15.inc, bf16[4,2,256,256]{3,2,1,0:T(8,128)(2,1)S(1)} %get-tuple-element.16.far, ...), custom_call_target="tpu_custom_call" | custom-call | tf_op jit(solution)/shard_map/pallas_call | solution.py:298
  68.9 0.5 collective-permute-start.9
  69.4 1.1 collective-permute-done.9.theirs
  70.5 0.8 shard_map.169
  71.4 3.7 %collective-permute-start.10 = (bf16[2,256,256]{2,1,0:T(8,128)(2,1)S(1)}, bf16[2,256,256]{2,1,0:T(8,128)(2,1)S(1)}, u32[]{:S(2)}, u32[]{:S(2)}) collective-permute-start(bf16[2,256,256]{2,1,0:T(8,128)(2,1)S(1)} %get-tuple-element.20), channel_id=1, source_target_pairs={{0,32},{4,36},{8,40},{12,44},{16,48},{20,52},{24,56},{28,60},{32,6... | collective-permute-start | bytes 786440 | tf_op jit(solution)/shard_map/ppermute | solution.py:330
  75.0 0.7 iota_compare_fusion.1
  75.7 4.6 %collective-permute-done.10 = bf16[2,256,256]{2,1,0:T(8,128)(2,1)S(1)} collective-permute-done((bf16[2,256,256]{2,1,0:T(8,128)(2,1)S(1)}, bf16[2,256,256]{2,1,0:T(8,128)(2,1)S(1)}, u32[]{:S(2)}, u32[]{:S(2)}) %collective-permute-start.10) | collective-permute-done | bytes 262176 | tf_op jit(solution)/shard_map/ppermute | solution.py:330
  80.3 0.1 fusion.5
  80.4 3.6 %collective-permute-start.11 = (bf16[2,256,256]{2,1,0:T(8,128)(2,1)S(1)}, bf16[2,256,256]{2,1,0:T(8,128)(2,1)S(1)}, u32[]{:S(2)}, u32[]{:S(2)}) collective-permute-start(bf16[2,256,256]{2,1,0:T(8,128)(2,1)S(1)} %fusion.5), channel_id=1, source_target_pairs={{0,4},{4,8},{8,12},{12,16},{16,20},{20,24},{24,28},{28,32},{32,36}... | collective-permute-start | bytes 786440 | tf_op jit(solution)/shard_map/ppermute | solution.py:330
  83.9 7.2 %all-to-all-start.2 = ((bf16[16,8,16,256]{3,2,1,0:T(8,128)(2,1)}), bf16[16,8,16,256]{3,2,1,0:T(8,128)(2,1)S(1)}, u32[]{:S(2)}, u32[]{:S(2)}) async-start(bf16[16,8,16,256]{3,2,1,0:T(8,128)(2,1)} %bitcast.18), calls=%async_computation.2 | async-start | bytes 2097152 | tf_op jit(solution)/shard_map/all_to_all | solution.py:334
  91.2 0.1 fusion.3
  91.3 2.9 %collective-permute-start.12 = (bf16[2,256,256]{2,1,0:T(8,128)(2,1)S(1)}, bf16[2,256,256]{2,1,0:T(8,128)(2,1)S(1)}, u32[]{:S(2)}, u32[]{:S(2)}) collective-permute-start(bf16[2,256,256]{2,1,0:T(8,128)(2,1)S(1)} %fusion.3), channel_id=1, source_target_pairs={{0,2},{2,0},{1,3},{3,1},{4,6},{6,4},{5,7},{7,5},{8,10},{10,8},{9,1... | collective-permute-start | bytes 786440 | tf_op jit(solution)/shard_map/ppermute | solution.py:325
  94.2 18.5 %collective-permute-done.12 = bf16[2,256,256]{2,1,0:T(8,128)(2,1)S(1)} collective-permute-done((bf16[2,256,256]{2,1,0:T(8,128)(2,1)S(1)}, bf16[2,256,256]{2,1,0:T(8,128)(2,1)S(1)}, u32[]{:S(2)}, u32[]{:S(2)}) %collective-permute-start.12) | collective-permute-done | bytes 262176 | tf_op jit(solution)/shard_map/ppermute | solution.py:325
  112.8 0.1 convert_add_fusion.layer
  112.8 2.2 %collective-permute-start.13 = (f32[2,256,256]{2,1,0:T(8,128)S(1)}, f32[2,256,256]{2,1,0:T(8,128)S(1)}, u32[]{:S(2)}, u32[]{:S(2)}) collective-permute-start(f32[2,256,256]{2,1,0:T(8,128)S(1)} %convert_add_fusion.layer), channel_id=1, source_target_pairs={{0,1},{1,0},{2,3},{3,2},{4,5},{5,4},{6,7},{7,6},{8,9},{9,8},{10,11... | collective-permute-start | bytes 1572872 | tf_op jit(solution)/shard_map/ppermute | solution.py:325
  115.0 1.1 shard_map.170
  116.1 6.5 %all-to-all-start.3 = ((bf16[8,64,256]{2,1,0:T(8,128)(2,1)}), bf16[8,64,256]{2,1,0:T(8,128)(2,1)S(1)}, u32[]{:S(2)}, u32[]{:S(2)}) async-start(bf16[8,64,256]{2,1,0:T(8,128)(2,1)} %shard_map.170), calls=%async_computation.3 | async-start | bytes 524288 | tf_op jit(solution)/shard_map/all_to_all | solution.py:334
  123.3 0.6 fusion.11
  125.8 9.2 %all-to-all-done.3.src = bf16[8,64,256]{2,1,0:T(8,128)(2,1)S(1)} async-done(((bf16[8,64,256]{2,1,0:T(8,128)(2,1)}), bf16[8,64,256]{2,1,0:T(8,128)(2,1)S(1)}, u32[]{:S(2)}, u32[]{:S(2)}) %all-to-all-start.3) | async-done | bytes 262176 | tf_op jit(solution)/shard_map/all_to_all | solution.py:334
  135.0 0.3 shard_map.171
  135.2 0.7 broadcast_in_dim.63
  136.0 5.5 %all-to-all-start.4 = ((f32[256,1,128]{2,1,0:T(1,128)}), f32[256,1,128]{2,1,0:T(1,128)S(1)}, u32[]{:S(2)}, u32[]{:S(2)}) async-start(f32[256,1,128]{2,1,0:T(1,128)} %broadcast_in_dim.63), calls=%async_computation.4 | async-start | bytes 262144 | tf_op jit(solution)/shard_map/all_to_all | solution.py:334
  141.5 0.0 copy-start.4
  141.5 0.1 select_bitcast_fusion.1
  141.6 13.0 %all-to-all-done.4 = f32[256,1,128]{2,1,0:T(1,128)S(1)} async-done(((f32[256,1,128]{2,1,0:T(1,128)}), f32[256,1,128]{2,1,0:T(1,128)S(1)}, u32[]{:S(2)}, u32[]{:S(2)}) %all-to-all-start.4) | async-done | bytes 131104 | tf_op jit(solution)/shard_map/all_to_all | solution.py:334
  154.7 0.6 fusion.10
  156.7 0.7 multiply_add_fusion.1
  157.4 2.7 %multiply_add_fusion = (f32[1,2,2,256,256]{4,3,2,1,0:T(8,128)}, f32[1,2,2,256,256]{4,3,2,1,0:T(8,128)}) fusion(f32[1,2,2,256,256]{4,3,2,1,0:T(8,128)S(1)} %copy-done.4, f32[]{:T(128)} %bitcast, f32[1,2,2,256,256]{4,3,2,1,0:T(8,128)} %param.15, f32[]{:T(128)S(6)} %div.30, f32[1,1,2,256,256]{4,3,2,1,0:T(8,128)S(1)} %get-tuple-element.29, ...), kind=kLoop, calls=%fused_computation.2 | loop fusion | flops 1572864 | bytes 5242888 | tf_op jit(solution)/shard_map/add | solution.py:423
  (32 shorter events, 0.2 us)
Async XLA Ops:
  0.6 0.7 copy-start.8
  1.5 0.7 copy-start.9
  2.2 14.4 %collective-permute-start = (s32[1,128]{1,0:T(1,128)S(1)}, s32[1,128]{1,0:T(1,128)S(1)}, u32[]{:S(2)}, u32[]{:S(2)}) collective-permute-start(s32[1,128]{1,0:T(1,128)S(1)} %dynamic_update_slice.7), channel_id=1, source_target_pairs={{4,0},{8,4},{12,8},{0,12},{5,1},{9,5},{13,9},{1,13},{6,2},{10,6},{... | collective-permute-start | bytes 1544 | tf_op jit(solution)/shard_map/ppermute | solution.py:375
  5.7 10.9 %collective-permute-start.1 = (s32[1,128]{1,0:T(1,128)S(1)}, s32[1,128]{1,0:T(1,128)S(1)}, u32[]{:S(2)}, u32[]{:S(2)}) collective-permute-start(s32[1,128]{1,0:T(1,128)S(1)} %dynamic_update_slice.7), channel_id=1, source_target_pairs={{8,0},{12,4},{0,8},{4,12},{9,1},{13,5},{1,9},{5,13},{10,2},{14,6},... | collective-permute-start | bytes 1544 | tf_op jit(solution)/shard_map/ppermute | solution.py:375
  6.2 10.4 %collective-permute-start.2 = (s32[1,128]{1,0:T(1,128)S(1)}, s32[1,128]{1,0:T(1,128)S(1)}, u32[]{:S(2)}, u32[]{:S(2)}) collective-permute-start(s32[1,128]{1,0:T(1,128)S(1)} %dynamic_update_slice.7), channel_id=1, source_target_pairs={{12,0},{0,4},{4,8},{8,12},{13,1},{1,5},{5,9},{9,13},{14,2},{2,6},{... | collective-permute-start | bytes 1544 | tf_op jit(solution)/shard_map/ppermute | solution.py:375
  8.4 17.8 %all-to-all-start = ((bf16[8,64,256]{2,1,0:T(8,128)(2,1)}), bf16[8,64,256]{2,1,0:T(8,128)(2,1)S(1)}, u32[]{:S(2)}, u32[]{:S(2)}) async-start(bf16[8,64,256]{2,1,0:T(8,128)(2,1)} %broadcast_in_dim.59), calls=%async_computation | async-start | bytes 524288 | tf_op jit(solution)/shard_map/all_to_all | solution.py:334
  16.6 3.8 %collective-permute-start.3 = (s32[1,128]{1,0:T(1,128)S(1)}, s32[1,128]{1,0:T(1,128)S(1)}, u32[]{:S(2)}, u32[]{:S(2)}) collective-permute-start(s32[1,128]{1,0:T(1,128)S(1)} %add_add_fusion), channel_id=1, source_target_pairs={{0,16},{16,0},{1,17},{17,1},{2,18},{18,2},{3,19},{19,3},{4,20},{20... | collective-permute-start | bytes 1544 | tf_op jit(solution)/shard_map/ppermute | solution.py:325
  19.1 18.8 %collective-permute-start.4 = (bf16[2,256,256]{2,1,0:T(8,128)(2,1)S(1)}, bf16[2,256,256]{2,1,0:T(8,128)(2,1)S(1)}, u32[]{:S(2)}, u32[]{:S(2)}) collective-permute-start(bf16[2,256,256]{2,1,0:T(8,128)(2,1)S(1)} %fusion.6.own), channel_id=1, source_target_pairs={{4,0},{8,4},{12,8},{16,12},{20,16},{24,20},{28,24},{32,28},{36,32}... | collective-permute-start | bytes 786440 | tf_op jit(solution)/shard_map/ppermute | solution.py:330
  27.8 26.5 %all-to-all-start.1 = ((bf16[16,8,16,256]{3,2,1,0:T(8,128)(2,1)}), bf16[16,8,16,256]{3,2,1,0:T(8,128)(2,1)S(1)}, u32[]{:S(2)}, u32[]{:S(2)}) async-start(bf16[16,8,16,256]{3,2,1,0:T(8,128)(2,1)} %shard_map.165), calls=%async_computation.1 | async-start | bytes 2097152 | tf_op jit(solution)/shard_map/all_to_all | solution.py:334
  34.2 2.4 %collective-permute-start.5 = (s32[1,128]{1,0:T(1,128)S(1)}, s32[1,128]{1,0:T(1,128)S(1)}, u32[]{:S(2)}, u32[]{:S(2)}) collective-permute-start(s32[1,128]{1,0:T(1,128)S(1)} %dynamic_update_slice.7), channel_id=1, source_target_pairs={{0,32},{4,36},{8,40},{12,44},{16,48},{20,52},{24,56},{28,60},{32,6... | collective-permute-start | bytes 1544 | tf_op jit(solution)/shard_map/ppermute | solution.py:330
  39.0 7.4 %collective-permute-start.6 = (bf16[2,256,256]{2,1,0:T(8,128)(2,1)S(1)}, bf16[2,256,256]{2,1,0:T(8,128)(2,1)S(1)}, u32[]{:S(2)}, u32[]{:S(2)}) collective-permute-start(bf16[2,256,256]{2,1,0:T(8,128)(2,1)S(1)} %broadcast_select_fusion), channel_id=1, source_target_pairs={{32,0},{36,4},{40,8},{44,12},{48,16},{52,20},{56,24},{60,28},{64,3... | collective-permute-start | bytes 786440 | tf_op jit(solution)/shard_map/ppermute | solution.py:330
  42.9 11.4 %copy-start = (f32[2,256,256]{2,1,0:T(8,128)S(1)}, f32[2,256,256]{2,1,0:T(8,128)}, u32[]{:S(2)}) copy-start(f32[2,256,256]{2,1,0:T(8,128)} %constant.63.clone.kern) | copy-start | bytes 1572868
  42.9 11.4 %copy-start.1 = (bf16[2,256,256]{2,1,0:T(8,128)(2,1)S(1)}, bf16[2,256,256]{2,1,0:T(8,128)(2,1)}, u32[]{:S(2)}) copy-start(bf16[2,256,256]{2,1,0:T(8,128)(2,1)} %constant.62.clone.dft) | copy-start | bytes 786436
  42.9 11.4 %copy-start.3 = (bf16[128,128]{1,0:T(8,128)(2,1)S(1)}, bf16[128,128]{1,0:T(8,128)(2,1)}, u32[]{:S(2)}) copy-start(bf16[128,128]{1,0:T(8,128)(2,1)} %constant.64.clone.order) | copy-start | bytes 98308
  47.4 6.9 %collective-permute-start.7 = (bf16[2,256,256]{2,1,0:T(8,128)(2,1)S(1)}, bf16[2,256,256]{2,1,0:T(8,128)(2,1)S(1)}, u32[]{:S(2)}, u32[]{:S(2)}) collective-permute-start(bf16[2,256,256]{2,1,0:T(8,128)(2,1)S(1)} %shard_map.166.mine), channel_id=1, source_target_pairs={{0,1},{1,0},{2,3},{3,2},{4,5},{5,4},{6,7},{7,6},{8,9},{9,8},{10,11... | collective-permute-start | bytes 786440 | tf_op jit(solution)/shard_map/ppermute | solution.py:325
  54.3 7.3 %copy-start.2 = (f32[2,256,256]{2,1,0:T(8,128)S(1)}, f32[2,256,256]{2,1,0:T(8,128)}, u32[]{:S(2)}) copy-start(f32[2,256,256]{2,1,0:T(8,128)} %pattern.1) | copy-start | bytes 1572868
  60.0 1.6 %collective-permute-start.8 = (f32[256,256]{1,0:T(8,128)S(1)}, f32[256,256]{1,0:T(8,128)S(1)}, u32[]{:S(2)}, u32[]{:S(2)}) collective-permute-start(f32[256,256]{1,0:T(8,128)S(1)} %get-tuple-element.17.power_a), channel_id=1, source_target_pairs={{0,1},{1,0},{2,3},{3,2},{4,5},{5,4},{6,7},{7,6},{8,9},{9,8},{10,11... | collective-permute-start | bytes 786440 | tf_op jit(solution)/shard_map/ppermute | solution.py:325
  68.9 1.6 %collective-permute-start.9 = (bf16[2,256,256]{2,1,0:T(8,128)(2,1)S(1)}, bf16[2,256,256]{2,1,0:T(8,128)(2,1)S(1)}, u32[]{:S(2)}, u32[]{:S(2)}) collective-permute-start(bf16[2,256,256]{2,1,0:T(8,128)(2,1)S(1)} %fusion.7), channel_id=1, source_target_pairs={{0,1},{1,0},{2,3},{3,2},{4,5},{5,4},{6,7},{7,6},{8,9},{9,8},{10,11... | collective-permute-start | bytes 786440 | tf_op jit(solution)/shard_map/ppermute | solution.py:325
  71.4 8.9 %collective-permute-start.10 = (bf16[2,256,256]{2,1,0:T(8,128)(2,1)S(1)}, bf16[2,256,256]{2,1,0:T(8,128)(2,1)S(1)}, u32[]{:S(2)}, u32[]{:S(2)}) collective-permute-start(bf16[2,256,256]{2,1,0:T(8,128)(2,1)S(1)} %get-tuple-element.20), channel_id=1, source_target_pairs={{0,32},{4,36},{8,40},{12,44},{16,48},{20,52},{24,56},{28,60},{32,6... | collective-permute-start | bytes 786440 | tf_op jit(solution)/shard_map/ppermute | solution.py:330
  80.4 10.8 %collective-permute-start.11 = (bf16[2,256,256]{2,1,0:T(8,128)(2,1)S(1)}, bf16[2,256,256]{2,1,0:T(8,128)(2,1)S(1)}, u32[]{:S(2)}, u32[]{:S(2)}) collective-permute-start(bf16[2,256,256]{2,1,0:T(8,128)(2,1)S(1)} %fusion.5), channel_id=1, source_target_pairs={{0,4},{4,8},{8,12},{12,16},{16,20},{20,24},{24,28},{28,32},{32,36}... | collective-permute-start | bytes 786440 | tf_op jit(solution)/shard_map/ppermute | solution.py:330
  83.9 31.1 %all-to-all-start.2 = ((bf16[16,8,16,256]{3,2,1,0:T(8,128)(2,1)}), bf16[16,8,16,256]{3,2,1,0:T(8,128)(2,1)S(1)}, u32[]{:S(2)}, u32[]{:S(2)}) async-start(bf16[16,8,16,256]{3,2,1,0:T(8,128)(2,1)} %bitcast.18), calls=%async_computation.2 | async-start | bytes 2097152 | tf_op jit(solution)/shard_map/all_to_all | solution.py:334
  91.3 21.5 %collective-permute-start.12 = (bf16[2,256,256]{2,1,0:T(8,128)(2,1)S(1)}, bf16[2,256,256]{2,1,0:T(8,128)(2,1)S(1)}, u32[]{:S(2)}, u32[]{:S(2)}) collective-permute-start(bf16[2,256,256]{2,1,0:T(8,128)(2,1)S(1)} %fusion.3), channel_id=1, source_target_pairs={{0,2},{2,0},{1,3},{3,1},{4,6},{6,4},{5,7},{7,5},{8,10},{10,8},{9,1... | collective-permute-start | bytes 786440 | tf_op jit(solution)/shard_map/ppermute | solution.py:325
  112.8 28.7 %collective-permute-start.13 = (f32[2,256,256]{2,1,0:T(8,128)S(1)}, f32[2,256,256]{2,1,0:T(8,128)S(1)}, u32[]{:S(2)}, u32[]{:S(2)}) collective-permute-start(f32[2,256,256]{2,1,0:T(8,128)S(1)} %convert_add_fusion.layer), channel_id=1, source_target_pairs={{0,1},{1,0},{2,3},{3,2},{4,5},{5,4},{6,7},{7,6},{8,9},{9,8},{10,11... | collective-permute-start | bytes 1572872 | tf_op jit(solution)/shard_map/ppermute | solution.py:325
  116.1 18.9 %all-to-all-start.3 = ((bf16[8,64,256]{2,1,0:T(8,128)(2,1)}), bf16[8,64,256]{2,1,0:T(8,128)(2,1)S(1)}, u32[]{:S(2)}, u32[]{:S(2)}) async-start(bf16[8,64,256]{2,1,0:T(8,128)(2,1)} %shard_map.170), calls=%async_computation.3 | async-start | bytes 524288 | tf_op jit(solution)/shard_map/all_to_all | solution.py:334
  122.6 0.7 copy-start.7
  136.0 18.7 %all-to-all-start.4 = ((f32[256,1,128]{2,1,0:T(1,128)}), f32[256,1,128]{2,1,0:T(1,128)S(1)}, u32[]{:S(2)}, u32[]{:S(2)}) async-start(f32[256,1,128]{2,1,0:T(1,128)} %broadcast_in_dim.63), calls=%async_computation.4 | async-start | bytes 262144 | tf_op jit(solution)/shard_map/all_to_all | solution.py:334
  141.5 15.9 %copy-start.4 = (f32[1,2,2,256,256]{4,3,2,1,0:T(8,128)S(1)}, f32[1,2,2,256,256]{4,3,2,1,0:T(8,128)}, u32[]{:S(2)}) copy-start(f32[1,2,2,256,256]{4,3,2,1,0:T(8,128)} %param.14) | copy-start | bytes 3145732
  154.7 2.0 %copy-start.5 = (f32[4,2,2,4,256]{4,3,2,1,0:T(4,128)S(1)}, f32[4,2,2,4,256]{4,3,2,1,0:T(4,128)}, u32[]{:S(2)}) copy-start(f32[4,2,2,4,256]{4,3,2,1,0:T(4,128)} %param.16) | copy-start | bytes 196612
  154.7 2.0 %copy-start.6 = (f32[4,2,2,4,256]{4,3,2,1,0:T(4,128)S(1)}, f32[4,2,2,4,256]{4,3,2,1,0:T(4,128)}, u32[]{:S(2)}) copy-start(f32[4,2,2,4,256]{4,3,2,1,0:T(4,128)} %param.17) | copy-start | bytes 196612

commit v4 on v3

--- a/solution.py
+++ b/solution.py
@@ -35,12 +35,7 @@
     free = np.where(index < W // 2, index, index - W).astype(np.float32)
     phase = (free[:, None] * free[:, None] + free[None, :] * free[None, :]) * np.float32(math.pi / (4.0 * W))
     kernel = np.stack([np.cos(phase, dtype=np.float32), np.sin(phase, dtype=np.float32)])
-    rows = np.arange(128)
-    band, i, ri, r = rows // 16, rows // 8 % 2, rows // 4 % 2, rows % 4
-    natural = i * 64 + ri * 32 + band * 4 + r
-    order = np.zeros((128, 128), np.float32)
-    order[natural, rows] = 1.0
-    return dft, kernel, order
+    return dft, kernel
 
 
 def mm(a, b):
@@ -72,6 +67,13 @@
     return a_re * b_re + a_im * b_im, a_re * b_im - a_im * b_re
 
 
+def placing(axis):
+    natural = lax.broadcasted_iota(jnp.int32, (128, 128), axis)
+    rows = lax.broadcasted_iota(jnp.int32, (128, 128), 1 - axis)
+    band, i, ri, r = rows // 16, rows // 8 % 2, rows // 4 % 2, rows % 4
+    return (natural == i * 64 + ri * 32 + band * 4 + r).astype(F32).astype(BF16)
+
+
 def fill(step, dft, plus, minus):
     @pl.when(step == 0)
     def _():
@@ -90,12 +92,10 @@
     return rows >= row, cols >= col
 
 
-def patch_kernel(info, own, east, low, out):
+def patch_kernel(info, mixed, out):
     row, col = info[0], info[1]
-    upper, left = window_masks(row, col)
     for ri in range(2):
-        top = jnp.where(left, own[ri].astype(F32), east[ri].astype(F32))
-        value = jnp.where(upper, top, low[ri].astype(F32))
+        value = mixed[ri].astype(F32)
         value = pltpu.roll(value, (W - row) % W, 0)
         value = pltpu.roll(value, (W - col) % W, 1)
         out[ri] = value.astype(BF16)
@@ -106,13 +106,14 @@
         out[d] = src[:, ids[d]]
 
 
-def forward_kernel(info, blocks, mine, other, dft, kern, order, psi, inc, far, power, plus, minus):
+def forward_kernel(info, blocks, mine, other, dft, kern, psi, inc, far, power, plus, minus):
     step = pl.program_id(0)
     first = info[2] == 0
     fill(step, dft, plus, minus)
+    order = placing(0)
     for z in range(NZ):
         piece = blocks[:, 0, z].reshape(128, W)
-        placed = mm(order[...], piece).astype(BF16)
+        placed = mm(order, piece).astype(BF16)
         for i in range(2):
             for ri in range(2):
                 at = i * 64 + ri * 32
@@ -143,7 +144,7 @@
 
 
 def backward_kernel(
-    info, psi, inc, far, power_a, power_b, pattern, mine, other, dft, kern, order, terms, out, scratch, plus, minus
+    info, psi, inc, far, power_a, power_b, pattern, mine, other, dft, kern, terms, out, scratch, plus, minus
 ):
     step = pl.program_id(0)
     core = info[2]
@@ -164,7 +165,7 @@
         for ri, value in enumerate(conj_times(*p0, *back[i])):
             scratch[i, ri] = value.astype(BF16)
     sums = [t[0][ri] + t[1][ri] for t in (term0, term1) for ri in range(2)]
-    back = order[...].T
+    back = placing(1)
     for z in range(NZ):
         pieces = [
             scratch[i, ri, z * BAND : (z + 1) * BAND] for i in range(2) for ri in range(2)
@@ -185,16 +186,19 @@
             terms[slot, 1] += sums[2 * layer + 1]
 
 
-def place_kernel(info, mine, theirs, up, low):
-    row, col = info[0], info[1]
-    upper, _ = window_masks(row, col)
+def place_kernel(info, own, other, kept, right, low):
     zero = jnp.zeros((W, W), F32)
-    for ri in range(2):
-        value = mine[ri] + theirs[ri].astype(F32)
-        value = pltpu.roll(value, row, 0)
+    parts = [zero] * 4
+    for window, at in ((own, 0), (other, 5)):
+        row, col = info[at], info[at + 1]
+        upper, left = window_masks(row, col)
+        value = pltpu.roll(window[...].astype(F32), row, 0)
         value = pltpu.roll(value, col, 1)
-        up[ri] = jnp.where(upper, value, zero)
-        low[ri] = jnp.where(upper, zero, value).astype(BF16)
+        top, down = jnp.where(upper, value, zero), jnp.where(upper, zero, value)
+        pieces = [p for v in (top, down) for p in (jnp.where(left, v, zero), jnp.where(left, zero, v))]
+        parts = [p + q for p, q in zip(parts, pieces)]
+    kept[...], right[...] = parts[0], parts[1]
+    low[0], low[1] = parts[2].astype(BF16), parts[3].astype(BF16)
 
 
 def scan_sum_kernel(src, ids, out):
@@ -220,6 +224,58 @@
     probe_part = jnp.sum(total * total)
     lane = lax.broadcasted_iota(jnp.int32, (1, 128), 1)
     packed[...] = jnp.where(lane == 0, object_part, probe_part)
+
+
+def finish_kernel(
+    info, steps, object_norm, probe_norm, packed, layer, other, tiles, before, grad, probe, probe_before, *outs
+):
+    new_tiles, direction, new_probe, probe_direction, held, sems = outs
+    totals = jnp.sum(packed[...].reshape(4 * TILES, 128), axis=0, keepdims=True)
+    lane = lax.broadcasted_iota(jnp.int32, (1, 128), 1)
+
+    def square(at, count):
+        return jnp.sum(jnp.where(lane == at, totals, 0.0), axis=1, keepdims=True) / float(count)
+
+    ratio = square(0, TILES * LAYERS * 2 * W * W) / object_norm[0]
+    rate = steps[0].astype(F32) / 1024.0
+    copies = []
+    for l in range(LAYERS):
+        for ri in range(2):
+            gradient = jnp.where(info[2] == l, layer[ri], other[ri])
+            turned = ratio * before[0, l, ri] - gradient
+            held[1, l, ri] = turned
+            held[0, l, ri] = tiles[0, l, ri] + rate * turned
+            for k, target in enumerate((new_tiles, direction)):
+                copies.append(pltpu.make_async_copy(held.at[k, l, ri], target.at[0, l, ri], sems.at[k, l, ri]))
+                copies[-1].start()
+    ratio = square(1, SCANS * MODES * 2 * W * W) / probe_norm[0]
+    probe_rate = steps[1].astype(F32) / 16384.0
+    for s in range(SCANS):
+        for i in range(2):
+            for ri in range(2):
+                at = ROWS * (4 * s + 2 * i + ri)
+                value = ratio * probe_before[s, i, ri] - grad[at : at + ROWS]
+                probe_direction[s, i, ri] = value
+                new_probe[s, i, ri] = probe[s, i, ri] + probe_rate * value
+    for copy in copies:
+        copy.wait()
+
+
+def finish(scalars, arrays):
+    spec = pl.BlockSpec(memory_space=VMEM)
+    away = pl.BlockSpec(memory_space=pl.ANY)
+    return pl.pallas_call(
+        finish_kernel,
+        grid_spec=pltpu.PrefetchScalarGridSpec(
+            num_scalar_prefetch=4,
+            grid=(),
+            in_specs=[spec] * len(arrays),
+            out_specs=[away, away, spec, spec],
+            scratch_shapes=[VMEM((2, LAYERS, 2, W, W), F32), pltpu.SemaphoreType.DMA((2, LAYERS, 2))],
+        ),
+        out_shape=[shape((1, LAYERS, 2, W, W), F32)] * 2 + [shape((SCANS, 2, 2, ROWS, W), F32)] * 2,
+        compiler_params=pltpu.CompilerParams(vmem_limit_bytes=16 << 20),
+    )(*scalars, *arrays)
 
 
 def plain(kernel, out_shape, *arrays):
@@ -269,7 +325,7 @@
 
 
 def forward(info, blocks, mine, other, consts):
-    dft, kern, order = consts
+    dft, kern = consts
     half = (2, W, W)
     return pl.pallas_call(
         forward_kernel,
@@ -282,18 +338,17 @@
                 fixed(half),
                 fixed(half),
                 fixed(half),
-                fixed((128, 128)),
             ],
             out_specs=[stepped(PAIR, 0), stepped(PAIR, 0), stepped(PAIR, 0), fixed((W, W))],
             scratch_shapes=[VMEM((2 * W, 2 * W), BF16), VMEM((2 * W, 2 * W), BF16)],
         ),
         out_shape=[shape((4, 2, W, W), BF16)] * 3 + [shape((W, W), F32)],
         compiler_params=pltpu.CompilerParams(dimension_semantics=("arbitrary",), vmem_limit_bytes=28 << 20),
-    )(info, blocks, mine, other, dft, kern, order)
+    )(info, blocks, mine, other, dft, kern)
 
 
 def backward(info, psi, inc, far, power_a, power_b, patterns, mine, other, consts):
-    dft, kern, order = consts
+    dft, kern = consts
     half = (2, W, W)
     return pl.pallas_call(
         backward_kernel,
@@ -311,14 +366,13 @@
                 fixed(half),
                 fixed(half),
                 fixed(half),
-                fixed((128, 128)),
             ],
             out_specs=[fixed(PAIR), stepped(BLOCKS, 1)],
             scratch_shapes=[VMEM(PAIR, BF16), VMEM((2 * W, 2 * W), BF16), VMEM((2 * W, 2 * W), BF16)],
         ),
         out_shape=[shape(PAIR, F32), shape(ALL_BLOCKS, BF16)],
         compiler_params=pltpu.CompilerParams(dimension_semantics=("arbitrary",), vmem_limit_bytes=28 << 20),
-    )(info, psi, inc, far, power_a, power_b, patterns, mine, other, dft, kern, order)
+    )(info, psi, inc, far, power_a, power_b, patterns, mine, other, dft, kern)
 
 
 def swap(value, axis):
@@ -353,23 +407,24 @@
 ):
     core = lax.axis_index("c")
     slot = lax.axis_index("yh")
-    dft, kern, order = tables()
+    dft, kern = tables()
     consts = (
         jnp.asarray(dft, BF16),
         jnp.asarray(kern, F32),
-        jnp.asarray(order, BF16),
     )
     my_offset = lax.dynamic_index_in_dim(offsets, slot, 1, keepdims=False)
     used = (slot < tile_load[0]).astype(jnp.int32)
-    info = jnp.stack([my_offset[0], my_offset[1], core.astype(jnp.int32), slot.astype(jnp.int32), used])
+    twin_offset = lax.dynamic_index_in_dim(offsets, 1 - slot, 1, keepdims=False)
+    info = jnp.concatenate(
+        [my_offset, jnp.stack([core.astype(jnp.int32), slot.astype(jnp.int32), used]), twin_offset]
+    )
     columns = lax.broadcasted_iota(jnp.int32, (1, 1, W), 2)
-    my_left = columns >= my_offset[1]
+    lines = lax.broadcasted_iota(jnp.int32, (1, W, 1), 1)
+    my_upper, my_left = lines >= my_offset[0], columns >= my_offset[1]
 
     zeros = jnp.zeros((1, 128), jnp.int32)
     here = 2 * (NX * lax.axis_index("yl") + lax.axis_index("x"))
-    row = lax.dynamic_update_slice(zeros, offsets.reshape(1, 4), (0, 64))
-    row = lax.dynamic_update_slice(row, scan_of_slot[None], (0, here))
-    base_row = row
+    row = lax.dynamic_update_slice(zeros, scan_of_slot[None], (0, here))
     rows = [row]
     for d in range(1, NX):
         rows.append(lax.ppermute(row, "x", [((x + d) % NX, x) for x in range(NX)]))
@@ -378,8 +433,8 @@
     ids = row[0, : NYLX * NYH]
 
     own = lax.dynamic_index_in_dim(object_tiles[0], core, 0, keepdims=False).astype(BF16)
-    above_row = from_tile(base_row, -TGX)
-    above_col = lax.dynamic_slice(above_row, (0, 66 + slot), (1, 1)).reshape(1, 1, 1)
+    above_row = from_tile(jnp.pad(offsets.reshape(1, 4), ((0, 0), (0, 124))), -TGX)
+    above_col = lax.dynamic_slice(above_row, (0, 2 + slot), (1, 1)).reshape(1, 1, 1)
     above_left = columns >= above_col
     east = from_tile(own, 1)
     south = from_tile(jnp.where(above_left, own, east), TGX)
@@ -389,41 +444,41 @@
     picked = whole(pick_kernel, shape((NYLX * NYH, NZ, 16, W), BF16), ids, [banded])
     blocks = exchange(picked, PLANE).reshape(ALL_BLOCKS)
 
-    mine = whole(patch_kernel, shape((2, W, W), BF16), info, [own, east, south])
+    mixed = jnp.where(my_upper, jnp.where(my_left, own, east), south)
+    mine = whole(patch_kernel, shape((2, W, W), BF16), info, [mixed])
     other = swap(mine, "c")
 
     psi, inc, far, power = forward(info, blocks, mine, other, consts)
     power_other = swap(power, "c")
     terms, probe_terms = backward(info, psi, inc, far, power, power_other, patterns, mine, other, consts)
 
-    theirs = swap(terms[1].astype(BF16), "c")
-    half = (2, W, W)
-    up, low = whole(place_kernel, [shape(half, F32), shape(half, BF16)], info, [terms[0], theirs])
+    summed = terms[0] + swap(terms[1].astype(BF16), "c").astype(F32)
+    real = slot == 0
+    window = jnp.where(real, summed[0], summed[1])
+    twin = swap(jnp.where(real, summed[1], summed[0]).astype(BF16), "yh")
+    field = shape((W, W), F32)
+    kept, right, low = whole(
+        place_kernel, [field, field, shape((2, W, W), BF16)], info, [window, twin]
+    )
     from_above = from_tile(low, -TGX).astype(F32)
-    kept = jnp.where(my_left, up, 0.0) + jnp.where(above_left, from_above, 0.0)
-    right = jnp.where(my_left, 0.0, up) + jnp.where(above_left, 0.0, from_above)
-    from_left = from_tile(right.astype(BF16), -1)
+    kept = kept + from_above[0]
+    right = right + from_above[1]
     received = exchange(probe_terms.reshape(NYLX * NYH, NZ, 16, W), PLANE)
     by_scan = plain(scan_sum_kernel, shape((NZ, SCANS * 16, W), BF16), received, row)
-    layer_part = (kept + from_left.astype(F32)).astype(BF16)
-    layer_grad = layer_part.astype(F32) + swap(layer_part, "yh").astype(F32)
+    part_grad = kept + from_tile(right.astype(BF16), -1).astype(F32)
     summed = exchange(by_scan, "z")
-    probe_grad, packed = plain(grad_sum_kernel, [shape((SCANS * 16, W), F32), shape((1, 128), F32)], summed, layer_grad)
-    probe_grad = probe_grad.reshape(SCANS, 2, 2, ROWS, W)
-    packed = jnp.sum(spread(packed, ("z",) + PLANE + ("c",), 4 * TILES), axis=0)
-    object_square = packed[0, 0] / float(NYH * TILES * LAYERS * 2 * W * W)
-    probe_square = packed[0, 1] / float(SCANS * MODES * 2 * W * W)
+    probe_grad, packed = plain(grad_sum_kernel, [shape((SCANS * 16, W), F32), shape((1, 128), F32)], summed, part_grad)
+    packed = spread(packed, ("z",) + PLANE + ("c",), 4 * TILES)
+    twin_part = swap(part_grad, "yh")
+    layer_grad = jnp.stack(
+        [jnp.where(real, part_grad, twin_part), jnp.where(real, twin_part, part_grad)]
+    )
     other_grad = swap(layer_grad, "c")
-    first = core == 0
-    tile_grad = jnp.stack(
-        [jnp.where(first, layer_grad, other_grad), jnp.where(first, other_grad, layer_grad)]
-    )
-
-    object_direction = -tile_grad[None] + object_square / object_norm_before[0] * object_previous
-    new_object = object_tiles + step_sizes[0].astype(F32) / 1024.0 * object_direction
-    probe_direction = -probe_grad + probe_square / probe_norm_before[0] * probe_previous
-    new_probe = probe + step_sizes[1].astype(F32) / 16384.0 * probe_direction
-    return (new_object, object_direction, new_probe, probe_direction)
+
+    return finish(
+        (info, step_sizes, object_norm_before, probe_norm_before),
+        (packed, layer_grad, other_grad, object_tiles, object_previous, probe_grad, probe, probe_previous),
+    )
 
 
 def solution(mesh):

time: 161 us -> 149 us (0.925)
  waiting for transfers between devices: 58.7 us -> 50.9 us
  other arithmetic: 7.1 us -> 2.49 us
  Pallas kernels: 17.7 us -> 21.4 us
  local copies, waits for them, and re-layouts: 7.92 us -> 4.93 us
  between operations: 5.61 us -> 3.11 us
  starting transfers between devices: 63 us -> 65.2 us
    ppermute x6 -> x7, waiting for transfers between devices: 22 us -> 15.4 us  [swap(): return lax.ppermute(value, axis, [(0, 1), (1, 0)])]
    all_to_all x5, waiting for transfers between devices: 28 us -> 21.7 us  [exchange(): return lax.all_to_all(value, axes, 0, 0, tiled=True)]
    ppermute x5, waiting for transfers between devices: 8.73 us -> 13.8 us  [from_tile(): return lax.ppermute(value, TILE_AXES, route)]
    pallas_call x0 -> x1, Pallas kernels: none -> 3.83 us  [finish(): pl.pallas_call(finish_kernel, grid_spec=pltpu.PrefetchScalarGridSpec(num_...]
    add x3 -> x2, other arithmetic: 3.46 us -> 0.09 us  [the longest x1 0.05 us: update(): summed = terms[0] + swap(terms[1].astype(BF16), 'c').astype(F32)]
    all_to_all x5, starting transfers between devices: 33.8 us -> 35.5 us  [exchange(): return lax.all_to_all(value, axes, 0, 0, tiled=True)]
    ppermute x6 -> x7, starting transfers between devices: 13.2 us -> 14.1 us  [swap(): return lax.ppermute(value, axis, [(0, 1), (1, 0)])]
  transfers between devices with their start and end apart: 19 -> 20, of which waited for: 10 -> 12; matrix products, arithmetic and copies ran while one was open for 6% -> 4% of each run, Pallas kernels for 2% -> 2%
where the time goes in v4:
time: 149 us; the launch traced here: 148 us
  starting transfers between devices  65.2 us (44%)
  waiting for transfers between devices  50.9 us (34%)
  Pallas kernels  21.4 us (14%)
  local copies, waits for them, and re-layouts  4.93 us (3%)
  between operations  3.11 us (2%)
  other arithmetic  2.49 us (2%)
    all_to_all x5, starting transfers between devices, exchange(): return lax.all_to_all(value, axes, 0, 0, tiled=True)  35.5 us
    all_to_all x5, waiting for transfers between devices, exchange(): return lax.all_to_all(value, axes, 0, 0, tiled=True)  21.7 us
    ppermute x7, waiting for transfers between devices, swap(): return lax.ppermute(value, axis, [(0, 1), (1, 0)])  15.4 us
    ppermute x7, starting transfers between devices, swap(): return lax.ppermute(value, axis, [(0, 1), (1, 0)])  14.1 us
    ppermute x5, waiting for transfers between devices, from_tile(): return lax.ppermute(value, TILE_AXES, route)  13.8 us
    ppermute x5, starting transfers between devices, from_tile(): return lax.ppermute(value, TILE_AXES, route)  11 us
    pallas_call x1, Pallas kernels, backward(): pl.pallas_call(backward_kernel, grid_spec=pltpu.PrefetchScalarGridSpec(nu...  7.29 us
    pallas_call x1, Pallas kernels, forward(): pl.pallas_call(forward_kernel, grid_spec=pltpu.PrefetchScalarGridSpec(num...  5.68 us
  transfers between devices with their start and end apart: 20, of which 12 were waited for; matrix products, arithmetic and copies ran while one was open for 4% of the time, Pallas kernels for 2%

profile of v4, /device:TPU:1, one launch (start us, length us, event | category | flops | bytes accessed | tf_op | source)
XLA Modules:
  0.0 148.0 jit_solution(3232735738791203951)
XLA Ops:
  0.7 0.6 copy-done.9
  1.3 0.1 dynamic_update_slice.5
  1.4 3.5 %collective-permute-start = (s32[1,128]{1,0:T(1,128)S(1)}, s32[1,128]{1,0:T(1,128)S(1)}, u32[]{:S(2)}, u32[]{:S(2)}) collective-permute-start(s32[1,128]{1,0:T(1,128)S(1)} %dynamic_update_slice.5), channel_id=1, source_target_pairs={{4,0},{8,4},{12,8},{0,12},{5,1},{9,5},{13,9},{1,13},{6,2},{10,6},{... | collective-permute-start | bytes 1544 | tf_op jit(solution)/shard_map/ppermute | solution.py:430
  4.8 0.5 collective-permute-start.1
  5.3 0.6 collective-permute-start.2
  6.0 0.1 reshape.58
  6.0 3.5 %collective-permute-start.5 = (s32[1,128]{1,0:T(1,128)S(1)}, s32[1,128]{1,0:T(1,128)S(1)}, u32[]{:S(2)}, u32[]{:S(2)}) collective-permute-start(s32[1,128]{1,0:T(1,128)S(1)} %pad.4), channel_id=1, source_target_pairs={{0,32},{4,36},{8,40},{12,44},{16,48},{20,52},{24,56},{28,60},{32,6... | collective-permute-start | bytes 1544 | tf_op jit(solution)/shard_map/ppermute | solution.py:384
  9.6 0.0 copy-start.5
  9.6 1.1 fusion
  10.7 1.3 collective-permute-start.4
  12.1 0.7 broadcast_in_dim.45
  12.8 12.6 %all-to-all-start = ((bf16[8,64,256]{2,1,0:T(8,128)(2,1)}), bf16[8,64,256]{2,1,0:T(8,128)(2,1)S(1)}, u32[]{:S(2)}, u32[]{:S(2)}) async-start(bf16[8,64,256]{2,1,0:T(8,128)(2,1)} %broadcast_in_dim.45), calls=%async_computation | async-start | bytes 524288 | tf_op jit(solution)/shard_map/all_to_all | solution.py:388
  25.4 0.0 collective-permute-done
  25.4 0.1 fusion.8
  25.5 0.1 add.55
  25.6 0.0 collective-permute-done.1
  25.6 0.1 collective-permute-start.3
  25.7 0.6 constant_dynamic-slice_fusion
  26.3 0.6 iota_compare_fusion
  27.0 1.2 collective-permute-done.3
  28.1 6.7 %all-to-all-done = bf16[8,64,256]{2,1,0:T(8,128)(2,1)S(1)} async-done(((bf16[8,64,256]{2,1,0:T(8,128)(2,1)}), bf16[8,64,256]{2,1,0:T(8,128)(2,1)S(1)}, u32[]{:S(2)}, u32[]{:S(2)}) %all-to-all-start) | async-done | bytes 262176 | tf_op jit(solution)/shard_map/all_to_all | solution.py:388
  34.9 1.6 %shard_map.156 = bf16[16,8,16,256]{3,2,1,0:T(8,128)(2,1)} custom-call(s32[16]{0:T(128)S(1)} %slice_bitcast_fusion.2.ids, bf16[8,4,16,256]{3,2,1,0:T(8,128)(2,1)S(1)} %bitcast.47), custom_call_target="tpu_custom_call" | custom-call | tf_op jit(solution)/shard_map/pallas_call | solution.py:300
  36.4 4.1 %all-to-all-start.1 = ((bf16[16,8,16,256]{3,2,1,0:T(8,128)(2,1)}), bf16[16,8,16,256]{3,2,1,0:T(8,128)(2,1)S(1)}, u32[]{:S(2)}, u32[]{:S(2)}) async-start(bf16[16,8,16,256]{3,2,1,0:T(8,128)(2,1)} %shard_map.156), calls=%async_computation.1 | async-start | bytes 2097152 | tf_op jit(solution)/shard_map/all_to_all | solution.py:388
  40.7 1.3 collective-permute-start.6
  42.0 0.2 fusion.9
  42.8 0.1 concatenate.3.info
  42.9 0.5 fusion.10
  43.4 1.3 iota_compare_fusion.1
  44.8 3.3 %collective-permute-done.6 = bf16[2,256,256]{2,1,0:T(8,128)(2,1)S(1)} collective-permute-done((bf16[2,256,256]{2,1,0:T(8,128)(2,1)S(1)}, bf16[2,256,256]{2,1,0:T(8,128)(2,1)S(1)}, u32[]{:S(2)}, u32[]{:S(2)}) %collective-permute-start.6) | collective-permute-done | bytes 262176 | tf_op jit(solution)/shard_map/ppermute | solution.py:384
  48.1 0.1 select_select_fusion.mixed
  48.2 0.0 copy-start.1
  48.2 0.8 shard_map.157.mine
  49.0 4.6 %collective-permute-start.7 = (bf16[2,256,256]{2,1,0:T(8,128)(2,1)S(1)}, bf16[2,256,256]{2,1,0:T(8,128)(2,1)S(1)}, u32[]{:S(2)}, u32[]{:S(2)}) collective-permute-start(bf16[2,256,256]{2,1,0:T(8,128)(2,1)S(1)} %shard_map.157.mine), channel_id=1, source_target_pairs={{0,1},{1,0},{2,3},{3,2},{4,5},{5,4},{6,7},{7,6},{8,9},{9,8},{10,11... | collective-permute-start | bytes 786440 | tf_op jit(solution)/shard_map/ppermute | solution.py:379
  53.6 1.2 collective-permute-done.7.other
  54.8 0.0 all-to-all-done.1
  54.8 5.7 %shard_map.158 = (bf16[4,2,256,256]{3,2,1,0:T(8,128)(2,1)S(1)}, bf16[4,2,256,256]{3,2,1,0:T(8,128)(2,1)S(1)}, bf16[4,2,256,256]{3,2,1,0:T(8,128)(2,1)S(1)}, f32[256,256]{1,0:T(8,128)S(1)}) custom-call(s32[7]{0:T(128)S(1)} %concatenate.3.info, bf16[8,2,8,16,256]{4,3,2,1,0:T(8,128)(2,1)S(1)} %bitcast.46, bf16[2,256,256]{2,1,0:T(8,128)(2,1)S(1)} %shard_map.157.mine, ...), custom_call_target="tpu_custom_call" | custom-call | tf_op jit(solution)/shard_map/pallas_call | solution.py:330
  60.5 4.6 %collective-permute-start.8 = (f32[256,256]{1,0:T(8,128)S(1)}, f32[256,256]{1,0:T(8,128)S(1)}, u32[]{:S(2)}, u32[]{:S(2)}) collective-permute-start(f32[256,256]{1,0:T(8,128)S(1)} %get-tuple-element.18.power_a), channel_id=1, source_target_pairs={{0,1},{1,0},{2,3},{3,2},{4,5},{5,4},{6,7},{7,6},{8,9},{9,8},{10,11... | collective-permute-start | bytes 786440 | tf_op jit(solution)/shard_map/ppermute | solution.py:379
  65.1 1.2 collective-permute-done.8.power_b
  66.2 7.3 %shard_map.159 = (f32[2,2,256,256]{3,2,1,0:T(8,128)S(1)}, bf16[8,2,8,16,256]{4,3,2,1,0:T(8,128)(2,1)}) custom-call(s32[7]{0:T(128)S(1)} %concatenate.3.info, bf16[4,2,256,256]{3,2,1,0:T(8,128)(2,1)S(1)} %get-tuple-element.15.psi, bf16[4,2,256,256]{3,2,1,0:T(8,128)(2,1)S(1)} %get-tuple-element.16.inc, bf16[4,2,256,256]{3,2,1,0:T(8,128)(2,1)S(1)} %get-tuple-element.17.far, ...), custom_call_target="tpu_custom_call" | custom-call | tf_op jit(solution)/shard_map/pallas_call | solution.py:353
  73.6 0.5 collective-permute-start.9
  74.0 1.2 collective-permute-done.9
  75.2 0.1 bitcast_add_fusion
  75.3 1.2 collective-permute-start.10
  76.5 5.2 %collective-permute-done.10.other = bf16[256,256]{1,0:T(8,128)(2,1)S(1)} collective-permute-done((bf16[256,256]{1,0:T(8,128)(2,1)S(1)}, bf16[256,256]{1,0:T(8,128)(2,1)S(1)}, u32[]{:S(2)}, u32[]{:S(2)}) %collective-permute-start.10) | collective-permute-done | bytes 131104 | tf_op jit(solution)/shard_map/ppermute | solution.py:379
  81.7 0.9 shard_map.161
  82.6 2.4 %collective-permute-start.11 = (bf16[2,256,256]{2,1,0:T(8,128)(2,1)S(1)}, bf16[2,256,256]{2,1,0:T(8,128)(2,1)S(1)}, u32[]{:S(2)}, u32[]{:S(2)}) collective-permute-start(bf16[2,256,256]{2,1,0:T(8,128)(2,1)S(1)} %get-tuple-element.22), channel_id=1, source_target_pairs={{0,32},{4,36},{8,40},{12,44},{16,48},{20,52},{24,56},{28,60},{32,6... | collective-permute-start | bytes 786440 | tf_op jit(solution)/shard_map/ppermute | solution.py:384
  85.1 3.7 %all-to-all-start.2 = ((bf16[16,8,16,256]{3,2,1,0:T(8,128)(2,1)}), bf16[16,8,16,256]{3,2,1,0:T(8,128)(2,1)S(1)}, u32[]{:S(2)}, u32[]{:S(2)}) async-start(bf16[16,8,16,256]{3,2,1,0:T(8,128)(2,1)} %bitcast.12), calls=%async_computation.2 | async-start | bytes 2097152 | tf_op jit(solution)/shard_map/all_to_all | solution.py:388
  88.7 0.7 collective-permute-done.11
  89.6 2.4 %collective-permute-start.12 = (bf16[256,256]{1,0:T(8,128)(2,1)S(1)}, bf16[256,256]{1,0:T(8,128)(2,1)S(1)}, u32[]{:S(2)}, u32[]{:S(2)}) collective-permute-start(bf16[256,256]{1,0:T(8,128)(2,1)S(1)} %fusion.3), channel_id=1, source_target_pairs={{0,4},{4,8},{8,12},{12,16},{16,20},{20,24},{24,28},{28,32},{32,36}... | collective-permute-start | bytes 393224 | tf_op jit(solution)/shard_map/ppermute | solution.py:384
  92.0 9.7 %collective-permute-done.12 = bf16[256,256]{1,0:T(8,128)(2,1)S(1)} collective-permute-done((bf16[256,256]{1,0:T(8,128)(2,1)S(1)}, bf16[256,256]{1,0:T(8,128)(2,1)S(1)}, u32[]{:S(2)}, u32[]{:S(2)}) %collective-permute-start.12) | collective-permute-done | bytes 131104 | tf_op jit(solution)/shard_map/ppermute | solution.py:384
  101.8 2.6 %collective-permute-start.13 = (f32[256,256]{1,0:T(8,128)S(1)}, f32[256,256]{1,0:T(8,128)S(1)}, u32[]{:S(2)}, u32[]{:S(2)}) collective-permute-start(f32[256,256]{1,0:T(8,128)S(1)} %fusion.5.layer), channel_id=1, source_target_pairs={{0,2},{2,0},{1,3},{3,1},{4,6},{6,4},{5,7},{7,5},{8,10},{10,8},{9,1... | collective-permute-start | bytes 786440 | tf_op jit(solution)/shard_map/ppermute | solution.py:379
  104.4 0.0 all-to-all-done.2.src
  104.4 1.1 shard_map.160
  105.5 4.7 %all-to-all-start.3 = ((bf16[8,64,256]{2,1,0:T(8,128)(2,1)}), bf16[8,64,256]{2,1,0:T(8,128)(2,1)S(1)}, u32[]{:S(2)}, u32[]{:S(2)}) async-start(bf16[8,64,256]{2,1,0:T(8,128)(2,1)} %shard_map.160), calls=%async_computation.3 | async-start | bytes 524288 | tf_op jit(solution)/shard_map/all_to_all | solution.py:388
  110.2 5.6 %collective-permute-done.13 = f32[256,256]{1,0:T(8,128)S(1)} collective-permute-done((f32[256,256]{1,0:T(8,128)S(1)}, f32[256,256]{1,0:T(8,128)S(1)}, u32[]{:S(2)}, u32[]{:S(2)}) %collective-permute-start.13) | collective-permute-done | bytes 262176 | tf_op jit(solution)/shard_map/ppermute | solution.py:379
  115.9 0.0 copy-start.2
  115.9 0.5 collective-permute-start.14
  116.4 3.2 %all-to-all-done.3.src = bf16[8,64,256]{2,1,0:T(8,128)(2,1)S(1)} async-done(((bf16[8,64,256]{2,1,0:T(8,128)(2,1)}), bf16[8,64,256]{2,1,0:T(8,128)(2,1)S(1)}, u32[]{:S(2)}, u32[]{:S(2)}) %all-to-all-start.3) | async-done | bytes 262176 | tf_op jit(solution)/shard_map/all_to_all | solution.py:388
  119.6 0.2 shard_map.162
  119.8 0.7 broadcast_in_dim.50
  120.5 10.4 %all-to-all-start.4 = ((f32[256,1,128]{2,1,0:T(1,128)}), f32[256,1,128]{2,1,0:T(1,128)S(1)}, u32[]{:S(2)}, u32[]{:S(2)}) async-start(f32[256,1,128]{2,1,0:T(1,128)} %broadcast_in_dim.50), calls=%async_computation.4 | async-start | bytes 262144 | tf_op jit(solution)/shard_map/all_to_all | solution.py:388
  132.2 0.0 copy-start.7
  132.3 11.8 %all-to-all-done.4.packed = f32[256,1,128]{2,1,0:T(1,128)S(1)} async-done(((f32[256,1,128]{2,1,0:T(1,128)}), f32[256,1,128]{2,1,0:T(1,128)S(1)}, u32[]{:S(2)}, u32[]{:S(2)}) %all-to-all-start.4) | async-done | bytes 131104 | tf_op jit(solution)/shard_map/all_to_all | solution.py:388
  144.0 3.8 %shard_map.163 = (f32[1,2,2,256,256]{4,3,2,1,0:T(8,128)}, f32[1,2,2,256,256]{4,3,2,1,0:T(8,128)}, f32[4,2,2,4,256]{4,3,2,1,0:T(4,128)}, f32[4,2,2,4,256]{4,3,2,1,0:T(4,128)}) custom-call(s32[7]{0:T(128)S(1)} %concatenate.3.info, s32[2]{0:T(128)S(1)} %copy-done.7, f32[1]{0:T(128)S(6)} %copy.20.object_norm, f32[1]{0:T(128)S(6)} %copy.21.probe_norm, ...), custom_call_target="tpu_custom_call" | custom-call | tf_op jit(solution)/shard_map/pallas_call | solution.py:267
  (35 shorter events, 0.4 us)
Async XLA Ops:
  0.6 0.7 copy-start.9
  1.3 4.7 %copy-start.8 = (s32[2,2]{1,0:T(2,128)S(1)}, s32[2,2]{1,0:T(2,128)}, u32[]{:S(2)}) copy-start(s32[2,2]{1,0:T(2,128)} %param.18) | copy-start | bytes 52
  1.4 24.1 %collective-permute-start = (s32[1,128]{1,0:T(1,128)S(1)}, s32[1,128]{1,0:T(1,128)S(1)}, u32[]{:S(2)}, u32[]{:S(2)}) collective-permute-start(s32[1,128]{1,0:T(1,128)S(1)} %dynamic_update_slice.5), channel_id=1, source_target_pairs={{4,0},{8,4},{12,8},{0,12},{5,1},{9,5},{13,9},{1,13},{6,2},{10,6},{... | collective-permute-start | bytes 1544 | tf_op jit(solution)/shard_map/ppermute | solution.py:430
  4.8 20.8 %collective-permute-start.1 = (s32[1,128]{1,0:T(1,128)S(1)}, s32[1,128]{1,0:T(1,128)S(1)}, u32[]{:S(2)}, u32[]{:S(2)}) collective-permute-start(s32[1,128]{1,0:T(1,128)S(1)} %dynamic_update_slice.5), channel_id=1, source_target_pairs={{8,0},{12,4},{0,8},{4,12},{9,1},{13,5},{1,9},{5,13},{10,2},{14,6},... | collective-permute-start | bytes 1544 | tf_op jit(solution)/shard_map/ppermute | solution.py:430
  5.3 20.3 %collective-permute-start.2 = (s32[1,128]{1,0:T(1,128)S(1)}, s32[1,128]{1,0:T(1,128)S(1)}, u32[]{:S(2)}, u32[]{:S(2)}) collective-permute-start(s32[1,128]{1,0:T(1,128)S(1)} %dynamic_update_slice.5), channel_id=1, source_target_pairs={{12,0},{0,4},{4,8},{8,12},{13,1},{1,5},{5,9},{9,13},{14,2},{2,6},{... | collective-permute-start | bytes 1544 | tf_op jit(solution)/shard_map/ppermute | solution.py:430
  6.0 19.7 %collective-permute-start.5 = (s32[1,128]{1,0:T(1,128)S(1)}, s32[1,128]{1,0:T(1,128)S(1)}, u32[]{:S(2)}, u32[]{:S(2)}) collective-permute-start(s32[1,128]{1,0:T(1,128)S(1)} %pad.4), channel_id=1, source_target_pairs={{0,32},{4,36},{8,40},{12,44},{16,48},{20,52},{24,56},{28,60},{32,6... | collective-permute-start | bytes 1544 | tf_op jit(solution)/shard_map/ppermute | solution.py:384
  9.6 2.4 %copy-start.5 = (f32[4,2,2,4,256]{4,3,2,1,0:T(4,128)S(1)}, f32[4,2,2,4,256]{4,3,2,1,0:T(4,128)}, u32[]{:S(2)}) copy-start(f32[4,2,2,4,256]{4,3,2,1,0:T(4,128)} %probe.1) | copy-start | bytes 196612
  10.7 29.9 %collective-permute-start.4 = (bf16[2,256,256]{2,1,0:T(8,128)(2,1)S(1)}, bf16[2,256,256]{2,1,0:T(8,128)(2,1)S(1)}, u32[]{:S(2)}, u32[]{:S(2)}) collective-permute-start(bf16[2,256,256]{2,1,0:T(8,128)(2,1)S(1)} %fusion), channel_id=1, source_target_pairs={{4,0},{8,4},{12,8},{16,12},{20,16},{24,20},{28,24},{32,28},{36,32}... | collective-permute-start | bytes 786440 | tf_op jit(solution)/shard_map/ppermute | solution.py:384
  12.8 22.1 %all-to-all-start = ((bf16[8,64,256]{2,1,0:T(8,128)(2,1)}), bf16[8,64,256]{2,1,0:T(8,128)(2,1)S(1)}, u32[]{:S(2)}, u32[]{:S(2)}) async-start(bf16[8,64,256]{2,1,0:T(8,128)(2,1)} %broadcast_in_dim.45), calls=%async_computation | async-start | bytes 524288 | tf_op jit(solution)/shard_map/all_to_all | solution.py:388
  25.6 2.5 %collective-permute-start.3 = (s32[1,128]{1,0:T(1,128)S(1)}, s32[1,128]{1,0:T(1,128)S(1)}, u32[]{:S(2)}, u32[]{:S(2)}) collective-permute-start(s32[1,128]{1,0:T(1,128)S(1)} %add_add_fusion), channel_id=1, source_target_pairs={{0,16},{16,0},{1,17},{17,1},{2,18},{18,2},{3,19},{19,3},{4,20},{20... | collective-permute-start | bytes 1544 | tf_op jit(solution)/shard_map/ppermute | solution.py:379
  36.4 4.2 %copy-start = (f32[1,2,2,256,256]{4,3,2,1,0:T(8,128)S(1)}, f32[1,2,2,256,256]{4,3,2,1,0:T(8,128)}, u32[]{:S(2)}) copy-start(f32[1,2,2,256,256]{4,3,2,1,0:T(8,128)} %tiles.1) | copy-start | bytes 3145732
  36.4 18.4 %all-to-all-start.1 = ((bf16[16,8,16,256]{3,2,1,0:T(8,128)(2,1)}), bf16[16,8,16,256]{3,2,1,0:T(8,128)(2,1)S(1)}, u32[]{:S(2)}, u32[]{:S(2)}) async-start(bf16[16,8,16,256]{3,2,1,0:T(8,128)(2,1)} %shard_map.156), calls=%async_computation.1 | async-start | bytes 2097152 | tf_op jit(solution)/shard_map/all_to_all | solution.py:388
  40.7 7.4 %collective-permute-start.6 = (bf16[2,256,256]{2,1,0:T(8,128)(2,1)S(1)}, bf16[2,256,256]{2,1,0:T(8,128)(2,1)S(1)}, u32[]{:S(2)}, u32[]{:S(2)}) collective-permute-start(bf16[2,256,256]{2,1,0:T(8,128)(2,1)S(1)} %broadcast_select_fusion), channel_id=1, source_target_pairs={{32,0},{36,4},{40,8},{44,12},{48,16},{52,20},{56,24},{60,28},{64,3... | collective-permute-start | bytes 786440 | tf_op jit(solution)/shard_map/ppermute | solution.py:384
  48.1 6.7 %copy-start.3 = (bf16[2,256,256]{2,1,0:T(8,128)(2,1)S(1)}, bf16[2,256,256]{2,1,0:T(8,128)(2,1)}, u32[]{:S(2)}) copy-start(bf16[2,256,256]{2,1,0:T(8,128)(2,1)} %constant.45.clone.dft) | copy-start | bytes 786436
  48.2 6.6 %copy-start.1 = (f32[2,256,256]{2,1,0:T(8,128)S(1)}, f32[2,256,256]{2,1,0:T(8,128)}, u32[]{:S(2)}) copy-start(f32[2,256,256]{2,1,0:T(8,128)} %constant.46.clone.kern) | copy-start | bytes 1572868
  49.0 5.8 %collective-permute-start.7 = (bf16[2,256,256]{2,1,0:T(8,128)(2,1)S(1)}, bf16[2,256,256]{2,1,0:T(8,128)(2,1)S(1)}, u32[]{:S(2)}, u32[]{:S(2)}) collective-permute-start(bf16[2,256,256]{2,1,0:T(8,128)(2,1)S(1)} %shard_map.157.mine), channel_id=1, source_target_pairs={{0,1},{1,0},{2,3},{3,2},{4,5},{5,4},{6,7},{7,6},{8,9},{9,8},{10,11... | collective-permute-start | bytes 786440 | tf_op jit(solution)/shard_map/ppermute | solution.py:379
  54.8 11.4 %copy-start.4 = (f32[2,256,256]{2,1,0:T(8,128)S(1)}, f32[2,256,256]{2,1,0:T(8,128)}, u32[]{:S(2)}) copy-start(f32[2,256,256]{2,1,0:T(8,128)} %pattern.1) | copy-start | bytes 1572868
  60.5 5.7 %collective-permute-start.8 = (f32[256,256]{1,0:T(8,128)S(1)}, f32[256,256]{1,0:T(8,128)S(1)}, u32[]{:S(2)}, u32[]{:S(2)}) collective-permute-start(f32[256,256]{1,0:T(8,128)S(1)} %get-tuple-element.18.power_a), channel_id=1, source_target_pairs={{0,1},{1,0},{2,3},{3,2},{4,5},{5,4},{6,7},{7,6},{8,9},{9,8},{10,11... | collective-permute-start | bytes 786440 | tf_op jit(solution)/shard_map/ppermute | solution.py:379
  73.6 1.6 %collective-permute-start.9 = (bf16[2,256,256]{2,1,0:T(8,128)(2,1)S(1)}, bf16[2,256,256]{2,1,0:T(8,128)(2,1)S(1)}, u32[]{:S(2)}, u32[]{:S(2)}) collective-permute-start(bf16[2,256,256]{2,1,0:T(8,128)(2,1)S(1)} %fusion.1), channel_id=1, source_target_pairs={{0,1},{1,0},{2,3},{3,2},{4,5},{5,4},{6,7},{7,6},{8,9},{9,8},{10,11... | collective-permute-start | bytes 786440 | tf_op jit(solution)/shard_map/ppermute | solution.py:379
  75.3 6.5 %collective-permute-start.10 = (bf16[256,256]{1,0:T(8,128)(2,1)S(1)}, bf16[256,256]{1,0:T(8,128)(2,1)S(1)}, u32[]{:S(2)}, u32[]{:S(2)}) collective-permute-start(bf16[256,256]{1,0:T(8,128)(2,1)S(1)} %fusion.6), channel_id=1, source_target_pairs={{0,2},{2,0},{1,3},{3,1},{4,6},{6,4},{5,7},{7,5},{8,10},{10,8},{9,1... | collective-permute-start | bytes 393224 | tf_op jit(solution)/shard_map/ppermute | solution.py:379
  82.6 6.8 %collective-permute-start.11 = (bf16[2,256,256]{2,1,0:T(8,128)(2,1)S(1)}, bf16[2,256,256]{2,1,0:T(8,128)(2,1)S(1)}, u32[]{:S(2)}, u32[]{:S(2)}) collective-permute-start(bf16[2,256,256]{2,1,0:T(8,128)(2,1)S(1)} %get-tuple-element.22), channel_id=1, source_target_pairs={{0,32},{4,36},{8,40},{12,44},{16,48},{20,52},{24,56},{28,60},{32,6... | collective-permute-start | bytes 786440 | tf_op jit(solution)/shard_map/ppermute | solution.py:384
  85.1 19.3 %all-to-all-start.2 = ((bf16[16,8,16,256]{3,2,1,0:T(8,128)(2,1)}), bf16[16,8,16,256]{3,2,1,0:T(8,128)(2,1)S(1)}, u32[]{:S(2)}, u32[]{:S(2)}) async-start(bf16[16,8,16,256]{3,2,1,0:T(8,128)(2,1)} %bitcast.12), calls=%async_computation.2 | async-start | bytes 2097152 | tf_op jit(solution)/shard_map/all_to_all | solution.py:388
  89.6 12.2 %collective-permute-start.12 = (bf16[256,256]{1,0:T(8,128)(2,1)S(1)}, bf16[256,256]{1,0:T(8,128)(2,1)S(1)}, u32[]{:S(2)}, u32[]{:S(2)}) collective-permute-start(bf16[256,256]{1,0:T(8,128)(2,1)S(1)} %fusion.3), channel_id=1, source_target_pairs={{0,4},{4,8},{8,12},{12,16},{16,20},{20,24},{24,28},{28,32},{32,36}... | collective-permute-start | bytes 393224 | tf_op jit(solution)/shard_map/ppermute | solution.py:384
  101.8 14.0 %collective-permute-start.13 = (f32[256,256]{1,0:T(8,128)S(1)}, f32[256,256]{1,0:T(8,128)S(1)}, u32[]{:S(2)}, u32[]{:S(2)}) collective-permute-start(f32[256,256]{1,0:T(8,128)S(1)} %fusion.5.layer), channel_id=1, source_target_pairs={{0,2},{2,0},{1,3},{3,1},{4,6},{6,4},{5,7},{7,5},{8,10},{10,8},{9,1... | collective-permute-start | bytes 786440 | tf_op jit(solution)/shard_map/ppermute | solution.py:379
  105.5 14.1 %all-to-all-start.3 = ((bf16[8,64,256]{2,1,0:T(8,128)(2,1)}), bf16[8,64,256]{2,1,0:T(8,128)(2,1)S(1)}, u32[]{:S(2)}, u32[]{:S(2)}) async-start(bf16[8,64,256]{2,1,0:T(8,128)(2,1)} %shard_map.160), calls=%async_computation.3 | async-start | bytes 524288 | tf_op jit(solution)/shard_map/all_to_all | solution.py:388
  115.9 28.1 %copy-start.2 = (f32[1,2,2,256,256]{4,3,2,1,0:T(8,128)S(1)}, f32[1,2,2,256,256]{4,3,2,1,0:T(8,128)}, u32[]{:S(2)}) copy-start(f32[1,2,2,256,256]{4,3,2,1,0:T(8,128)} %before.1) | copy-start | bytes 3145732
  115.9 16.3 %collective-permute-start.14 = (f32[2,256,256]{2,1,0:T(8,128)S(1)}, f32[2,256,256]{2,1,0:T(8,128)}, u32[]{:S(2)}, u32[]{:S(2)}) collective-permute-start(f32[2,256,256]{2,1,0:T(8,128)S(1)} %pad_maximum_fusion.layer), channel_id=1, source_target_pairs={{0,1},{1,0},{2,3},{3,2},{4,5},{5,4},{6,7},{7,6},{8,9},{9,8},{10,11... | collective-permute-start | bytes 1572872 | tf_op jit(solution)/shard_map/ppermute | solution.py:379
  120.5 23.5 %copy-start.6 = (f32[4,2,2,4,256]{4,3,2,1,0:T(4,128)S(1)}, f32[4,2,2,4,256]{4,3,2,1,0:T(4,128)}, u32[]{:S(2)}) copy-start(f32[4,2,2,4,256]{4,3,2,1,0:T(4,128)} %probe_before.1) | copy-start | bytes 196612
  120.5 23.5 %all-to-all-start.4 = ((f32[256,1,128]{2,1,0:T(1,128)}), f32[256,1,128]{2,1,0:T(1,128)S(1)}, u32[]{:S(2)}, u32[]{:S(2)}) async-start(f32[256,1,128]{2,1,0:T(1,128)} %broadcast_in_dim.50), calls=%async_computation.4 | async-start | bytes 262144 | tf_op jit(solution)/shard_map/all_to_all | solution.py:388
  132.2 11.8 %copy-start.7 = (s32[2]{0:T(128)S(1)}, s32[2]{0:T(128)}, u32[]{:S(2)}) copy-start(s32[2]{0:T(128)} %steps.1) | copy-start | bytes 28

commit v5 on v4

--- a/solution.py
+++ b/solution.py
@@ -74,22 +74,27 @@
     return (natural == i * 64 + ri * 32 + band * 4 + r).astype(F32).astype(BF16)
 
 
-def fill(step, dft, plus, minus):
-    @pl.when(step == 0)
-    def _():
-        for i in range(2):
-            at = slice(i * W, (i + 1) * W)
-            plus[at, at] = dft[0]
-            minus[at, at] = dft[0]
-        for ref, a, b in ((plus, dft[1], -dft[1]), (minus, -dft[1], dft[1])):
-            ref[:W, W:] = a
-            ref[W:, :W] = b
+def fill(dft, plus, minus):
+    for i in range(2):
+        at = slice(i * W, (i + 1) * W)
+        plus[at, at] = dft[0]
+        minus[at, at] = dft[0]
+    for ref, a, b in ((plus, dft[1], -dft[1]), (minus, -dft[1], dft[1])):
+        ref[:W, W:] = a
+        ref[W:, :W] = b
 
 
 def window_masks(row, col):
     rows = lax.broadcasted_iota(jnp.int32, (W, W), 0)
     cols = lax.broadcasted_iota(jnp.int32, (W, W), 1)
     return rows >= row, cols >= col
+
+
+def choose_kernel(above, own, east, out):
+    col = above[2 + lax.axis_index("yh")]
+    left = lax.broadcasted_iota(jnp.int32, (W, W), 1) >= col
+    for ri in range(2):
+        out[ri] = jnp.where(left, own[ri].astype(F32), east[ri].astype(F32)).astype(BF16)
 
 
 def patch_kernel(info, mixed, out):
@@ -106,84 +111,78 @@
         out[d] = src[:, ids[d]]
 
 
-def forward_kernel(info, blocks, mine, other, dft, kern, psi, inc, far, power, plus, minus):
-    step = pl.program_id(0)
+def forward_kernel(info, blocks, mine, other, dft, kern, all_psi, all_inc, all_far, power, plus, minus):
     first = info[2] == 0
-    fill(step, dft, plus, minus)
+    fill(dft, plus, minus)
     order = placing(0)
-    for z in range(NZ):
-        piece = blocks[:, 0, z].reshape(128, W)
-        placed = mm(order, piece).astype(BF16)
-        for i in range(2):
-            for ri in range(2):
-                at = i * 64 + ri * 32
-                psi[i, ri, z * BAND : (z + 1) * BAND] = placed[at : at + BAND]
-    fwd, inv = plus[...], minus[...]
-    p0 = [jnp.where(first, mine[ri], other[ri]) for ri in range(2)]
-    p1 = [jnp.where(first, other[ri], mine[ri]) for ri in range(2)]
-    pairs = range(2)
-    spec = transform([times(psi[i, 0], psi[i, 1], *p0) for i in pairs], fwd, inv)
-    moved = transform([times(*spec[i], kern[0], kern[1]) for i in pairs], inv, fwd)
-    for i in pairs:
-        inc[i, 0], inc[i, 1] = moved[i]
-    waves = transform([times(*moved[i], *p1) for i in pairs], fwd, inv)
-    total = None
-    for i in pairs:
-        far[i, 0], far[i, 1] = waves[i]
-        f_re, f_im = waves[i][0].astype(F32), waves[i][1].astype(F32)
-        part = f_re * f_re + f_im * f_im
-        total = part if total is None else total + part
-
-    @pl.when(step == 0)
-    def _():
+    power[...] = jnp.zeros_like(power)
+
+    def pair(g, carry):
+        psi, inc, far = (ref.at[pl.ds(2 * g, 2)] for ref in (all_psi, all_inc, all_far))
+        for z in range(NZ):
+            piece = blocks[:, g, z].reshape(128, W)
+            placed = mm(order, piece).astype(BF16)
+            for i in range(2):
+                for ri in range(2):
+                    at = i * 64 + ri * 32
+                    psi[i, ri, z * BAND : (z + 1) * BAND] = placed[at : at + BAND]
+        fwd, inv = plus[...], minus[...]
+        p0 = [jnp.where(first, mine[ri], other[ri]) for ri in range(2)]
+        p1 = [jnp.where(first, other[ri], mine[ri]) for ri in range(2)]
+        pairs = range(2)
+        spec = transform([times(psi[i, 0], psi[i, 1], *p0) for i in pairs], fwd, inv)
+        moved = transform([times(*spec[i], kern[0], kern[1]) for i in pairs], inv, fwd)
+        for i in pairs:
+            inc[i, 0], inc[i, 1] = moved[i]
+        waves = transform([times(*moved[i], *p1) for i in pairs], fwd, inv)
+        total = power[...]
+        for i in pairs:
+            far[i, 0], far[i, 1] = waves[i]
+            f_re, f_im = waves[i][0].astype(F32), waves[i][1].astype(F32)
+            total = total + (f_re * f_re + f_im * f_im)
         power[...] = total
-
-    @pl.when(step != 0)
-    def _():
-        power[...] += total
-
-
-def backward_kernel(
-    info, psi, inc, far, power_a, power_b, pattern, mine, other, dft, kern, terms, out, scratch, plus, minus
-):
-    step = pl.program_id(0)
+        return carry
+
+    lax.fori_loop(0, 2, pair, 0)
+
+
+def backward_kernel(info, *refs):
+    all_psi, all_inc, all_far, power_a, power_b, patterns, mine, other, dft, kern = refs[:10]
+    terms, out, scratch, plus, minus = refs[10:]
     core = info[2]
     first = core == 0
-    fill(step, dft, plus, minus)
+    fill(dft, plus, minus)
     used = info[4].astype(F32)
-    fwd, inv = plus[...], minus[...]
-    p0 = [jnp.where(first, mine[ri], other[ri]) for ri in range(2)]
-    p1 = [jnp.where(first, other[ri], mine[ri]) for ri in range(2)]
-    double = 2.0 * ((power_a[...] + power_b[...] - pattern[0]) * used)
-    pairs = range(2)
-    back = transform([[double * far[i, ri].astype(F32) for ri in range(2)] for i in pairs], inv, fwd)
-    term1 = [conj_times(inc[i, 0], inc[i, 1], *back[i]) for i in pairs]
-    spec = transform([conj_times(*p1, *back[i]) for i in pairs], fwd, inv)
-    back = transform([times(*spec[i], kern[0], -kern[1]) for i in pairs], inv, fwd)
-    term0 = [conj_times(psi[i, 0], psi[i, 1], *back[i]) for i in pairs]
-    for i in pairs:
-        for ri, value in enumerate(conj_times(*p0, *back[i])):
-            scratch[i, ri] = value.astype(BF16)
-    sums = [t[0][ri] + t[1][ri] for t in (term0, term1) for ri in range(2)]
-    back = placing(1)
-    for z in range(NZ):
-        pieces = [
-            scratch[i, ri, z * BAND : (z + 1) * BAND] for i in range(2) for ri in range(2)
-        ]
-        piece = mm(back, jnp.concatenate(pieces, axis=0)).astype(BF16)
-        out[:, 0, z] = piece.reshape(NYLX, 16, W)
-    for layer in range(LAYERS):
-        slot = core if layer == 0 else 1 - core
-
-        @pl.when(step == 0)
-        def _():
-            terms[slot, 0] = sums[2 * layer]
-            terms[slot, 1] = sums[2 * layer + 1]
-
-        @pl.when(step != 0)
-        def _():
-            terms[slot, 0] += sums[2 * layer]
-            terms[slot, 1] += sums[2 * layer + 1]
+    back_order = placing(1)
+    terms[...] = jnp.zeros_like(terms)
+
+    def pair(g, carry):
+        psi, inc, far = (ref.at[pl.ds(2 * g, 2)] for ref in (all_psi, all_inc, all_far))
+        fwd, inv = plus[...], minus[...]
+        p0 = [jnp.where(first, mine[ri], other[ri]) for ri in range(2)]
+        p1 = [jnp.where(first, other[ri], mine[ri]) for ri in range(2)]
+        double = 2.0 * ((power_a[...] + power_b[...] - patterns[info[3]]) * used)
+        pairs = range(2)
+        back = transform([[double * far[i, ri].astype(F32) for ri in range(2)] for i in pairs], inv, fwd)
+        term1 = [conj_times(inc[i, 0], inc[i, 1], *back[i]) for i in pairs]
+        spec = transform([conj_times(*p1, *back[i]) for i in pairs], fwd, inv)
+        back = transform([times(*spec[i], kern[0], -kern[1]) for i in pairs], inv, fwd)
+        term0 = [conj_times(psi[i, 0], psi[i, 1], *back[i]) for i in pairs]
+        for i in pairs:
+            for ri, value in enumerate(conj_times(*p0, *back[i])):
+                scratch[i, ri] = value.astype(BF16)
+        for layer, term in enumerate((term0, term1)):
+            slot = core if layer == 0 else 1 - core
+            for ri in range(2):
+                terms[slot, ri] += term[0][ri] + term[1][ri]
+        for z in range(NZ):
+            at = slice(z * BAND, (z + 1) * BAND)
+            pieces = [scratch[i, ri, at] for i in range(2) for ri in range(2)]
+            piece = mm(back_order, jnp.concatenate(pieces, axis=0)).astype(BF16)
+            out[:, g, z] = piece.reshape(NYLX, 16, W)
+        return carry
+
+    lax.fori_loop(0, 2, pair, 0)
 
 
 def place_kernel(info, own, other, kept, right, low):
@@ -229,7 +228,9 @@
 def finish_kernel(
     info, steps, object_norm, probe_norm, packed, layer, other, tiles, before, grad, probe, probe_before, *outs
 ):
-    new_tiles, direction, new_probe, probe_direction, held, sems = outs
+    new_tiles, direction, new_probe, probe_direction, held, fetched, sems, fetch_sem = outs
+    fetch = pltpu.make_async_copy(other, fetched, fetch_sem)
+    fetch.start()
     totals = jnp.sum(packed[...].reshape(4 * TILES, 128), axis=0, keepdims=True)
     lane = lax.broadcasted_iota(jnp.int32, (1, 128), 1)
 
@@ -239,14 +240,16 @@
     ratio = square(0, TILES * LAYERS * 2 * W * W) / object_norm[0]
     rate = steps[0].astype(F32) / 1024.0
     copies = []
-    for l in range(LAYERS):
+    for turn in range(LAYERS):
+        l = info[2] if turn == 0 else 1 - info[2]
+        if turn == 1:
+            fetch.wait()
         for ri in range(2):
-            gradient = jnp.where(info[2] == l, layer[ri], other[ri])
-            turned = ratio * before[0, l, ri] - gradient
-            held[1, l, ri] = turned
-            held[0, l, ri] = tiles[0, l, ri] + rate * turned
+            turned = ratio * before[0, l, ri] - (layer, fetched)[turn][ri]
+            held[1, turn, ri] = turned
+            held[0, turn, ri] = tiles[0, l, ri] + rate * turned
             for k, target in enumerate((new_tiles, direction)):
-                copies.append(pltpu.make_async_copy(held.at[k, l, ri], target.at[0, l, ri], sems.at[k, l, ri]))
+                copies.append(pltpu.make_async_copy(held.at[k, turn, ri], target.at[0, l, ri], sems.at[k, turn, ri]))
                 copies[-1].start()
     ratio = square(1, SCANS * MODES * 2 * W * W) / probe_norm[0]
     probe_rate = steps[1].astype(F32) / 16384.0
@@ -269,9 +272,14 @@
         grid_spec=pltpu.PrefetchScalarGridSpec(
             num_scalar_prefetch=4,
             grid=(),
-            in_specs=[spec] * len(arrays),
+            in_specs=[spec, spec, away] + [spec] * (len(arrays) - 3),
             out_specs=[away, away, spec, spec],
-            scratch_shapes=[VMEM((2, LAYERS, 2, W, W), F32), pltpu.SemaphoreType.DMA((2, LAYERS, 2))],
+            scratch_shapes=[
+                VMEM((2, LAYERS, 2, W, W), F32),
+                VMEM((2, W, W), F32),
+                pltpu.SemaphoreType.DMA((2, LAYERS, 2)),
+                pltpu.SemaphoreType.DMA,
+            ],
         ),
         out_shape=[shape((1, LAYERS, 2, W, W), F32)] * 2 + [shape((SCANS, 2, 2, ROWS, W), F32)] * 2,
         compiler_params=pltpu.CompilerParams(vmem_limit_bytes=16 << 20),
@@ -294,7 +302,7 @@
     return jax.ShapeDtypeStruct(dims, dtype)
 
 
-def whole(kernel, out_shape, scalars, arrays, scratch=()):
+def whole(kernel, out_shape, scalars, arrays, scratch=(), limit=8):
     spec = pl.BlockSpec(memory_space=VMEM)
     single = not isinstance(out_shape, (list, tuple))
     return pl.pallas_call(
@@ -307,72 +315,26 @@
             scratch_shapes=list(scratch),
         ),
         out_shape=out_shape,
-        compiler_params=pltpu.CompilerParams(vmem_limit_bytes=8 << 20),
+        compiler_params=pltpu.CompilerParams(vmem_limit_bytes=limit << 20),
     )(scalars, *arrays)
 
 
-def fixed(dims):
-    return pl.BlockSpec(dims, lambda g, info: (0,) * len(dims))
-
-
-def stepped(dims, axis):
-    return pl.BlockSpec(dims, lambda g, info: tuple(g if a == axis else 0 for a in range(len(dims))))
-
-
 PAIR = (2, 2, W, W)
-BLOCKS = (NYLX, 1, NZ, 16, W)
 ALL_BLOCKS = (NYLX, NYH, NZ, 16, W)
 
 
+MATRIX = VMEM((2 * W, 2 * W), BF16)
+
+
 def forward(info, blocks, mine, other, consts):
-    dft, kern = consts
-    half = (2, W, W)
-    return pl.pallas_call(
-        forward_kernel,
-        grid_spec=pltpu.PrefetchScalarGridSpec(
-            num_scalar_prefetch=1,
-            grid=(2,),
-            in_specs=[
-                stepped(BLOCKS, 1),
-                fixed(half),
-                fixed(half),
-                fixed(half),
-                fixed(half),
-            ],
-            out_specs=[stepped(PAIR, 0), stepped(PAIR, 0), stepped(PAIR, 0), fixed((W, W))],
-            scratch_shapes=[VMEM((2 * W, 2 * W), BF16), VMEM((2 * W, 2 * W), BF16)],
-        ),
-        out_shape=[shape((4, 2, W, W), BF16)] * 3 + [shape((W, W), F32)],
-        compiler_params=pltpu.CompilerParams(dimension_semantics=("arbitrary",), vmem_limit_bytes=28 << 20),
-    )(info, blocks, mine, other, dft, kern)
+    outs = [shape((4, 2, W, W), BF16)] * 3 + [shape((W, W), F32)]
+    return whole(forward_kernel, outs, info, [blocks, mine, other, *consts], [MATRIX] * 2, 24)
 
 
 def backward(info, psi, inc, far, power_a, power_b, patterns, mine, other, consts):
-    dft, kern = consts
-    half = (2, W, W)
-    return pl.pallas_call(
-        backward_kernel,
-        grid_spec=pltpu.PrefetchScalarGridSpec(
-            num_scalar_prefetch=1,
-            grid=(2,),
-            in_specs=[
-                stepped(PAIR, 0),
-                stepped(PAIR, 0),
-                stepped(PAIR, 0),
-                fixed((W, W)),
-                fixed((W, W)),
-                pl.BlockSpec((1, W, W), lambda g, info: (info[3], 0, 0)),
-                fixed(half),
-                fixed(half),
-                fixed(half),
-                fixed(half),
-            ],
-            out_specs=[fixed(PAIR), stepped(BLOCKS, 1)],
-            scratch_shapes=[VMEM(PAIR, BF16), VMEM((2 * W, 2 * W), BF16), VMEM((2 * W, 2 * W), BF16)],
-        ),
-        out_shape=[shape(PAIR, F32), shape(ALL_BLOCKS, BF16)],
-        compiler_params=pltpu.CompilerParams(dimension_semantics=("arbitrary",), vmem_limit_bytes=28 << 20),
-    )(info, psi, inc, far, power_a, power_b, patterns, mine, other, dft, kern)
+    outs = [shape(PAIR, F32), shape(ALL_BLOCKS, BF16)]
+    arrays = [psi, inc, far, power_a, power_b, patterns, mine, other, *consts]
+    return whole(backward_kernel, outs, info, arrays, [VMEM(PAIR, BF16), MATRIX, MATRIX], 24)
 
 
 def swap(value, axis):
@@ -433,11 +395,12 @@
     ids = row[0, : NYLX * NYH]
 
     own = lax.dynamic_index_in_dim(object_tiles[0], core, 0, keepdims=False).astype(BF16)
-    above_row = from_tile(jnp.pad(offsets.reshape(1, 4), ((0, 0), (0, 124))), -TGX)
-    above_col = lax.dynamic_slice(above_row, (0, 2 + slot), (1, 1)).reshape(1, 1, 1)
-    above_left = columns >= above_col
+    above = from_tile(offsets, -TGX)
     east = from_tile(own, 1)
-    south = from_tile(jnp.where(above_left, own, east), TGX)
+    chosen = whole(
+        choose_kernel, shape((2, W, W), BF16), above.reshape(4), [own, east]
+    )
+    south = from_tile(chosen, TGX)
 
     rows = probe.astype(BF16).reshape(SCANS * 16, W)
     banded = spread(rows, "z", NZ).reshape(NZ, SCANS, 16, W)
@@ -467,7 +430,9 @@
     by_scan = plain(scan_sum_kernel, shape((NZ, SCANS * 16, W), BF16), received, row)
     part_grad = kept + from_tile(right.astype(BF16), -1).astype(F32)
     summed = exchange(by_scan, "z")
-    probe_grad, packed = plain(grad_sum_kernel, [shape((SCANS * 16, W), F32), shape((1, 128), F32)], summed, part_grad)
+    probe_grad, packed = plain(
+        grad_sum_kernel, [shape((SCANS * 16, W), F32), shape((1, 128), F32)], summed, part_grad
+    )
     packed = spread(packed, ("z",) + PLANE + ("c",), 4 * TILES)
     twin_part = swap(part_grad, "yh")
     layer_grad = jnp.stack(

time: 149 us -> 146 us (0.980)
  waiting for transfers between devices: 50.9 us -> 46.7 us
    pallas_call x3 -> x6, Pallas kernels: 3.27 us -> 16.8 us  [whole(): pl.pallas_call(kernel, grid_spec=pltpu.PrefetchScalarGridSpec(num_scalar_...]
    pallas_call x2 -> x0, Pallas kernels: 13 us -> none  [the longest x1 7.29 us: backward(): pl.pallas_call(backward_kernel, grid_spec=pltpu.PrefetchScalarGridSpec(nu...]
    ppermute x7, waiting for transfers between devices: 15.4 us -> 11.4 us  [swap(): return lax.ppermute(value, axis, [(0, 1), (1, 0)])]
  transfers between devices with their start and end apart: 20 -> 20, of which waited for: 12 -> 11; matrix products, arithmetic and copies ran while one was open for 4% -> 4% of each run, Pallas kernels for 2% -> 3%
where the time goes in v5:
time: 146 us; the launch traced here: 145 us
  starting transfers between devices  66.4 us (45%)
  waiting for transfers between devices  46.7 us (32%)
  Pallas kernels  21.5 us (15%)
  local copies, waits for them, and re-layouts  4.29 us (3%)
  between operations  3.1 us (2%)
  other arithmetic  2.64 us (2%)
    all_to_all x5, starting transfers between devices, exchange(): return lax.all_to_all(value, axes, 0, 0, tiled=True)  36.1 us
    all_to_all x5, waiting for transfers between devices, exchange(): return lax.all_to_all(value, axes, 0, 0, tiled=True)  21.7 us
    pallas_call x6, Pallas kernels, whole(): pl.pallas_call(kernel, grid_spec=pltpu.PrefetchScalarGridSpec(num_scalar_...  16.8 us
    ppermute x7, starting transfers between devices, swap(): return lax.ppermute(value, axis, [(0, 1), (1, 0)])  14.6 us
    ppermute x5, waiting for transfers between devices, from_tile(): return lax.ppermute(value, TILE_AXES, route)  13.6 us
    ppermute x7, waiting for transfers between devices, swap(): return lax.ppermute(value, axis, [(0, 1), (1, 0)])  11.4 us
    ppermute x5, starting transfers between devices, from_tile(): return lax.ppermute(value, TILE_AXES, route)  11.1 us
    ppermute x3, starting transfers between devices, update(): rows.append(lax.ppermute(row, 'x', [((x + d) % NX, x) for x in range(NX)]))  4.58 us
  transfers between devices with their start and end apart: 20, of which 11 were waited for; matrix products, arithmetic and copies ran while one was open for 4% of the time, Pallas kernels for 3%

profile of v5, /device:TPU:1, one launch (start us, length us, event | category | flops | bytes accessed | tf_op | source)
XLA Modules:
  0.0 144.7 jit_solution(12072815387383056190)
XLA Ops:
  0.7 0.6 copy-done.9
  1.3 0.1 dynamic_update_slice.5
  1.4 3.5 %collective-permute-start = (s32[1,128]{1,0:T(1,128)S(1)}, s32[1,128]{1,0:T(1,128)S(1)}, u32[]{:S(2)}, u32[]{:S(2)}) collective-permute-start(s32[1,128]{1,0:T(1,128)S(1)} %dynamic_update_slice.5), channel_id=1, source_target_pairs={{4,0},{8,4},{12,8},{0,12},{5,1},{9,5},{13,9},{1,13},{6,2},{10,6},{... | collective-permute-start | bytes 1544 | tf_op jit(solution)/shard_map/ppermute | solution.py:392
  4.8 0.5 collective-permute-start.1
  5.3 0.6 collective-permute-start.2
  6.0 0.9 convert_element_type.31
  6.8 0.7 broadcast_in_dim.40
  7.5 8.2 %all-to-all-start = ((bf16[8,64,256]{2,1,0:T(8,128)(2,1)}), bf16[8,64,256]{2,1,0:T(8,128)(2,1)S(1)}, u32[]{:S(2)}, u32[]{:S(2)}) async-start(bf16[8,64,256]{2,1,0:T(8,128)(2,1)} %broadcast_in_dim.40), calls=%async_computation | async-start | bytes 524288 | tf_op jit(solution)/shard_map/all_to_all | solution.py:350
  15.7 0.0 collective-permute-done
  15.7 0.1 fusion.7
  15.8 0.1 add.47
  15.9 0.0 collective-permute-done.1
  15.9 0.0 collective-permute-done.2
  15.9 1.5 %collective-permute-start.3 = (s32[1,128]{1,0:T(1,128)S(1)}, s32[1,128]{1,0:T(1,128)S(1)}, u32[]{:S(2)}, u32[]{:S(2)}) collective-permute-start(s32[1,128]{1,0:T(1,128)S(1)} %add_add_fusion), channel_id=1, source_target_pairs={{0,16},{16,0},{1,17},{17,1},{2,18},{18,2},{3,19},{19,3},{4,20},{20... | collective-permute-start | bytes 1544 | tf_op jit(solution)/shard_map/ppermute | solution.py:341
  17.4 1.1 fusion.own
  18.5 1.3 collective-permute-start.4
  19.8 0.0 collective-permute-done.3
  19.8 5.6 %all-to-all-done = bf16[8,64,256]{2,1,0:T(8,128)(2,1)S(1)} async-done(((bf16[8,64,256]{2,1,0:T(8,128)(2,1)}), bf16[8,64,256]{2,1,0:T(8,128)(2,1)S(1)}, u32[]{:S(2)}, u32[]{:S(2)}) %all-to-all-start) | async-done | bytes 262176 | tf_op jit(solution)/shard_map/all_to_all | solution.py:350
  25.4 1.6 %shard_map.156 = bf16[16,8,16,256]{3,2,1,0:T(8,128)(2,1)} custom-call(s32[16]{0:T(128)S(1)} %slice_bitcast_fusion.2.ids, bf16[8,4,16,256]{3,2,1,0:T(8,128)(2,1)S(1)} %bitcast.44), custom_call_target="tpu_custom_call" | custom-call | tf_op jit(solution)/shard_map/pallas_call | solution.py:308
  27.0 6.5 %all-to-all-start.1 = ((bf16[16,8,16,256]{3,2,1,0:T(8,128)(2,1)}), bf16[16,8,16,256]{3,2,1,0:T(8,128)(2,1)S(1)}, u32[]{:S(2)}, u32[]{:S(2)}) async-start(bf16[16,8,16,256]{3,2,1,0:T(8,128)(2,1)} %shard_map.156), calls=%async_computation.1 | async-start | bytes 2097152 | tf_op jit(solution)/shard_map/all_to_all | solution.py:350
  33.5 1.7 %collective-permute-start.5 = (s32[2,2]{1,0:T(2,128)S(1)}, s32[2,2]{1,0:T(2,128)S(1)}, u32[]{:S(2)}, u32[]{:S(2)}) collective-permute-start(s32[2,2]{1,0:T(2,128)S(1)} %copy-done.8), channel_id=1, source_target_pairs={{0,32},{4,36},{8,40},{12,44},{16,48},{20,52},{24,56},{28,60},{32,6... | collective-permute-start | bytes 56 | tf_op jit(solution)/shard_map/ppermute | solution.py:346
  35.2 0.7 collective-permute-done.5
  35.9 0.1 reshape.49.above
  36.0 0.0 collective-permute-done.4.east
  36.0 0.6 shard_map.157
  36.6 1.3 collective-permute-start.6
  37.9 0.2 fusion.8
  38.8 0.1 concatenate.3.info
  38.9 0.5 fusion.9
  39.4 1.3 iota_compare_fusion
  40.7 3.6 %collective-permute-done.6 = bf16[2,256,256]{2,1,0:T(8,128)(2,1)S(1)} collective-permute-done((bf16[2,256,256]{2,1,0:T(8,128)(2,1)S(1)}, bf16[2,256,256]{2,1,0:T(8,128)(2,1)S(1)}, u32[]{:S(2)}, u32[]{:S(2)}) %collective-permute-start.6) | collective-permute-done | bytes 262176 | tf_op jit(solution)/shard_map/ppermute | solution.py:346
  44.3 0.1 select_select_fusion.mixed
  44.4 0.0 copy-start.1
  44.4 0.8 shard_map.158.mine.refs_6_
  45.2 5.5 %collective-permute-start.7 = (bf16[2,256,256]{2,1,0:T(8,128)(2,1)S(1)}, bf16[2,256,256]{2,1,0:T(8,128)(2,1)S(1)}, u32[]{:S(2)}, u32[]{:S(2)}) collective-permute-start(bf16[2,256,256]{2,1,0:T(8,128)(2,1)S(1)} %shard_map.158.mine.refs_6_), channel_id=1, source_target_pairs={{0,1},{1,0},{2,3},{3,2},{4,5},{5,4},{6,7},{7,6},{8,9},{9,8},{10,11... | collective-permute-start | bytes 786440 | tf_op jit(solution)/shard_map/ppermute | solution.py:341
  50.6 1.2 collective-permute-done.7.other.refs_7_
  51.8 5.4 %shard_map.159 = (bf16[4,2,256,256]{3,2,1,0:T(8,128)(2,1)S(1)}, bf16[4,2,256,256]{3,2,1,0:T(8,128)(2,1)S(1)}, bf16[4,2,256,256]{3,2,1,0:T(8,128)(2,1)S(1)}, f32[256,256]{1,0:T(8,128)S(1)}) custom-call(s32[7]{0:T(128)S(1)} %concatenate.3.info, bf16[8,2,8,16,256]{4,3,2,1,0:T(8,128)(2,1)S(1)} %bitcast.43, bf16[2,256,256]{2,1,0:T(8,128)(2,1)S(1)} %shard_map.158.mine.refs_6_, ...), custom_call_target="tpu_custom_call" | custom-call | tf_op jit(solution)/shard_map/pallas_call | solution.py:308
  57.3 0.5 collective-permute-start.8
  57.7 1.2 collective-permute-done.8.refs_4_
  58.9 7.5 %shard_map.160 = (f32[2,2,256,256]{3,2,1,0:T(8,128)S(1)}, bf16[8,2,8,16,256]{4,3,2,1,0:T(8,128)(2,1)}) custom-call(s32[7]{0:T(128)S(1)} %concatenate.3.info, bf16[4,2,256,256]{3,2,1,0:T(8,128)(2,1)S(1)} %get-tuple-element.15.refs_0_, bf16[4,2,256,256]{3,2,1,0:T(8,128)(2,1)S(1)} %get-tuple-element.16.refs_1_, ...), custom_call_target="tpu_custom_call" | custom-call | tf_op jit(solution)/shard_map/pallas_call | solution.py:308
  66.4 0.5 collective-permute-start.9
  66.8 1.2 collective-permute-done.9
  68.0 0.1 bitcast_add_fusion
  68.1 3.4 %collective-permute-start.10 = (bf16[256,256]{1,0:T(8,128)(2,1)S(1)}, bf16[256,256]{1,0:T(8,128)(2,1)S(1)}, u32[]{:S(2)}, u32[]{:S(2)}) collective-permute-start(bf16[256,256]{1,0:T(8,128)(2,1)S(1)} %fusion.6), channel_id=1, source_target_pairs={{0,2},{2,0},{1,3},{3,1},{4,6},{6,4},{5,7},{7,5},{8,10},{10,8},{9,1... | collective-permute-start | bytes 393224 | tf_op jit(solution)/shard_map/ppermute | solution.py:341
  71.6 3.4 %collective-permute-done.10.other = bf16[256,256]{1,0:T(8,128)(2,1)S(1)} collective-permute-done((bf16[256,256]{1,0:T(8,128)(2,1)S(1)}, bf16[256,256]{1,0:T(8,128)(2,1)S(1)}, u32[]{:S(2)}, u32[]{:S(2)}) %collective-permute-start.10) | collective-permute-done | bytes 131104 | tf_op jit(solution)/shard_map/ppermute | solution.py:341
  75.0 0.9 shard_map.162
  75.9 3.6 %collective-permute-start.11 = (bf16[2,256,256]{2,1,0:T(8,128)(2,1)S(1)}, bf16[2,256,256]{2,1,0:T(8,128)(2,1)S(1)}, u32[]{:S(2)}, u32[]{:S(2)}) collective-permute-start(bf16[2,256,256]{2,1,0:T(8,128)(2,1)S(1)} %get-tuple-element.22), channel_id=1, source_target_pairs={{0,32},{4,36},{8,40},{12,44},{16,48},{20,52},{24,56},{28,60},{32,6... | collective-permute-start | bytes 786440 | tf_op jit(solution)/shard_map/ppermute | solution.py:346
  79.5 6.6 %all-to-all-start.2 = ((bf16[16,8,16,256]{3,2,1,0:T(8,128)(2,1)}), bf16[16,8,16,256]{3,2,1,0:T(8,128)(2,1)S(1)}, u32[]{:S(2)}, u32[]{:S(2)}) async-start(bf16[16,8,16,256]{3,2,1,0:T(8,128)(2,1)} %bitcast.11), calls=%async_computation.2 | async-start | bytes 2097152 | tf_op jit(solution)/shard_map/all_to_all | solution.py:350
  86.2 3.3 %collective-permute-start.12 = (bf16[256,256]{1,0:T(8,128)(2,1)S(1)}, bf16[256,256]{1,0:T(8,128)(2,1)S(1)}, u32[]{:S(2)}, u32[]{:S(2)}) collective-permute-start(bf16[256,256]{1,0:T(8,128)(2,1)S(1)} %fusion.3), channel_id=1, source_target_pairs={{0,4},{4,8},{8,12},{12,16},{16,20},{20,24},{24,28},{28,32},{32,36}... | collective-permute-start | bytes 393224 | tf_op jit(solution)/shard_map/ppermute | solution.py:346
  89.5 9.3 %collective-permute-done.12 = bf16[256,256]{1,0:T(8,128)(2,1)S(1)} collective-permute-done((bf16[256,256]{1,0:T(8,128)(2,1)S(1)}, bf16[256,256]{1,0:T(8,128)(2,1)S(1)}, u32[]{:S(2)}, u32[]{:S(2)}) %collective-permute-start.12) | collective-permute-done | bytes 131104 | tf_op jit(solution)/shard_map/ppermute | solution.py:346
  98.8 2.8 %collective-permute-start.13 = (f32[256,256]{1,0:T(8,128)S(1)}, f32[256,256]{1,0:T(8,128)S(1)}, u32[]{:S(2)}, u32[]{:S(2)}) collective-permute-start(f32[256,256]{1,0:T(8,128)S(1)} %fusion.5.layer), channel_id=1, source_target_pairs={{0,2},{2,0},{1,3},{3,1},{4,6},{6,4},{5,7},{7,5},{8,10},{10,8},{9,1... | collective-permute-start | bytes 786440 | tf_op jit(solution)/shard_map/ppermute | solution.py:341
  101.6 1.1 shard_map.161
  102.7 5.8 %all-to-all-start.3 = ((bf16[8,64,256]{2,1,0:T(8,128)(2,1)}), bf16[8,64,256]{2,1,0:T(8,128)(2,1)S(1)}, u32[]{:S(2)}, u32[]{:S(2)}) async-start(bf16[8,64,256]{2,1,0:T(8,128)(2,1)} %shard_map.161), calls=%async_computation.3 | async-start | bytes 524288 | tf_op jit(solution)/shard_map/all_to_all | solution.py:350
  108.5 4.5 %collective-permute-done.13 = f32[256,256]{1,0:T(8,128)S(1)} collective-permute-done((f32[256,256]{1,0:T(8,128)S(1)}, f32[256,256]{1,0:T(8,128)S(1)}, u32[]{:S(2)}, u32[]{:S(2)}) %collective-permute-start.13) | collective-permute-done | bytes 262176 | tf_op jit(solution)/shard_map/ppermute | solution.py:341
  113.1 0.0 copy-start.2
  113.1 0.6 collective-permute-start.14
  113.7 4.4 %all-to-all-done.3.src = bf16[8,64,256]{2,1,0:T(8,128)(2,1)S(1)} async-done(((bf16[8,64,256]{2,1,0:T(8,128)(2,1)}), bf16[8,64,256]{2,1,0:T(8,128)(2,1)S(1)}, u32[]{:S(2)}, u32[]{:S(2)}) %all-to-all-start.3) | async-done | bytes 262176 | tf_op jit(solution)/shard_map/all_to_all | solution.py:350
  118.1 0.2 shard_map.163
  118.3 0.7 broadcast_in_dim.44
  119.0 9.0 %all-to-all-start.4 = ((f32[256,1,128]{2,1,0:T(1,128)}), f32[256,1,128]{2,1,0:T(1,128)S(1)}, u32[]{:S(2)}, u32[]{:S(2)}) async-start(f32[256,1,128]{2,1,0:T(1,128)} %broadcast_in_dim.44), calls=%async_computation.4 | async-start | bytes 262144 | tf_op jit(solution)/shard_map/all_to_all | solution.py:350
  129.3 0.0 copy-start.7
  129.3 0.0 collective-permute-done.14.other
  129.3 11.8 %all-to-all-done.4.packed = f32[256,1,128]{2,1,0:T(1,128)S(1)} async-done(((f32[256,1,128]{2,1,0:T(1,128)}), f32[256,1,128]{2,1,0:T(1,128)S(1)}, u32[]{:S(2)}, u32[]{:S(2)}) %all-to-all-start.4) | async-done | bytes 131104 | tf_op jit(solution)/shard_map/all_to_all | solution.py:350
  141.1 3.4 %shard_map.164 = (f32[1,2,2,256,256]{4,3,2,1,0:T(8,128)}, f32[1,2,2,256,256]{4,3,2,1,0:T(8,128)}, f32[4,2,2,4,256]{4,3,2,1,0:T(4,128)}, f32[4,2,2,4,256]{4,3,2,1,0:T(4,128)}) custom-call(s32[7]{0:T(128)S(1)} %concatenate.3.info, s32[2]{0:T(128)S(1)} %copy-done.7, f32[1]{0:T(128)S(6)} %copy.20.object_norm, f32[1]{0:T(128)S(6)} %copy.21.probe_norm, ...), custom_call_target="tpu_custom_call" | custom-call | tf_op jit(solution)/shard_map/pallas_call | solution.py:270
  (32 shorter events, 0.3 us)
Async XLA Ops:
  0.6 0.7 copy-start.9
  1.4 14.4 %collective-permute-start = (s32[1,128]{1,0:T(1,128)S(1)}, s32[1,128]{1,0:T(1,128)S(1)}, u32[]{:S(2)}, u32[]{:S(2)}) collective-permute-start(s32[1,128]{1,0:T(1,128)S(1)} %dynamic_update_slice.5), channel_id=1, source_target_pairs={{4,0},{8,4},{12,8},{0,12},{5,1},{9,5},{13,9},{1,13},{6,2},{10,6},{... | collective-permute-start | bytes 1544 | tf_op jit(solution)/shard_map/ppermute | solution.py:392
  4.8 11.1 %collective-permute-start.1 = (s32[1,128]{1,0:T(1,128)S(1)}, s32[1,128]{1,0:T(1,128)S(1)}, u32[]{:S(2)}, u32[]{:S(2)}) collective-permute-start(s32[1,128]{1,0:T(1,128)S(1)} %dynamic_update_slice.5), channel_id=1, source_target_pairs={{8,0},{12,4},{0,8},{4,12},{9,1},{13,5},{1,9},{5,13},{10,2},{14,6},... | collective-permute-start | bytes 1544 | tf_op jit(solution)/shard_map/ppermute | solution.py:392
  5.3 10.6 %collective-permute-start.2 = (s32[1,128]{1,0:T(1,128)S(1)}, s32[1,128]{1,0:T(1,128)S(1)}, u32[]{:S(2)}, u32[]{:S(2)}) collective-permute-start(s32[1,128]{1,0:T(1,128)S(1)} %dynamic_update_slice.5), channel_id=1, source_target_pairs={{12,0},{0,4},{4,8},{8,12},{13,1},{1,5},{5,9},{9,13},{14,2},{2,6},{... | collective-permute-start | bytes 1544 | tf_op jit(solution)/shard_map/ppermute | solution.py:392
  7.5 17.8 %all-to-all-start = ((bf16[8,64,256]{2,1,0:T(8,128)(2,1)}), bf16[8,64,256]{2,1,0:T(8,128)(2,1)S(1)}, u32[]{:S(2)}, u32[]{:S(2)}) async-start(bf16[8,64,256]{2,1,0:T(8,128)(2,1)} %broadcast_in_dim.40), calls=%async_computation | async-start | bytes 524288 | tf_op jit(solution)/shard_map/all_to_all | solution.py:350
  15.9 3.9 %collective-permute-start.3 = (s32[1,128]{1,0:T(1,128)S(1)}, s32[1,128]{1,0:T(1,128)S(1)}, u32[]{:S(2)}, u32[]{:S(2)}) collective-permute-start(s32[1,128]{1,0:T(1,128)S(1)} %add_add_fusion), channel_id=1, source_target_pairs={{0,16},{16,0},{1,17},{17,1},{2,18},{18,2},{3,19},{19,3},{4,20},{20... | collective-permute-start | bytes 1544 | tf_op jit(solution)/shard_map/ppermute | solution.py:341
  18.5 17.5 %collective-permute-start.4 = (bf16[2,256,256]{2,1,0:T(8,128)(2,1)S(1)}, bf16[2,256,256]{2,1,0:T(8,128)(2,1)S(1)}, u32[]{:S(2)}, u32[]{:S(2)}) collective-permute-start(bf16[2,256,256]{2,1,0:T(8,128)(2,1)S(1)} %fusion.own), channel_id=1, source_target_pairs={{4,0},{8,4},{12,8},{16,12},{20,16},{24,20},{28,24},{32,28},{36,32}... | collective-permute-start | bytes 786440 | tf_op jit(solution)/shard_map/ppermute | solution.py:346
  27.0 6.5 %copy-start.8 = (s32[2,2]{1,0:T(2,128)S(1)}, s32[2,2]{1,0:T(2,128)}, u32[]{:S(2)}) copy-start(s32[2,2]{1,0:T(2,128)} %param.18) | copy-start | bytes 52
  27.0 17.3 %copy-start = (f32[1,2,2,256,256]{4,3,2,1,0:T(8,128)S(1)}, f32[1,2,2,256,256]{4,3,2,1,0:T(8,128)}, u32[]{:S(2)}) copy-start(f32[1,2,2,256,256]{4,3,2,1,0:T(8,128)} %tiles.1) | copy-start | bytes 3145732
  27.0 24.8 %all-to-all-start.1 = ((bf16[16,8,16,256]{3,2,1,0:T(8,128)(2,1)}), bf16[16,8,16,256]{3,2,1,0:T(8,128)(2,1)S(1)}, u32[]{:S(2)}, u32[]{:S(2)}) async-start(bf16[16,8,16,256]{3,2,1,0:T(8,128)(2,1)} %shard_map.156), calls=%async_computation.1 | async-start | bytes 2097152 | tf_op jit(solution)/shard_map/all_to_all | solution.py:350
  33.5 2.4 %collective-permute-start.5 = (s32[2,2]{1,0:T(2,128)S(1)}, s32[2,2]{1,0:T(2,128)S(1)}, u32[]{:S(2)}, u32[]{:S(2)}) collective-permute-start(s32[2,2]{1,0:T(2,128)S(1)} %copy-done.8), channel_id=1, source_target_pairs={{0,32},{4,36},{8,40},{12,44},{16,48},{20,52},{24,56},{28,60},{32,6... | collective-permute-start | bytes 56 | tf_op jit(solution)/shard_map/ppermute | solution.py:346
  36.6 7.7 %collective-permute-start.6 = (bf16[2,256,256]{2,1,0:T(8,128)(2,1)S(1)}, bf16[2,256,256]{2,1,0:T(8,128)(2,1)S(1)}, u32[]{:S(2)}, u32[]{:S(2)}) collective-permute-start(bf16[2,256,256]{2,1,0:T(8,128)(2,1)S(1)} %shard_map.157), channel_id=1, source_target_pairs={{32,0},{36,4},{40,8},{44,12},{48,16},{52,20},{56,24},{60,28},{64,3... | collective-permute-start | bytes 786440 | tf_op jit(solution)/shard_map/ppermute | solution.py:346
  44.3 7.5 %copy-start.3 = (bf16[2,256,256]{2,1,0:T(8,128)(2,1)S(1)}, bf16[2,256,256]{2,1,0:T(8,128)(2,1)}, u32[]{:S(2)}) copy-start(bf16[2,256,256]{2,1,0:T(8,128)(2,1)} %constant.43.clone.dft.refs_8_) | copy-start | bytes 786436
  44.4 7.4 %copy-start.1 = (f32[2,256,256]{2,1,0:T(8,128)S(1)}, f32[2,256,256]{2,1,0:T(8,128)}, u32[]{:S(2)}) copy-start(f32[2,256,256]{2,1,0:T(8,128)} %constant.44.clone.kern.refs_9_) | copy-start | bytes 1572868
  45.2 6.6 %collective-permute-start.7 = (bf16[2,256,256]{2,1,0:T(8,128)(2,1)S(1)}, bf16[2,256,256]{2,1,0:T(8,128)(2,1)S(1)}, u32[]{:S(2)}, u32[]{:S(2)}) collective-permute-start(bf16[2,256,256]{2,1,0:T(8,128)(2,1)S(1)} %shard_map.158.mine.refs_6_), channel_id=1, source_target_pairs={{0,1},{1,0},{2,3},{3,2},{4,5},{5,4},{6,7},{7,6},{8,9},{9,8},{10,11... | collective-permute-start | bytes 786440 | tf_op jit(solution)/shard_map/ppermute | solution.py:341
  51.8 7.1 %copy-start.4 = (f32[2,256,256]{2,1,0:T(8,128)S(1)}, f32[2,256,256]{2,1,0:T(8,128)}, u32[]{:S(2)}) copy-start(f32[2,256,256]{2,1,0:T(8,128)} %refs_5_.1) | copy-start | bytes 1572868
  57.3 1.6 %collective-permute-start.8 = (f32[256,256]{1,0:T(8,128)S(1)}, f32[256,256]{1,0:T(8,128)S(1)}, u32[]{:S(2)}, u32[]{:S(2)}) collective-permute-start(f32[256,256]{1,0:T(8,128)S(1)} %get-tuple-element.18.refs_3_), channel_id=1, source_target_pairs={{0,1},{1,0},{2,3},{3,2},{4,5},{5,4},{6,7},{7,6},{8,9},{9,8},{10,11... | collective-permute-start | bytes 786440 | tf_op jit(solution)/shard_map/ppermute | solution.py:341
  66.4 1.6 %collective-permute-start.9 = (bf16[2,256,256]{2,1,0:T(8,128)(2,1)S(1)}, bf16[2,256,256]{2,1,0:T(8,128)(2,1)S(1)}, u32[]{:S(2)}, u32[]{:S(2)}) collective-permute-start(bf16[2,256,256]{2,1,0:T(8,128)(2,1)S(1)} %fusion.1), channel_id=1, source_target_pairs={{0,1},{1,0},{2,3},{3,2},{4,5},{5,4},{6,7},{7,6},{8,9},{9,8},{10,11... | collective-permute-start | bytes 786440 | tf_op jit(solution)/shard_map/ppermute | solution.py:341
  68.1 6.9 %collective-permute-start.10 = (bf16[256,256]{1,0:T(8,128)(2,1)S(1)}, bf16[256,256]{1,0:T(8,128)(2,1)S(1)}, u32[]{:S(2)}, u32[]{:S(2)}) collective-permute-start(bf16[256,256]{1,0:T(8,128)(2,1)S(1)} %fusion.6), channel_id=1, source_target_pairs={{0,2},{2,0},{1,3},{3,1},{4,6},{6,4},{5,7},{7,5},{8,10},{10,8},{9,1... | collective-permute-start | bytes 393224 | tf_op jit(solution)/shard_map/ppermute | solution.py:341
  75.9 10.2 %collective-permute-start.11 = (bf16[2,256,256]{2,1,0:T(8,128)(2,1)S(1)}, bf16[2,256,256]{2,1,0:T(8,128)(2,1)S(1)}, u32[]{:S(2)}, u32[]{:S(2)}) collective-permute-start(bf16[2,256,256]{2,1,0:T(8,128)(2,1)S(1)} %get-tuple-element.22), channel_id=1, source_target_pairs={{0,32},{4,36},{8,40},{12,44},{16,48},{20,52},{24,56},{28,60},{32,6... | collective-permute-start | bytes 786440 | tf_op jit(solution)/shard_map/ppermute | solution.py:346
  79.5 22.1 %all-to-all-start.2 = ((bf16[16,8,16,256]{3,2,1,0:T(8,128)(2,1)}), bf16[16,8,16,256]{3,2,1,0:T(8,128)(2,1)S(1)}, u32[]{:S(2)}, u32[]{:S(2)}) async-start(bf16[16,8,16,256]{3,2,1,0:T(8,128)(2,1)} %bitcast.11), calls=%async_computation.2 | async-start | bytes 2097152 | tf_op jit(solution)/shard_map/all_to_all | solution.py:350
  86.2 12.6 %collective-permute-start.12 = (bf16[256,256]{1,0:T(8,128)(2,1)S(1)}, bf16[256,256]{1,0:T(8,128)(2,1)S(1)}, u32[]{:S(2)}, u32[]{:S(2)}) collective-permute-start(bf16[256,256]{1,0:T(8,128)(2,1)S(1)} %fusion.3), channel_id=1, source_target_pairs={{0,4},{4,8},{8,12},{12,16},{16,20},{20,24},{24,28},{28,32},{32,36}... | collective-permute-start | bytes 393224 | tf_op jit(solution)/shard_map/ppermute | solution.py:346
  98.8 14.2 %collective-permute-start.13 = (f32[256,256]{1,0:T(8,128)S(1)}, f32[256,256]{1,0:T(8,128)S(1)}, u32[]{:S(2)}, u32[]{:S(2)}) collective-permute-start(f32[256,256]{1,0:T(8,128)S(1)} %fusion.5.layer), channel_id=1, source_target_pairs={{0,2},{2,0},{1,3},{3,1},{4,6},{6,4},{5,7},{7,5},{8,10},{10,8},{9,1... | collective-permute-start | bytes 786440 | tf_op jit(solution)/shard_map/ppermute | solution.py:341
  102.7 15.4 %all-to-all-start.3 = ((bf16[8,64,256]{2,1,0:T(8,128)(2,1)}), bf16[8,64,256]{2,1,0:T(8,128)(2,1)S(1)}, u32[]{:S(2)}, u32[]{:S(2)}) async-start(bf16[8,64,256]{2,1,0:T(8,128)(2,1)} %shard_map.161), calls=%async_computation.3 | async-start | bytes 524288 | tf_op jit(solution)/shard_map/all_to_all | solution.py:350
  113.1 28.1 %copy-start.2 = (f32[1,2,2,256,256]{4,3,2,1,0:T(8,128)S(1)}, f32[1,2,2,256,256]{4,3,2,1,0:T(8,128)}, u32[]{:S(2)}) copy-start(f32[1,2,2,256,256]{4,3,2,1,0:T(8,128)} %before.1) | copy-start | bytes 3145732
  113.1 16.2 %collective-permute-start.14 = (f32[2,256,256]{2,1,0:T(8,128)S(1)}, f32[2,256,256]{2,1,0:T(8,128)}, u32[]{:S(2)}, u32[]{:S(2)}) collective-permute-start(f32[2,256,256]{2,1,0:T(8,128)S(1)} %pad_maximum_fusion.layer), channel_id=1, source_target_pairs={{0,1},{1,0},{2,3},{3,2},{4,5},{5,4},{6,7},{7,6},{8,9},{9,8},{10,11... | collective-permute-start | bytes 1572872 | tf_op jit(solution)/shard_map/ppermute | solution.py:341
  119.0 22.1 %copy-start.5 = (f32[4,2,2,4,256]{4,3,2,1,0:T(4,128)S(1)}, f32[4,2,2,4,256]{4,3,2,1,0:T(4,128)}, u32[]{:S(2)}) copy-start(f32[4,2,2,4,256]{4,3,2,1,0:T(4,128)} %probe.1) | copy-start | bytes 196612
  119.0 22.1 %copy-start.6 = (f32[4,2,2,4,256]{4,3,2,1,0:T(4,128)S(1)}, f32[4,2,2,4,256]{4,3,2,1,0:T(4,128)}, u32[]{:S(2)}) copy-start(f32[4,2,2,4,256]{4,3,2,1,0:T(4,128)} %probe_before.1) | copy-start | bytes 196612
  119.0 22.1 %all-to-all-start.4 = ((f32[256,1,128]{2,1,0:T(1,128)}), f32[256,1,128]{2,1,0:T(1,128)S(1)}, u32[]{:S(2)}, u32[]{:S(2)}) async-start(f32[256,1,128]{2,1,0:T(1,128)} %broadcast_in_dim.44), calls=%async_computation.4 | async-start | bytes 262144 | tf_op jit(solution)/shard_map/all_to_all | solution.py:350
  129.3 11.8 %copy-start.7 = (s32[2]{0:T(128)S(1)}, s32[2]{0:T(128)}, u32[]{:S(2)}) copy-start(s32[2]{0:T(128)} %steps.1) | copy-start | bytes 28

commit v6 on v5

--- a/solution.py
+++ b/solution.py
@@ -115,10 +115,9 @@
     first = info[2] == 0
     fill(dft, plus, minus)
     order = placing(0)
-    power[...] = jnp.zeros_like(power)
-
-    def pair(g, carry):
-        psi, inc, far = (ref.at[pl.ds(2 * g, 2)] for ref in (all_psi, all_inc, all_far))
+
+    def pair(g):
+        psi, inc, far = (ref.at[2 * g : 2 * g + 2] for ref in (all_psi, all_inc, all_far))
         for z in range(NZ):
             piece = blocks[:, g, z].reshape(128, W)
             placed = mm(order, piece).astype(BF16)
@@ -135,15 +134,15 @@
         for i in pairs:
             inc[i, 0], inc[i, 1] = moved[i]
         waves = transform([times(*moved[i], *p1) for i in pairs], fwd, inv)
-        total = power[...]
+        total = power[...] if g else 0.0
         for i in pairs:
             far[i, 0], far[i, 1] = waves[i]
             f_re, f_im = waves[i][0].astype(F32), waves[i][1].astype(F32)
             total = total + (f_re * f_re + f_im * f_im)
         power[...] = total
-        return carry
-
-    lax.fori_loop(0, 2, pair, 0)
+
+    for g in range(2):
+        pair(g)
 
 
 def backward_kernel(info, *refs):
@@ -154,10 +153,9 @@
     fill(dft, plus, minus)
     used = info[4].astype(F32)
     back_order = placing(1)
-    terms[...] = jnp.zeros_like(terms)
-
-    def pair(g, carry):
-        psi, inc, far = (ref.at[pl.ds(2 * g, 2)] for ref in (all_psi, all_inc, all_far))
+
+    def pair(g):
+        psi, inc, far = (ref.at[2 * g : 2 * g + 2] for ref in (all_psi, all_inc, all_far))
         fwd, inv = plus[...], minus[...]
         p0 = [jnp.where(first, mine[ri], other[ri]) for ri in range(2)]
         p1 = [jnp.where(first, other[ri], mine[ri]) for ri in range(2)]
@@ -174,15 +172,16 @@
         for layer, term in enumerate((term0, term1)):
             slot = core if layer == 0 else 1 - core
             for ri in range(2):
-                terms[slot, ri] += term[0][ri] + term[1][ri]
+                value = term[0][ri] + term[1][ri]
+                terms[slot, ri] = terms[slot, ri] + value if g else value
         for z in range(NZ):
             at = slice(z * BAND, (z + 1) * BAND)
             pieces = [scratch[i, ri, at] for i in range(2) for ri in range(2)]
             piece = mm(back_order, jnp.concatenate(pieces, axis=0)).astype(BF16)
             out[:, g, z] = piece.reshape(NYLX, 16, W)
-        return carry
-
-    lax.fori_loop(0, 2, pair, 0)
+
+    for g in range(2):
+        pair(g)
 
 
 def place_kernel(info, own, other, kept, right, low):

time: 146 us -> 145 us (level)
  no operation moved by 1% of the time
where the time goes in v6:
time: 145 us; the launch traced here: 144 us
  starting transfers between devices  66.5 us (46%)
  waiting for transfers between devices  46.7 us (32%)
  Pallas kernels  20.9 us (14%)
  local copies, waits for them, and re-layouts  4.29 us (3%)
  between operations  3.1 us (2%)
  other arithmetic  2.64 us (2%)
    all_to_all x5, starting transfers between devices, exchange(): return lax.all_to_all(value, axes, 0, 0, tiled=True)  36.1 us
    all_to_all x5, waiting for transfers between devices, exchange(): return lax.all_to_all(value, axes, 0, 0, tiled=True)  21.7 us
    pallas_call x6, Pallas kernels, whole(): pl.pallas_call(kernel, grid_spec=pltpu.PrefetchScalarGridSpec(num_scalar_...  16.2 us
    ppermute x7, starting transfers between devices, swap(): return lax.ppermute(value, axis, [(0, 1), (1, 0)])  14.7 us
    ppermute x5, waiting for transfers between devices, from_tile(): return lax.ppermute(value, TILE_AXES, route)  13.6 us
    ppermute x7, waiting for transfers between devices, swap(): return lax.ppermute(value, axis, [(0, 1), (1, 0)])  11.4 us
    ppermute x5, starting transfers between devices, from_tile(): return lax.ppermute(value, TILE_AXES, route)  11.2 us
    ppermute x3, starting transfers between devices, update(): rows.append(lax.ppermute(row, 'x', [((x + d) % NX, x) for x in range(NX)]))  4.58 us
  transfers between devices with their start and end apart: 20, of which 11 were waited for; matrix products, arithmetic and copies ran while one was open for 4% of the time, Pallas kernels for 3%

profile of v6, /device:TPU:1, one launch (start us, length us, event | category | flops | bytes accessed | tf_op | source)
XLA Modules:
  0.0 144.1 jit_solution(12862745321863002236)
XLA Ops:
  0.7 0.6 copy-done.9
  1.3 0.1 dynamic_update_slice.5
  1.4 3.5 %collective-permute-start = (s32[1,128]{1,0:T(1,128)S(1)}, s32[1,128]{1,0:T(1,128)S(1)}, u32[]{:S(2)}, u32[]{:S(2)}) collective-permute-start(s32[1,128]{1,0:T(1,128)S(1)} %dynamic_update_slice.5), channel_id=1, source_target_pairs={{4,0},{8,4},{12,8},{0,12},{5,1},{9,5},{13,9},{1,13},{6,2},{10,6},{... | collective-permute-start | bytes 1544 | tf_op jit(solution)/shard_map/ppermute | solution.py:391
  4.8 0.5 collective-permute-start.1
  5.3 0.6 collective-permute-start.2
  6.0 0.9 convert_element_type.31
  6.8 0.7 broadcast_in_dim.40
  7.5 8.2 %all-to-all-start = ((bf16[8,64,256]{2,1,0:T(8,128)(2,1)}), bf16[8,64,256]{2,1,0:T(8,128)(2,1)S(1)}, u32[]{:S(2)}, u32[]{:S(2)}) async-start(bf16[8,64,256]{2,1,0:T(8,128)(2,1)} %broadcast_in_dim.40), calls=%async_computation | async-start | bytes 524288 | tf_op jit(solution)/shard_map/all_to_all | solution.py:349
  15.7 0.0 collective-permute-done
  15.7 0.1 fusion.7
  15.8 0.1 add.47
  15.9 0.0 collective-permute-done.1
  15.9 0.0 collective-permute-done.2
  15.9 1.5 %collective-permute-start.3 = (s32[1,128]{1,0:T(1,128)S(1)}, s32[1,128]{1,0:T(1,128)S(1)}, u32[]{:S(2)}, u32[]{:S(2)}) collective-permute-start(s32[1,128]{1,0:T(1,128)S(1)} %add_add_fusion), channel_id=1, source_target_pairs={{0,16},{16,0},{1,17},{17,1},{2,18},{18,2},{3,19},{19,3},{4,20},{20... | collective-permute-start | bytes 1544 | tf_op jit(solution)/shard_map/ppermute | solution.py:340
  17.4 1.1 fusion.own
  18.5 1.3 collective-permute-start.4
  19.8 0.0 collective-permute-done.3
  19.8 5.6 %all-to-all-done = bf16[8,64,256]{2,1,0:T(8,128)(2,1)S(1)} async-done(((bf16[8,64,256]{2,1,0:T(8,128)(2,1)}), bf16[8,64,256]{2,1,0:T(8,128)(2,1)S(1)}, u32[]{:S(2)}, u32[]{:S(2)}) %all-to-all-start) | async-done | bytes 262176 | tf_op jit(solution)/shard_map/all_to_all | solution.py:349
  25.4 1.6 %shard_map.156 = bf16[16,8,16,256]{3,2,1,0:T(8,128)(2,1)} custom-call(s32[16]{0:T(128)S(1)} %slice_bitcast_fusion.2.ids, bf16[8,4,16,256]{3,2,1,0:T(8,128)(2,1)S(1)} %bitcast.44), custom_call_target="tpu_custom_call" | custom-call | tf_op jit(solution)/shard_map/pallas_call | solution.py:307
  27.0 6.5 %all-to-all-start.1 = ((bf16[16,8,16,256]{3,2,1,0:T(8,128)(2,1)}), bf16[16,8,16,256]{3,2,1,0:T(8,128)(2,1)S(1)}, u32[]{:S(2)}, u32[]{:S(2)}) async-start(bf16[16,8,16,256]{3,2,1,0:T(8,128)(2,1)} %shard_map.156), calls=%async_computation.1 | async-start | bytes 2097152 | tf_op jit(solution)/shard_map/all_to_all | solution.py:349
  33.5 1.7 %collective-permute-start.5 = (s32[2,2]{1,0:T(2,128)S(1)}, s32[2,2]{1,0:T(2,128)S(1)}, u32[]{:S(2)}, u32[]{:S(2)}) collective-permute-start(s32[2,2]{1,0:T(2,128)S(1)} %copy-done.8), channel_id=1, source_target_pairs={{0,32},{4,36},{8,40},{12,44},{16,48},{20,52},{24,56},{28,60},{32,6... | collective-permute-start | bytes 56 | tf_op jit(solution)/shard_map/ppermute | solution.py:345
  35.2 0.7 collective-permute-done.5
  35.9 0.1 reshape.49.above
  36.0 0.0 collective-permute-done.4.east
  36.0 0.6 shard_map.157
  36.6 1.3 collective-permute-start.6
  37.9 0.2 fusion.8
  38.8 0.1 concatenate.3.info
  38.9 0.5 fusion.9
  39.4 1.3 iota_compare_fusion
  40.7 3.6 %collective-permute-done.6 = bf16[2,256,256]{2,1,0:T(8,128)(2,1)S(1)} collective-permute-done((bf16[2,256,256]{2,1,0:T(8,128)(2,1)S(1)}, bf16[2,256,256]{2,1,0:T(8,128)(2,1)S(1)}, u32[]{:S(2)}, u32[]{:S(2)}) %collective-permute-start.6) | collective-permute-done | bytes 262176 | tf_op jit(solution)/shard_map/ppermute | solution.py:345
  44.3 0.1 select_select_fusion.mixed
  44.4 0.0 copy-start.1
  44.4 0.8 shard_map.158.mine.refs_6_
  45.2 5.5 %collective-permute-start.7 = (bf16[2,256,256]{2,1,0:T(8,128)(2,1)S(1)}, bf16[2,256,256]{2,1,0:T(8,128)(2,1)S(1)}, u32[]{:S(2)}, u32[]{:S(2)}) collective-permute-start(bf16[2,256,256]{2,1,0:T(8,128)(2,1)S(1)} %shard_map.158.mine.refs_6_), channel_id=1, source_target_pairs={{0,1},{1,0},{2,3},{3,2},{4,5},{5,4},{6,7},{7,6},{8,9},{9,8},{10,11... | collective-permute-start | bytes 786440 | tf_op jit(solution)/shard_map/ppermute | solution.py:340
  50.6 1.2 collective-permute-done.7.other.refs_7_
  51.8 0.0 all-to-all-done.1
  51.8 5.2 %shard_map.159 = (bf16[4,2,256,256]{3,2,1,0:T(8,128)(2,1)S(1)}, bf16[4,2,256,256]{3,2,1,0:T(8,128)(2,1)S(1)}, bf16[4,2,256,256]{3,2,1,0:T(8,128)(2,1)S(1)}, f32[256,256]{1,0:T(8,128)S(1)}) custom-call(s32[7]{0:T(128)S(1)} %concatenate.3.info, bf16[8,2,8,16,256]{4,3,2,1,0:T(8,128)(2,1)S(1)} %bitcast.43, bf16[2,256,256]{2,1,0:T(8,128)(2,1)S(1)} %shard_map.158.mine.refs_6_, ...), custom_call_target="tpu_custom_call" | custom-call | tf_op jit(solution)/shard_map/pallas_call | solution.py:307
  57.0 0.7 collective-permute-start.8
  57.7 1.2 collective-permute-done.8.refs_4_
  58.9 7.1 %shard_map.160 = (f32[2,2,256,256]{3,2,1,0:T(8,128)S(1)}, bf16[8,2,8,16,256]{4,3,2,1,0:T(8,128)(2,1)}) custom-call(s32[7]{0:T(128)S(1)} %concatenate.3.info, bf16[4,2,256,256]{3,2,1,0:T(8,128)(2,1)S(1)} %get-tuple-element.15.refs_0_, bf16[4,2,256,256]{3,2,1,0:T(8,128)(2,1)S(1)} %get-tuple-element.16.refs_1_, ...), custom_call_target="tpu_custom_call" | custom-call | tf_op jit(solution)/shard_map/pallas_call | solution.py:307
  66.0 0.5 collective-permute-start.9
  66.4 1.2 collective-permute-done.9
  67.6 0.1 bitcast_add_fusion
  67.7 3.2 %collective-permute-start.10 = (bf16[256,256]{1,0:T(8,128)(2,1)S(1)}, bf16[256,256]{1,0:T(8,128)(2,1)S(1)}, u32[]{:S(2)}, u32[]{:S(2)}) collective-permute-start(bf16[256,256]{1,0:T(8,128)(2,1)S(1)} %fusion.6), channel_id=1, source_target_pairs={{0,2},{2,0},{1,3},{3,1},{4,6},{6,4},{5,7},{7,5},{8,10},{10,8},{9,1... | collective-permute-start | bytes 393224 | tf_op jit(solution)/shard_map/ppermute | solution.py:340
  71.0 3.4 %collective-permute-done.10.other = bf16[256,256]{1,0:T(8,128)(2,1)S(1)} collective-permute-done((bf16[256,256]{1,0:T(8,128)(2,1)S(1)}, bf16[256,256]{1,0:T(8,128)(2,1)S(1)}, u32[]{:S(2)}, u32[]{:S(2)}) %collective-permute-start.10) | collective-permute-done | bytes 131104 | tf_op jit(solution)/shard_map/ppermute | solution.py:340
  74.4 0.9 shard_map.162
  75.3 3.6 %collective-permute-start.11 = (bf16[2,256,256]{2,1,0:T(8,128)(2,1)S(1)}, bf16[2,256,256]{2,1,0:T(8,128)(2,1)S(1)}, u32[]{:S(2)}, u32[]{:S(2)}) collective-permute-start(bf16[2,256,256]{2,1,0:T(8,128)(2,1)S(1)} %get-tuple-element.22), channel_id=1, source_target_pairs={{0,32},{4,36},{8,40},{12,44},{16,48},{20,52},{24,56},{28,60},{32,6... | collective-permute-start | bytes 786440 | tf_op jit(solution)/shard_map/ppermute | solution.py:345
  78.9 6.6 %all-to-all-start.2 = ((bf16[16,8,16,256]{3,2,1,0:T(8,128)(2,1)}), bf16[16,8,16,256]{3,2,1,0:T(8,128)(2,1)S(1)}, u32[]{:S(2)}, u32[]{:S(2)}) async-start(bf16[16,8,16,256]{3,2,1,0:T(8,128)(2,1)} %bitcast.11), calls=%async_computation.2 | async-start | bytes 2097152 | tf_op jit(solution)/shard_map/all_to_all | solution.py:349
  85.6 3.3 %collective-permute-start.12 = (bf16[256,256]{1,0:T(8,128)(2,1)S(1)}, bf16[256,256]{1,0:T(8,128)(2,1)S(1)}, u32[]{:S(2)}, u32[]{:S(2)}) collective-permute-start(bf16[256,256]{1,0:T(8,128)(2,1)S(1)} %fusion.3), channel_id=1, source_target_pairs={{0,4},{4,8},{8,12},{12,16},{16,20},{20,24},{24,28},{28,32},{32,36}... | collective-permute-start | bytes 393224 | tf_op jit(solution)/shard_map/ppermute | solution.py:345
  88.9 9.3 %collective-permute-done.12 = bf16[256,256]{1,0:T(8,128)(2,1)S(1)} collective-permute-done((bf16[256,256]{1,0:T(8,128)(2,1)S(1)}, bf16[256,256]{1,0:T(8,128)(2,1)S(1)}, u32[]{:S(2)}, u32[]{:S(2)}) %collective-permute-start.12) | collective-permute-done | bytes 131104 | tf_op jit(solution)/shard_map/ppermute | solution.py:345
  98.2 2.8 %collective-permute-start.13 = (f32[256,256]{1,0:T(8,128)S(1)}, f32[256,256]{1,0:T(8,128)S(1)}, u32[]{:S(2)}, u32[]{:S(2)}) collective-permute-start(f32[256,256]{1,0:T(8,128)S(1)} %fusion.5.layer), channel_id=1, source_target_pairs={{0,2},{2,0},{1,3},{3,1},{4,6},{6,4},{5,7},{7,5},{8,10},{10,8},{9,1... | collective-permute-start | bytes 786440 | tf_op jit(solution)/shard_map/ppermute | solution.py:340
  101.0 1.1 shard_map.161
  102.1 5.8 %all-to-all-start.3 = ((bf16[8,64,256]{2,1,0:T(8,128)(2,1)}), bf16[8,64,256]{2,1,0:T(8,128)(2,1)S(1)}, u32[]{:S(2)}, u32[]{:S(2)}) async-start(bf16[8,64,256]{2,1,0:T(8,128)(2,1)} %shard_map.161), calls=%async_computation.3 | async-start | bytes 524288 | tf_op jit(solution)/shard_map/all_to_all | solution.py:349
  107.9 4.5 %collective-permute-done.13 = f32[256,256]{1,0:T(8,128)S(1)} collective-permute-done((f32[256,256]{1,0:T(8,128)S(1)}, f32[256,256]{1,0:T(8,128)S(1)}, u32[]{:S(2)}, u32[]{:S(2)}) %collective-permute-start.13) | collective-permute-done | bytes 262176 | tf_op jit(solution)/shard_map/ppermute | solution.py:340
  112.5 0.0 copy-start.2
  112.5 0.6 collective-permute-start.14
  113.1 4.4 %all-to-all-done.3.src = bf16[8,64,256]{2,1,0:T(8,128)(2,1)S(1)} async-done(((bf16[8,64,256]{2,1,0:T(8,128)(2,1)}), bf16[8,64,256]{2,1,0:T(8,128)(2,1)S(1)}, u32[]{:S(2)}, u32[]{:S(2)}) %all-to-all-start.3) | async-done | bytes 262176 | tf_op jit(solution)/shard_map/all_to_all | solution.py:349
  117.5 0.2 shard_map.163
  117.7 0.7 broadcast_in_dim.44
  118.4 9.0 %all-to-all-start.4 = ((f32[256,1,128]{2,1,0:T(1,128)}), f32[256,1,128]{2,1,0:T(1,128)S(1)}, u32[]{:S(2)}, u32[]{:S(2)}) async-start(f32[256,1,128]{2,1,0:T(1,128)} %broadcast_in_dim.44), calls=%async_computation.4 | async-start | bytes 262144 | tf_op jit(solution)/shard_map/all_to_all | solution.py:349
  128.7 0.0 copy-start.7
  128.7 11.8 %all-to-all-done.4.packed = f32[256,1,128]{2,1,0:T(1,128)S(1)} async-done(((f32[256,1,128]{2,1,0:T(1,128)}), f32[256,1,128]{2,1,0:T(1,128)S(1)}, u32[]{:S(2)}, u32[]{:S(2)}) %all-to-all-start.4) | async-done | bytes 131104 | tf_op jit(solution)/shard_map/all_to_all | solution.py:349
  140.5 3.4 %shard_map.164 = (f32[1,2,2,256,256]{4,3,2,1,0:T(8,128)}, f32[1,2,2,256,256]{4,3,2,1,0:T(8,128)}, f32[4,2,2,4,256]{4,3,2,1,0:T(4,128)}, f32[4,2,2,4,256]{4,3,2,1,0:T(4,128)}) custom-call(s32[7]{0:T(128)S(1)} %concatenate.3.info, s32[2]{0:T(128)S(1)} %copy-done.7, f32[1]{0:T(128)S(6)} %copy.20.object_norm, f32[1]{0:T(128)S(6)} %copy.21.probe_norm, ...), custom_call_target="tpu_custom_call" | custom-call | tf_op jit(solution)/shard_map/pallas_call | solution.py:269
  (32 shorter events, 0.3 us)
Async XLA Ops:
  0.6 0.7 copy-start.9
  1.4 14.4 %collective-permute-start = (s32[1,128]{1,0:T(1,128)S(1)}, s32[1,128]{1,0:T(1,128)S(1)}, u32[]{:S(2)}, u32[]{:S(2)}) collective-permute-start(s32[1,128]{1,0:T(1,128)S(1)} %dynamic_update_slice.5), channel_id=1, source_target_pairs={{4,0},{8,4},{12,8},{0,12},{5,1},{9,5},{13,9},{1,13},{6,2},{10,6},{... | collective-permute-start | bytes 1544 | tf_op jit(solution)/shard_map/ppermute | solution.py:391
  4.8 11.1 %collective-permute-start.1 = (s32[1,128]{1,0:T(1,128)S(1)}, s32[1,128]{1,0:T(1,128)S(1)}, u32[]{:S(2)}, u32[]{:S(2)}) collective-permute-start(s32[1,128]{1,0:T(1,128)S(1)} %dynamic_update_slice.5), channel_id=1, source_target_pairs={{8,0},{12,4},{0,8},{4,12},{9,1},{13,5},{1,9},{5,13},{10,2},{14,6},... | collective-permute-start | bytes 1544 | tf_op jit(solution)/shard_map/ppermute | solution.py:391
  5.3 10.6 %collective-permute-start.2 = (s32[1,128]{1,0:T(1,128)S(1)}, s32[1,128]{1,0:T(1,128)S(1)}, u32[]{:S(2)}, u32[]{:S(2)}) collective-permute-start(s32[1,128]{1,0:T(1,128)S(1)} %dynamic_update_slice.5), channel_id=1, source_target_pairs={{12,0},{0,4},{4,8},{8,12},{13,1},{1,5},{5,9},{9,13},{14,2},{2,6},{... | collective-permute-start | bytes 1544 | tf_op jit(solution)/shard_map/ppermute | solution.py:391
  7.5 17.8 %all-to-all-start = ((bf16[8,64,256]{2,1,0:T(8,128)(2,1)}), bf16[8,64,256]{2,1,0:T(8,128)(2,1)S(1)}, u32[]{:S(2)}, u32[]{:S(2)}) async-start(bf16[8,64,256]{2,1,0:T(8,128)(2,1)} %broadcast_in_dim.40), calls=%async_computation | async-start | bytes 524288 | tf_op jit(solution)/shard_map/all_to_all | solution.py:349
  15.9 3.9 %collective-permute-start.3 = (s32[1,128]{1,0:T(1,128)S(1)}, s32[1,128]{1,0:T(1,128)S(1)}, u32[]{:S(2)}, u32[]{:S(2)}) collective-permute-start(s32[1,128]{1,0:T(1,128)S(1)} %add_add_fusion), channel_id=1, source_target_pairs={{0,16},{16,0},{1,17},{17,1},{2,18},{18,2},{3,19},{19,3},{4,20},{20... | collective-permute-start | bytes 1544 | tf_op jit(solution)/shard_map/ppermute | solution.py:340
  18.5 17.5 %collective-permute-start.4 = (bf16[2,256,256]{2,1,0:T(8,128)(2,1)S(1)}, bf16[2,256,256]{2,1,0:T(8,128)(2,1)S(1)}, u32[]{:S(2)}, u32[]{:S(2)}) collective-permute-start(bf16[2,256,256]{2,1,0:T(8,128)(2,1)S(1)} %fusion.own), channel_id=1, source_target_pairs={{4,0},{8,4},{12,8},{16,12},{20,16},{24,20},{28,24},{32,28},{36,32}... | collective-permute-start | bytes 786440 | tf_op jit(solution)/shard_map/ppermute | solution.py:345
  27.0 6.5 %copy-start.8 = (s32[2,2]{1,0:T(2,128)S(1)}, s32[2,2]{1,0:T(2,128)}, u32[]{:S(2)}) copy-start(s32[2,2]{1,0:T(2,128)} %param.18) | copy-start | bytes 52
  27.0 17.3 %copy-start = (f32[1,2,2,256,256]{4,3,2,1,0:T(8,128)S(1)}, f32[1,2,2,256,256]{4,3,2,1,0:T(8,128)}, u32[]{:S(2)}) copy-start(f32[1,2,2,256,256]{4,3,2,1,0:T(8,128)} %tiles.1) | copy-start | bytes 3145732
  27.0 24.8 %all-to-all-start.1 = ((bf16[16,8,16,256]{3,2,1,0:T(8,128)(2,1)}), bf16[16,8,16,256]{3,2,1,0:T(8,128)(2,1)S(1)}, u32[]{:S(2)}, u32[]{:S(2)}) async-start(bf16[16,8,16,256]{3,2,1,0:T(8,128)(2,1)} %shard_map.156), calls=%async_computation.1 | async-start | bytes 2097152 | tf_op jit(solution)/shard_map/all_to_all | solution.py:349
  33.5 2.4 %collective-permute-start.5 = (s32[2,2]{1,0:T(2,128)S(1)}, s32[2,2]{1,0:T(2,128)S(1)}, u32[]{:S(2)}, u32[]{:S(2)}) collective-permute-start(s32[2,2]{1,0:T(2,128)S(1)} %copy-done.8), channel_id=1, source_target_pairs={{0,32},{4,36},{8,40},{12,44},{16,48},{20,52},{24,56},{28,60},{32,6... | collective-permute-start | bytes 56 | tf_op jit(solution)/shard_map/ppermute | solution.py:345
  36.6 7.7 %collective-permute-start.6 = (bf16[2,256,256]{2,1,0:T(8,128)(2,1)S(1)}, bf16[2,256,256]{2,1,0:T(8,128)(2,1)S(1)}, u32[]{:S(2)}, u32[]{:S(2)}) collective-permute-start(bf16[2,256,256]{2,1,0:T(8,128)(2,1)S(1)} %shard_map.157), channel_id=1, source_target_pairs={{32,0},{36,4},{40,8},{44,12},{48,16},{52,20},{56,24},{60,28},{64,3... | collective-permute-start | bytes 786440 | tf_op jit(solution)/shard_map/ppermute | solution.py:345
  44.3 7.5 %copy-start.3 = (bf16[2,256,256]{2,1,0:T(8,128)(2,1)S(1)}, bf16[2,256,256]{2,1,0:T(8,128)(2,1)}, u32[]{:S(2)}) copy-start(bf16[2,256,256]{2,1,0:T(8,128)(2,1)} %constant.43.clone.dft.refs_8_) | copy-start | bytes 786436
  44.4 7.4 %copy-start.1 = (f32[2,256,256]{2,1,0:T(8,128)S(1)}, f32[2,256,256]{2,1,0:T(8,128)}, u32[]{:S(2)}) copy-start(f32[2,256,256]{2,1,0:T(8,128)} %constant.44.clone.kern.refs_9_) | copy-start | bytes 1572868
  45.2 6.6 %collective-permute-start.7 = (bf16[2,256,256]{2,1,0:T(8,128)(2,1)S(1)}, bf16[2,256,256]{2,1,0:T(8,128)(2,1)S(1)}, u32[]{:S(2)}, u32[]{:S(2)}) collective-permute-start(bf16[2,256,256]{2,1,0:T(8,128)(2,1)S(1)} %shard_map.158.mine.refs_6_), channel_id=1, source_target_pairs={{0,1},{1,0},{2,3},{3,2},{4,5},{5,4},{6,7},{7,6},{8,9},{9,8},{10,11... | collective-permute-start | bytes 786440 | tf_op jit(solution)/shard_map/ppermute | solution.py:340
  51.8 7.0 %copy-start.4 = (f32[2,256,256]{2,1,0:T(8,128)S(1)}, f32[2,256,256]{2,1,0:T(8,128)}, u32[]{:S(2)}) copy-start(f32[2,256,256]{2,1,0:T(8,128)} %refs_5_.1) | copy-start | bytes 1572868
  57.0 1.8 %collective-permute-start.8 = (f32[256,256]{1,0:T(8,128)S(1)}, f32[256,256]{1,0:T(8,128)S(1)}, u32[]{:S(2)}, u32[]{:S(2)}) collective-permute-start(f32[256,256]{1,0:T(8,128)S(1)} %get-tuple-element.18.refs_3_), channel_id=1, source_target_pairs={{0,1},{1,0},{2,3},{3,2},{4,5},{5,4},{6,7},{7,6},{8,9},{9,8},{10,11... | collective-permute-start | bytes 786440 | tf_op jit(solution)/shard_map/ppermute | solution.py:340
  66.0 1.6 %collective-permute-start.9 = (bf16[2,256,256]{2,1,0:T(8,128)(2,1)S(1)}, bf16[2,256,256]{2,1,0:T(8,128)(2,1)S(1)}, u32[]{:S(2)}, u32[]{:S(2)}) collective-permute-start(bf16[2,256,256]{2,1,0:T(8,128)(2,1)S(1)} %fusion.1), channel_id=1, source_target_pairs={{0,1},{1,0},{2,3},{3,2},{4,5},{5,4},{6,7},{7,6},{8,9},{9,8},{10,11... | collective-permute-start | bytes 786440 | tf_op jit(solution)/shard_map/ppermute | solution.py:340
  67.7 6.7 %collective-permute-start.10 = (bf16[256,256]{1,0:T(8,128)(2,1)S(1)}, bf16[256,256]{1,0:T(8,128)(2,1)S(1)}, u32[]{:S(2)}, u32[]{:S(2)}) collective-permute-start(bf16[256,256]{1,0:T(8,128)(2,1)S(1)} %fusion.6), channel_id=1, source_target_pairs={{0,2},{2,0},{1,3},{3,1},{4,6},{6,4},{5,7},{7,5},{8,10},{10,8},{9,1... | collective-permute-start | bytes 393224 | tf_op jit(solution)/shard_map/ppermute | solution.py:340
  75.3 10.2 %collective-permute-start.11 = (bf16[2,256,256]{2,1,0:T(8,128)(2,1)S(1)}, bf16[2,256,256]{2,1,0:T(8,128)(2,1)S(1)}, u32[]{:S(2)}, u32[]{:S(2)}) collective-permute-start(bf16[2,256,256]{2,1,0:T(8,128)(2,1)S(1)} %get-tuple-element.22), channel_id=1, source_target_pairs={{0,32},{4,36},{8,40},{12,44},{16,48},{20,52},{24,56},{28,60},{32,6... | collective-permute-start | bytes 786440 | tf_op jit(solution)/shard_map/ppermute | solution.py:345
  78.9 22.1 %all-to-all-start.2 = ((bf16[16,8,16,256]{3,2,1,0:T(8,128)(2,1)}), bf16[16,8,16,256]{3,2,1,0:T(8,128)(2,1)S(1)}, u32[]{:S(2)}, u32[]{:S(2)}) async-start(bf16[16,8,16,256]{3,2,1,0:T(8,128)(2,1)} %bitcast.11), calls=%async_computation.2 | async-start | bytes 2097152 | tf_op jit(solution)/shard_map/all_to_all | solution.py:349
  85.6 12.6 %collective-permute-start.12 = (bf16[256,256]{1,0:T(8,128)(2,1)S(1)}, bf16[256,256]{1,0:T(8,128)(2,1)S(1)}, u32[]{:S(2)}, u32[]{:S(2)}) collective-permute-start(bf16[256,256]{1,0:T(8,128)(2,1)S(1)} %fusion.3), channel_id=1, source_target_pairs={{0,4},{4,8},{8,12},{12,16},{16,20},{20,24},{24,28},{28,32},{32,36}... | collective-permute-start | bytes 393224 | tf_op jit(solution)/shard_map/ppermute | solution.py:345
  98.2 14.2 %collective-permute-start.13 = (f32[256,256]{1,0:T(8,128)S(1)}, f32[256,256]{1,0:T(8,128)S(1)}, u32[]{:S(2)}, u32[]{:S(2)}) collective-permute-start(f32[256,256]{1,0:T(8,128)S(1)} %fusion.5.layer), channel_id=1, source_target_pairs={{0,2},{2,0},{1,3},{3,1},{4,6},{6,4},{5,7},{7,5},{8,10},{10,8},{9,1... | collective-permute-start | bytes 786440 | tf_op jit(solution)/shard_map/ppermute | solution.py:340
  102.1 15.4 %all-to-all-start.3 = ((bf16[8,64,256]{2,1,0:T(8,128)(2,1)}), bf16[8,64,256]{2,1,0:T(8,128)(2,1)S(1)}, u32[]{:S(2)}, u32[]{:S(2)}) async-start(bf16[8,64,256]{2,1,0:T(8,128)(2,1)} %shard_map.161), calls=%async_computation.3 | async-start | bytes 524288 | tf_op jit(solution)/shard_map/all_to_all | solution.py:349
  112.5 28.0 %copy-start.2 = (f32[1,2,2,256,256]{4,3,2,1,0:T(8,128)S(1)}, f32[1,2,2,256,256]{4,3,2,1,0:T(8,128)}, u32[]{:S(2)}) copy-start(f32[1,2,2,256,256]{4,3,2,1,0:T(8,128)} %before.1) | copy-start | bytes 3145732
  112.5 16.2 %collective-permute-start.14 = (f32[2,256,256]{2,1,0:T(8,128)S(1)}, f32[2,256,256]{2,1,0:T(8,128)}, u32[]{:S(2)}, u32[]{:S(2)}) collective-permute-start(f32[2,256,256]{2,1,0:T(8,128)S(1)} %pad_maximum_fusion.layer), channel_id=1, source_target_pairs={{0,1},{1,0},{2,3},{3,2},{4,5},{5,4},{6,7},{7,6},{8,9},{9,8},{10,11... | collective-permute-start | bytes 1572872 | tf_op jit(solution)/shard_map/ppermute | solution.py:340
  118.4 22.1 %copy-start.5 = (f32[4,2,2,4,256]{4,3,2,1,0:T(4,128)S(1)}, f32[4,2,2,4,256]{4,3,2,1,0:T(4,128)}, u32[]{:S(2)}) copy-start(f32[4,2,2,4,256]{4,3,2,1,0:T(4,128)} %probe.1) | copy-start | bytes 196612
  118.4 22.1 %copy-start.6 = (f32[4,2,2,4,256]{4,3,2,1,0:T(4,128)S(1)}, f32[4,2,2,4,256]{4,3,2,1,0:T(4,128)}, u32[]{:S(2)}) copy-start(f32[4,2,2,4,256]{4,3,2,1,0:T(4,128)} %probe_before.1) | copy-start | bytes 196612
  118.4 22.1 %all-to-all-start.4 = ((f32[256,1,128]{2,1,0:T(1,128)}), f32[256,1,128]{2,1,0:T(1,128)S(1)}, u32[]{:S(2)}, u32[]{:S(2)}) async-start(f32[256,1,128]{2,1,0:T(1,128)} %broadcast_in_dim.44), calls=%async_computation.4 | async-start | bytes 262144 | tf_op jit(solution)/shard_map/all_to_all | solution.py:349
  128.7 11.8 %copy-start.7 = (s32[2]{0:T(128)S(1)}, s32[2]{0:T(128)}, u32[]{:S(2)}) copy-start(s32[2]{0:T(128)} %steps.1) | copy-start | bytes 28

commit v7 on v6

--- a/solution.py
+++ b/solution.py
@@ -230,7 +230,7 @@
     new_tiles, direction, new_probe, probe_direction, held, fetched, sems, fetch_sem = outs
     fetch = pltpu.make_async_copy(other, fetched, fetch_sem)
     fetch.start()
-    totals = jnp.sum(packed[...].reshape(4 * TILES, 128), axis=0, keepdims=True)
+    totals = jnp.sum(packed[...].reshape(4 * NYLX, 128), axis=0, keepdims=True)
     lane = lax.broadcasted_iota(jnp.int32, (1, 128), 1)
 
     def square(at, count):
@@ -432,7 +432,8 @@
     probe_grad, packed = plain(
         grad_sum_kernel, [shape((SCANS * 16, W), F32), shape((1, 128), F32)], summed, part_grad
     )
-    packed = spread(packed, ("z",) + PLANE + ("c",), 4 * TILES)
+    packed = jnp.sum(spread(packed, "z", NZ), axis=0)
+    packed = spread(packed, PLANE + ("c",), 4 * NYLX)
     twin_part = swap(part_grad, "yh")
     layer_grad = jnp.stack(
         [jnp.where(real, part_grad, twin_part), jnp.where(real, twin_part, part_grad)]

time: 145 us -> 162 us (1.12)
  blocking collectives: 0 us -> 26.7 us
  starting transfers between devices: 66.5 us -> 60.7 us
  waiting for transfers between devices: 46.7 us -> 44.8 us
    all_to_all x0 -> x2, blocking collectives: none -> 26.7 us  [exchange(): return lax.all_to_all(value, axes, 0, 0, tiled=True)]
    ppermute x7, waiting for transfers between devices: 11.4 us -> 24.8 us  [swap(): return lax.ppermute(value, axis, [(0, 1), (1, 0)])]
    all_to_all x5 -> x4, waiting for transfers between devices: 21.7 us -> 11.1 us  [exchange(): return lax.all_to_all(value, axes, 0, 0, tiled=True)]
    all_to_all x5 -> x4, starting transfers between devices: 36.1 us -> 28.7 us  [exchange(): return lax.all_to_all(value, axes, 0, 0, tiled=True)]
    ppermute x5, waiting for transfers between devices: 13.6 us -> 8.86 us  [from_tile(): return lax.ppermute(value, TILE_AXES, route)]
    ppermute x7, starting transfers between devices: 14.7 us -> 16.5 us  [swap(): return lax.ppermute(value, axis, [(0, 1), (1, 0)])]
  transfers between devices with their start and end apart: 20 -> 19, of which waited for: 11 -> 10; matrix products, arithmetic and copies ran while one was open for 4% -> 4% of each run, Pallas kernels for 3% -> 2%
where the time goes in v7:
time: 162 us
  starting transfers between devices  60.7 us (37%)
  waiting for transfers between devices  44.8 us (28%)
  blocking collectives  26.7 us (16%)
  Pallas kernels  19.5 us (12%)
  local copies, waits for them, and re-layouts  4.19 us (3%)
  between operations  3.13 us (2%)
  other arithmetic  2.65 us (2%)
    all_to_all x4, starting transfers between devices, exchange(): return lax.all_to_all(value, axes, 0, 0, tiled=True)  28.7 us
    all_to_all x2, blocking collectives, exchange(): return lax.all_to_all(value, axes, 0, 0, tiled=True)  26.7 us
    ppermute x7, waiting for transfers between devices, swap(): return lax.ppermute(value, axis, [(0, 1), (1, 0)])  24.8 us
    ppermute x7, starting transfers between devices, swap(): return lax.ppermute(value, axis, [(0, 1), (1, 0)])  16.5 us
    pallas_call x6, Pallas kernels, whole(): pl.pallas_call(kernel, grid_spec=pltpu.PrefetchScalarGridSpec(num_scalar_...  16.2 us
    all_to_all x4, waiting for transfers between devices, exchange(): return lax.all_to_all(value, axes, 0, 0, tiled=True)  11.1 us
    ppermute x5, starting transfers between devices, from_tile(): return lax.ppermute(value, TILE_AXES, route)  10.9 us
    ppermute x5, waiting for transfers between devices, from_tile(): return lax.ppermute(value, TILE_AXES, route)  8.86 us
  transfers between devices with their start and end apart: 19, of which 10 were waited for; matrix products, arithmetic and copies ran while one was open for 4% of the time, Pallas kernels for 2%

profile of v7, /device:TPU:1, one launch (start us, length us, event | category | flops | bytes accessed | tf_op | source)
XLA Modules:
  0.0 161.7 jit_solution(16110121990734704970)
XLA Ops:
  0.7 0.6 copy-done.9
  1.3 0.1 dynamic_update_slice.5
  1.4 3.5 %collective-permute-start = (s32[1,128]{1,0:T(1,128)S(1)}, s32[1,128]{1,0:T(1,128)S(1)}, u32[]{:S(2)}, u32[]{:S(2)}) collective-permute-start(s32[1,128]{1,0:T(1,128)S(1)} %dynamic_update_slice.5), channel_id=1, source_target_pairs={{4,0},{8,4},{12,8},{0,12},{5,1},{9,5},{13,9},{1,13},{6,2},{10,6},{... | collective-permute-start | bytes 1544 | tf_op jit(solution)/shard_map/ppermute | solution.py:391
  4.8 0.5 collective-permute-start.1
  5.3 0.6 collective-permute-start.2
  6.0 0.9 convert_element_type.31
  6.8 0.7 broadcast_in_dim.46
  7.5 8.2 %all-to-all-start = ((bf16[8,64,256]{2,1,0:T(8,128)(2,1)}), bf16[8,64,256]{2,1,0:T(8,128)(2,1)S(1)}, u32[]{:S(2)}, u32[]{:S(2)}) async-start(bf16[8,64,256]{2,1,0:T(8,128)(2,1)} %broadcast_in_dim.46), calls=%async_computation | async-start | bytes 524288 | tf_op jit(solution)/shard_map/all_to_all | solution.py:349
  15.7 0.0 collective-permute-done
  15.7 0.1 fusion.7
  15.8 0.1 add.47
  15.9 0.0 collective-permute-done.1
  15.9 0.0 collective-permute-done.2
  15.9 1.5 collective-permute-start.3
  17.4 1.1 fusion.own
  18.5 1.3 collective-permute-start.4
  19.8 0.0 collective-permute-done.3
  19.8 5.6 %all-to-all-done = bf16[8,64,256]{2,1,0:T(8,128)(2,1)S(1)} async-done(((bf16[8,64,256]{2,1,0:T(8,128)(2,1)}), bf16[8,64,256]{2,1,0:T(8,128)(2,1)S(1)}, u32[]{:S(2)}, u32[]{:S(2)}) %all-to-all-start) | async-done | bytes 262176 | tf_op jit(solution)/shard_map/all_to_all | solution.py:349
  25.4 1.6 shard_map.156
  27.0 6.5 %all-to-all-start.1 = ((bf16[16,8,16,256]{3,2,1,0:T(8,128)(2,1)}), bf16[16,8,16,256]{3,2,1,0:T(8,128)(2,1)S(1)}, u32[]{:S(2)}, u32[]{:S(2)}) async-start(bf16[16,8,16,256]{3,2,1,0:T(8,128)(2,1)} %shard_map.156), calls=%async_computation.1 | async-start | bytes 2097152 | tf_op jit(solution)/shard_map/all_to_all | solution.py:349
  33.5 1.7 %collective-permute-start.5 = (s32[2,2]{1,0:T(2,128)S(1)}, s32[2,2]{1,0:T(2,128)S(1)}, u32[]{:S(2)}, u32[]{:S(2)}) collective-permute-start(s32[2,2]{1,0:T(2,128)S(1)} %copy-done.8), channel_id=1, source_target_pairs={{0,32},{4,36},{8,40},{12,44},{16,48},{20,52},{24,56},{28,60},{32,6... | collective-permute-start | bytes 56 | tf_op jit(solution)/shard_map/ppermute | solution.py:345
  35.2 0.7 collective-permute-done.5
  35.9 0.1 reshape.54.above
  36.0 0.6 shard_map.157
  36.6 1.3 collective-permute-start.6
  37.9 0.2 fusion.8
  38.8 0.1 concatenate.3.info
  38.9 0.5 fusion.9
  39.4 1.3 iota_compare_fusion
  40.7 3.6 %collective-permute-done.6 = bf16[2,256,256]{2,1,0:T(8,128)(2,1)S(1)} collective-permute-done((bf16[2,256,256]{2,1,0:T(8,128)(2,1)S(1)}, bf16[2,256,256]{2,1,0:T(8,128)(2,1)S(1)}, u32[]{:S(2)}, u32[]{:S(2)}) %collective-permute-start.6) | collective-permute-done | bytes 262176 | tf_op jit(solution)/shard_map/ppermute | solution.py:345
  44.3 0.1 select_select_fusion.mixed
  44.4 0.0 copy-start.1
  44.4 0.8 shard_map.158.mine.refs_6_
  45.2 5.5 %collective-permute-start.7 = (bf16[2,256,256]{2,1,0:T(8,128)(2,1)S(1)}, bf16[2,256,256]{2,1,0:T(8,128)(2,1)S(1)}, u32[]{:S(2)}, u32[]{:S(2)}) collective-permute-start(bf16[2,256,256]{2,1,0:T(8,128)(2,1)S(1)} %shard_map.158.mine.refs_6_), channel_id=1, source_target_pairs={{0,1},{1,0},{2,3},{3,2},{4,5},{5,4},{6,7},{7,6},{8,9},{9,8},{10,11... | collective-permute-start | bytes 786440 | tf_op jit(solution)/shard_map/ppermute | solution.py:340
  50.6 1.2 collective-permute-done.7.other.refs_7_
  51.8 5.2 %shard_map.159 = (bf16[4,2,256,256]{3,2,1,0:T(8,128)(2,1)S(1)}, bf16[4,2,256,256]{3,2,1,0:T(8,128)(2,1)S(1)}, bf16[4,2,256,256]{3,2,1,0:T(8,128)(2,1)S(1)}, f32[256,256]{1,0:T(8,128)S(1)}) custom-call(s32[7]{0:T(128)S(1)} %concatenate.3.info, bf16[8,2,8,16,256]{4,3,2,1,0:T(8,128)(2,1)S(1)} %bitcast.44, bf16[2,256,256]{2,1,0:T(8,128)(2,1)S(1)} %shard_map.158.mine.refs_6_, ...), custom_call_target="tpu_custom_call" | custom-call | tf_op jit(solution)/shard_map/pallas_call | solution.py:307
  57.0 0.7 collective-permute-start.8
  57.7 1.2 collective-permute-done.8.refs_4_
  58.9 7.1 %shard_map.160 = (f32[2,2,256,256]{3,2,1,0:T(8,128)S(1)}, bf16[8,2,8,16,256]{4,3,2,1,0:T(8,128)(2,1)}) custom-call(s32[7]{0:T(128)S(1)} %concatenate.3.info, bf16[4,2,256,256]{3,2,1,0:T(8,128)(2,1)S(1)} %get-tuple-element.15.refs_0_, bf16[4,2,256,256]{3,2,1,0:T(8,128)(2,1)S(1)} %get-tuple-element.16.refs_1_, ...), custom_call_target="tpu_custom_call" | custom-call | tf_op jit(solution)/shard_map/pallas_call | solution.py:307
  66.0 0.5 collective-permute-start.9
  66.4 1.2 collective-permute-done.9
  67.6 0.1 bitcast_add_fusion
  67.7 3.2 %collective-permute-start.10 = (bf16[256,256]{1,0:T(8,128)(2,1)S(1)}, bf16[256,256]{1,0:T(8,128)(2,1)S(1)}, u32[]{:S(2)}, u32[]{:S(2)}) collective-permute-start(bf16[256,256]{1,0:T(8,128)(2,1)S(1)} %fusion.6), channel_id=1, source_target_pairs={{0,2},{2,0},{1,3},{3,1},{4,6},{6,4},{5,7},{7,5},{8,10},{10,8},{9,1... | collective-permute-start | bytes 393224 | tf_op jit(solution)/shard_map/ppermute | solution.py:340
  71.0 3.4 %collective-permute-done.10.other = bf16[256,256]{1,0:T(8,128)(2,1)S(1)} collective-permute-done((bf16[256,256]{1,0:T(8,128)(2,1)S(1)}, bf16[256,256]{1,0:T(8,128)(2,1)S(1)}, u32[]{:S(2)}, u32[]{:S(2)}) %collective-permute-start.10) | collective-permute-done | bytes 131104 | tf_op jit(solution)/shard_map/ppermute | solution.py:340
  74.4 0.9 shard_map.162
  75.3 3.6 %collective-permute-start.11 = (bf16[2,256,256]{2,1,0:T(8,128)(2,1)S(1)}, bf16[2,256,256]{2,1,0:T(8,128)(2,1)S(1)}, u32[]{:S(2)}, u32[]{:S(2)}) collective-permute-start(bf16[2,256,256]{2,1,0:T(8,128)(2,1)S(1)} %get-tuple-element.22), channel_id=1, source_target_pairs={{0,32},{4,36},{8,40},{12,44},{16,48},{20,52},{24,56},{28,60},{32,6... | collective-permute-start | bytes 786440 | tf_op jit(solution)/shard_map/ppermute | solution.py:345
  78.9 4.6 %collective-permute-done.11 = bf16[2,256,256]{2,1,0:T(8,128)(2,1)S(1)} collective-permute-done((bf16[2,256,256]{2,1,0:T(8,128)(2,1)S(1)}, bf16[2,256,256]{2,1,0:T(8,128)(2,1)S(1)}, u32[]{:S(2)}, u32[]{:S(2)}) %collective-permute-start.11) | collective-permute-done | bytes 262176 | tf_op jit(solution)/shard_map/ppermute | solution.py:345
  83.6 3.0 %collective-permute-start.12 = (bf16[256,256]{1,0:T(8,128)(2,1)S(1)}, bf16[256,256]{1,0:T(8,128)(2,1)S(1)}, u32[]{:S(2)}, u32[]{:S(2)}) collective-permute-start(bf16[256,256]{1,0:T(8,128)(2,1)S(1)} %fusion.3), channel_id=1, source_target_pairs={{0,4},{4,8},{8,12},{12,16},{16,20},{20,24},{24,28},{28,32},{32,36}... | collective-permute-start | bytes 393224 | tf_op jit(solution)/shard_map/ppermute | solution.py:345
  86.6 7.2 %all-to-all-start.2 = ((bf16[16,8,16,256]{3,2,1,0:T(8,128)(2,1)}), bf16[16,8,16,256]{3,2,1,0:T(8,128)(2,1)S(1)}, u32[]{:S(2)}, u32[]{:S(2)}) async-start(bf16[16,8,16,256]{3,2,1,0:T(8,128)(2,1)} %bitcast.11), calls=%async_computation.2 | async-start | bytes 2097152 | tf_op jit(solution)/shard_map/all_to_all | solution.py:349
  93.8 0.0 collective-permute-done.12
  93.9 3.0 %collective-permute-start.13 = (f32[256,256]{1,0:T(8,128)S(1)}, f32[256,256]{1,0:T(8,128)S(1)}, u32[]{:S(2)}, u32[]{:S(2)}) collective-permute-start(f32[256,256]{1,0:T(8,128)S(1)} %fusion.5.layer), channel_id=1, source_target_pairs={{0,2},{2,0},{1,3},{3,1},{4,6},{6,4},{5,7},{7,5},{8,10},{10,8},{9,1... | collective-permute-start | bytes 786440 | tf_op jit(solution)/shard_map/ppermute | solution.py:340
  96.8 17.9 %collective-permute-done.13 = f32[256,256]{1,0:T(8,128)S(1)} collective-permute-done((f32[256,256]{1,0:T(8,128)S(1)}, f32[256,256]{1,0:T(8,128)S(1)}, u32[]{:S(2)}, u32[]{:S(2)}) %collective-permute-start.13) | collective-permute-done | bytes 262176 | tf_op jit(solution)/shard_map/ppermute | solution.py:340
  114.8 2.3 %collective-permute-start.14 = (f32[2,256,256]{2,1,0:T(8,128)S(1)}, f32[2,256,256]{2,1,0:T(8,128)S(1)}, u32[]{:S(2)}, u32[]{:S(2)}) collective-permute-start(f32[2,256,256]{2,1,0:T(8,128)S(1)} %pad_maximum_fusion.layer), channel_id=1, source_target_pairs={{0,1},{1,0},{2,3},{3,2},{4,5},{5,4},{6,7},{7,6},{8,9},{9,8},{10,11... | collective-permute-start | bytes 1572872 | tf_op jit(solution)/shard_map/ppermute | solution.py:340
  117.1 0.4 shard_map.161
  117.5 0.0 copy-start.2
  117.5 17.7 %all_to_all.30.src = bf16[8,64,256]{2,1,0:T(8,128)(2,1)S(1)} all-to-all(bf16[8,64,256]{2,1,0:T(8,128)(2,1)S(1)} %shard_map.161), channel_id=1, replica_groups=mesh['z'=8,'yl'=2,'x'=4,'yh'=2,'c'=2] {'z'}, dimensions={0} | all-to-all | bytes 524288 | tf_op jit(solution)/shard_map/all_to_all | solution.py:349
  135.3 0.2 shard_map.163
  135.5 0.0 copy-start.5
  135.5 8.9 %all_to_all.31 = f32[8,1,128]{2,1,0:T(1,128)S(1)} all-to-all(f32[8,1,128]{2,1,0:T(1,128)S(1)} %broadcast_in_dim.50), channel_id=1, replica_groups=mesh['z'=8,'yl'=2,'x'=4,'yh'=2,'c'=2] {'z'}, dimensions={0} | all-to-all | bytes 8192 | tf_op jit(solution)/shard_map/all_to_all | solution.py:349
  144.4 0.6 broadcast_in_dim.51
  145.0 6.8 %all-to-all-start.5 = ((f32[32,1,128]{2,1,0:T(1,128)}), f32[32,1,128]{2,1,0:T(1,128)S(1)}, u32[]{:S(2)}, u32[]{:S(2)}) async-start(f32[32,1,128]{2,1,0:T(1,128)} %broadcast_in_dim.51), calls=%async_computation.5 | async-start | bytes 32768 | tf_op jit(solution)/shard_map/all_to_all | solution.py:349
  153.1 0.0 copy-start.7
  153.2 5.6 %all-to-all-done.5.packed = f32[32,1,128]{2,1,0:T(1,128)S(1)} async-done(((f32[32,1,128]{2,1,0:T(1,128)}), f32[32,1,128]{2,1,0:T(1,128)S(1)}, u32[]{:S(2)}, u32[]{:S(2)}) %all-to-all-start.5) | async-done | bytes 16416 | tf_op jit(solution)/shard_map/all_to_all | solution.py:349
  158.7 2.8 %shard_map.164 = (f32[1,2,2,256,256]{4,3,2,1,0:T(8,128)}, f32[1,2,2,256,256]{4,3,2,1,0:T(8,128)}, f32[4,2,2,4,256]{4,3,2,1,0:T(4,128)}, f32[4,2,2,4,256]{4,3,2,1,0:T(4,128)}) custom-call(s32[7]{0:T(128)S(1)} %concatenate.3.info, s32[2]{0:T(128)S(1)} %copy-done.7, f32[1]{0:T(128)S(6)} %copy.21.object_norm, f32[1]{0:T(128)S(6)} %copy.22.probe_norm, ...), custom_call_target="tpu_custom_call" | custom-call | tf_op jit(solution)/shard_map/pallas_call | solution.py:269
  (34 shorter events, 0.4 us)
Async XLA Ops:
  0.6 0.7 copy-start.9
  1.4 14.4 %collective-permute-start = (s32[1,128]{1,0:T(1,128)S(1)}, s32[1,128]{1,0:T(1,128)S(1)}, u32[]{:S(2)}, u32[]{:S(2)}) collective-permute-start(s32[1,128]{1,0:T(1,128)S(1)} %dynamic_update_slice.5), channel_id=1, source_target_pairs={{4,0},{8,4},{12,8},{0,12},{5,1},{9,5},{13,9},{1,13},{6,2},{10,6},{... | collective-permute-start | bytes 1544 | tf_op jit(solution)/shard_map/ppermute | solution.py:391
  4.8 11.1 %collective-permute-start.1 = (s32[1,128]{1,0:T(1,128)S(1)}, s32[1,128]{1,0:T(1,128)S(1)}, u32[]{:S(2)}, u32[]{:S(2)}) collective-permute-start(s32[1,128]{1,0:T(1,128)S(1)} %dynamic_update_slice.5), channel_id=1, source_target_pairs={{8,0},{12,4},{0,8},{4,12},{9,1},{13,5},{1,9},{5,13},{10,2},{14,6},... | collective-permute-start | bytes 1544 | tf_op jit(solution)/shard_map/ppermute | solution.py:391
  5.3 10.6 %collective-permute-start.2 = (s32[1,128]{1,0:T(1,128)S(1)}, s32[1,128]{1,0:T(1,128)S(1)}, u32[]{:S(2)}, u32[]{:S(2)}) collective-permute-start(s32[1,128]{1,0:T(1,128)S(1)} %dynamic_update_slice.5), channel_id=1, source_target_pairs={{12,0},{0,4},{4,8},{8,12},{13,1},{1,5},{5,9},{9,13},{14,2},{2,6},{... | collective-permute-start | bytes 1544 | tf_op jit(solution)/shard_map/ppermute | solution.py:391
  7.5 17.8 %all-to-all-start = ((bf16[8,64,256]{2,1,0:T(8,128)(2,1)}), bf16[8,64,256]{2,1,0:T(8,128)(2,1)S(1)}, u32[]{:S(2)}, u32[]{:S(2)}) async-start(bf16[8,64,256]{2,1,0:T(8,128)(2,1)} %broadcast_in_dim.46), calls=%async_computation | async-start | bytes 524288 | tf_op jit(solution)/shard_map/all_to_all | solution.py:349
  15.9 3.9 %collective-permute-start.3 = (s32[1,128]{1,0:T(1,128)S(1)}, s32[1,128]{1,0:T(1,128)S(1)}, u32[]{:S(2)}, u32[]{:S(2)}) collective-permute-start(s32[1,128]{1,0:T(1,128)S(1)} %add_add_fusion), channel_id=1, source_target_pairs={{0,16},{16,0},{1,17},{17,1},{2,18},{18,2},{3,19},{19,3},{4,20},{20... | collective-permute-start | bytes 1544 | tf_op jit(solution)/shard_map/ppermute | solution.py:340
  18.5 17.5 %collective-permute-start.4 = (bf16[2,256,256]{2,1,0:T(8,128)(2,1)S(1)}, bf16[2,256,256]{2,1,0:T(8,128)(2,1)S(1)}, u32[]{:S(2)}, u32[]{:S(2)}) collective-permute-start(bf16[2,256,256]{2,1,0:T(8,128)(2,1)S(1)} %fusion.own), channel_id=1, source_target_pairs={{4,0},{8,4},{12,8},{16,12},{20,16},{24,20},{28,24},{32,28},{36,32}... | collective-permute-start | bytes 786440 | tf_op jit(solution)/shard_map/ppermute | solution.py:345
  27.0 6.5 %copy-start.8 = (s32[2,2]{1,0:T(2,128)S(1)}, s32[2,2]{1,0:T(2,128)}, u32[]{:S(2)}) copy-start(s32[2,2]{1,0:T(2,128)} %param.18) | copy-start | bytes 52
  27.0 17.3 %copy-start = (f32[1,2,2,256,256]{4,3,2,1,0:T(8,128)S(1)}, f32[1,2,2,256,256]{4,3,2,1,0:T(8,128)}, u32[]{:S(2)}) copy-start(f32[1,2,2,256,256]{4,3,2,1,0:T(8,128)} %tiles.1) | copy-start | bytes 3145732
  27.0 24.8 %all-to-all-start.1 = ((bf16[16,8,16,256]{3,2,1,0:T(8,128)(2,1)}), bf16[16,8,16,256]{3,2,1,0:T(8,128)(2,1)S(1)}, u32[]{:S(2)}, u32[]{:S(2)}) async-start(bf16[16,8,16,256]{3,2,1,0:T(8,128)(2,1)} %shard_map.156), calls=%async_computation.1 | async-start | bytes 2097152 | tf_op jit(solution)/shard_map/all_to_all | solution.py:349
  33.5 2.4 %collective-permute-start.5 = (s32[2,2]{1,0:T(2,128)S(1)}, s32[2,2]{1,0:T(2,128)S(1)}, u32[]{:S(2)}, u32[]{:S(2)}) collective-permute-start(s32[2,2]{1,0:T(2,128)S(1)} %copy-done.8), channel_id=1, source_target_pairs={{0,32},{4,36},{8,40},{12,44},{16,48},{20,52},{24,56},{28,60},{32,6... | collective-permute-start | bytes 56 | tf_op jit(solution)/shard_map/ppermute | solution.py:345
  36.6 7.7 %collective-permute-start.6 = (bf16[2,256,256]{2,1,0:T(8,128)(2,1)S(1)}, bf16[2,256,256]{2,1,0:T(8,128)(2,1)S(1)}, u32[]{:S(2)}, u32[]{:S(2)}) collective-permute-start(bf16[2,256,256]{2,1,0:T(8,128)(2,1)S(1)} %shard_map.157), channel_id=1, source_target_pairs={{32,0},{36,4},{40,8},{44,12},{48,16},{52,20},{56,24},{60,28},{64,3... | collective-permute-start | bytes 786440 | tf_op jit(solution)/shard_map/ppermute | solution.py:345
  44.3 7.5 %copy-start.3 = (bf16[2,256,256]{2,1,0:T(8,128)(2,1)S(1)}, bf16[2,256,256]{2,1,0:T(8,128)(2,1)}, u32[]{:S(2)}) copy-start(bf16[2,256,256]{2,1,0:T(8,128)(2,1)} %constant.45.clone.dft.refs_8_) | copy-start | bytes 786436
  44.4 7.4 %copy-start.1 = (f32[2,256,256]{2,1,0:T(8,128)S(1)}, f32[2,256,256]{2,1,0:T(8,128)}, u32[]{:S(2)}) copy-start(f32[2,256,256]{2,1,0:T(8,128)} %constant.46.clone.kern.refs_9_) | copy-start | bytes 1572868
  45.2 6.6 %collective-permute-start.7 = (bf16[2,256,256]{2,1,0:T(8,128)(2,1)S(1)}, bf16[2,256,256]{2,1,0:T(8,128)(2,1)S(1)}, u32[]{:S(2)}, u32[]{:S(2)}) collective-permute-start(bf16[2,256,256]{2,1,0:T(8,128)(2,1)S(1)} %shard_map.158.mine.refs_6_), channel_id=1, source_target_pairs={{0,1},{1,0},{2,3},{3,2},{4,5},{5,4},{6,7},{7,6},{8,9},{9,8},{10,11... | collective-permute-start | bytes 786440 | tf_op jit(solution)/shard_map/ppermute | solution.py:340
  51.8 7.0 %copy-start.4 = (f32[2,256,256]{2,1,0:T(8,128)S(1)}, f32[2,256,256]{2,1,0:T(8,128)}, u32[]{:S(2)}) copy-start(f32[2,256,256]{2,1,0:T(8,128)} %refs_5_.1) | copy-start | bytes 1572868
  57.0 1.8 %collective-permute-start.8 = (f32[256,256]{1,0:T(8,128)S(1)}, f32[256,256]{1,0:T(8,128)S(1)}, u32[]{:S(2)}, u32[]{:S(2)}) collective-permute-start(f32[256,256]{1,0:T(8,128)S(1)} %get-tuple-element.18.refs_3_), channel_id=1, source_target_pairs={{0,1},{1,0},{2,3},{3,2},{4,5},{5,4},{6,7},{7,6},{8,9},{9,8},{10,11... | collective-permute-start | bytes 786440 | tf_op jit(solution)/shard_map/ppermute | solution.py:340
  66.0 1.6 %collective-permute-start.9 = (bf16[2,256,256]{2,1,0:T(8,128)(2,1)S(1)}, bf16[2,256,256]{2,1,0:T(8,128)(2,1)S(1)}, u32[]{:S(2)}, u32[]{:S(2)}) collective-permute-start(bf16[2,256,256]{2,1,0:T(8,128)(2,1)S(1)} %fusion.1), channel_id=1, source_target_pairs={{0,1},{1,0},{2,3},{3,2},{4,5},{5,4},{6,7},{7,6},{8,9},{9,8},{10,11... | collective-permute-start | bytes 786440 | tf_op jit(solution)/shard_map/ppermute | solution.py:340
  67.7 6.7 %collective-permute-start.10 = (bf16[256,256]{1,0:T(8,128)(2,1)S(1)}, bf16[256,256]{1,0:T(8,128)(2,1)S(1)}, u32[]{:S(2)}, u32[]{:S(2)}) collective-permute-start(bf16[256,256]{1,0:T(8,128)(2,1)S(1)} %fusion.6), channel_id=1, source_target_pairs={{0,2},{2,0},{1,3},{3,1},{4,6},{6,4},{5,7},{7,5},{8,10},{10,8},{9,1... | collective-permute-start | bytes 393224 | tf_op jit(solution)/shard_map/ppermute | solution.py:340
  75.3 8.2 %collective-permute-start.11 = (bf16[2,256,256]{2,1,0:T(8,128)(2,1)S(1)}, bf16[2,256,256]{2,1,0:T(8,128)(2,1)S(1)}, u32[]{:S(2)}, u32[]{:S(2)}) collective-permute-start(bf16[2,256,256]{2,1,0:T(8,128)(2,1)S(1)} %get-tuple-element.22), channel_id=1, source_target_pairs={{0,32},{4,36},{8,40},{12,44},{16,48},{20,52},{24,56},{28,60},{32,6... | collective-permute-start | bytes 786440 | tf_op jit(solution)/shard_map/ppermute | solution.py:345
  83.6 10.2 %collective-permute-start.12 = (bf16[256,256]{1,0:T(8,128)(2,1)S(1)}, bf16[256,256]{1,0:T(8,128)(2,1)S(1)}, u32[]{:S(2)}, u32[]{:S(2)}) collective-permute-start(bf16[256,256]{1,0:T(8,128)(2,1)S(1)} %fusion.3), channel_id=1, source_target_pairs={{0,4},{4,8},{8,12},{12,16},{16,20},{20,24},{24,28},{28,32},{32,36}... | collective-permute-start | bytes 393224 | tf_op jit(solution)/shard_map/ppermute | solution.py:345
  86.6 30.5 %all-to-all-start.2 = ((bf16[16,8,16,256]{3,2,1,0:T(8,128)(2,1)}), bf16[16,8,16,256]{3,2,1,0:T(8,128)(2,1)S(1)}, u32[]{:S(2)}, u32[]{:S(2)}) async-start(bf16[16,8,16,256]{3,2,1,0:T(8,128)(2,1)} %bitcast.11), calls=%async_computation.2 | async-start | bytes 2097152 | tf_op jit(solution)/shard_map/all_to_all | solution.py:349
  93.9 20.9 %collective-permute-start.13 = (f32[256,256]{1,0:T(8,128)S(1)}, f32[256,256]{1,0:T(8,128)S(1)}, u32[]{:S(2)}, u32[]{:S(2)}) collective-permute-start(f32[256,256]{1,0:T(8,128)S(1)} %fusion.5.layer), channel_id=1, source_target_pairs={{0,2},{2,0},{1,3},{3,1},{4,6},{6,4},{5,7},{7,5},{8,10},{10,8},{9,1... | collective-permute-start | bytes 786440 | tf_op jit(solution)/shard_map/ppermute | solution.py:340
  114.8 43.9 %collective-permute-start.14 = (f32[2,256,256]{2,1,0:T(8,128)S(1)}, f32[2,256,256]{2,1,0:T(8,128)S(1)}, u32[]{:S(2)}, u32[]{:S(2)}) collective-permute-start(f32[2,256,256]{2,1,0:T(8,128)S(1)} %pad_maximum_fusion.layer), channel_id=1, source_target_pairs={{0,1},{1,0},{2,3},{3,2},{4,5},{5,4},{6,7},{7,6},{8,9},{9,8},{10,11... | collective-permute-start | bytes 1572872 | tf_op jit(solution)/shard_map/ppermute | solution.py:340
  117.1 41.6 %copy-start.6 = (f32[4,2,2,4,256]{4,3,2,1,0:T(4,128)S(1)}, f32[4,2,2,4,256]{4,3,2,1,0:T(4,128)}, u32[]{:S(2)}) copy-start(f32[4,2,2,4,256]{4,3,2,1,0:T(4,128)} %probe_before.1) | copy-start | bytes 196612
  117.5 41.2 %copy-start.2 = (f32[1,2,2,256,256]{4,3,2,1,0:T(8,128)S(1)}, f32[1,2,2,256,256]{4,3,2,1,0:T(8,128)}, u32[]{:S(2)}) copy-start(f32[1,2,2,256,256]{4,3,2,1,0:T(8,128)} %before.1) | copy-start | bytes 3145732
  135.5 23.3 %copy-start.5 = (f32[4,2,2,4,256]{4,3,2,1,0:T(4,128)S(1)}, f32[4,2,2,4,256]{4,3,2,1,0:T(4,128)}, u32[]{:S(2)}) copy-start(f32[4,2,2,4,256]{4,3,2,1,0:T(4,128)} %probe.1) | copy-start | bytes 196612
  145.0 13.7 %all-to-all-start.5 = ((f32[32,1,128]{2,1,0:T(1,128)}), f32[32,1,128]{2,1,0:T(1,128)S(1)}, u32[]{:S(2)}, u32[]{:S(2)}) async-start(f32[32,1,128]{2,1,0:T(1,128)} %broadcast_in_dim.51), calls=%async_computation.5 | async-start | bytes 32768 | tf_op jit(solution)/shard_map/all_to_all | solution.py:349
  153.1 5.6 %copy-start.7 = (s32[2]{0:T(128)S(1)}, s32[2]{0:T(128)}, u32[]{:S(2)}) copy-start(s32[2]{0:T(128)} %steps.1) | copy-start | bytes 28
